TPU v7x, 32 devices: a whole 2x2x4 slice. The times are simulated.
32 devices in a mesh: dp: 16 (over z, y, core), tensor: 2 (over x).
Axes of the slice: x: 2, y: 2, z: 4, core: 2. Of those that a mesh axis runs over, the one named last changes fastest.
Arguments:
- tokens: bfloat16 [16, 1024, 768], P(None, 'dp', 'tensor'), may hold values from -6 to 6
- cotangent: bfloat16 [16, 1024, 768], P(None, 'dp', 'tensor'), may hold values from -6 to 6
- thoughts: bfloat16 [16, 6, 768], P('dp', None, 'tensor'), may hold values from -6 to 6
- latent_pos: int32 [16, 6], P('dp'), may hold values from 1 to 63, as said below
- lengths: int32 [16], replicated, may hold values from 64 to 1024, as said below
- dealing: int32 [16], replicated, may hold values from 0 to 15, each once
- qkv_weight: bfloat16 [3, 768, 768], P(None, None, 'tensor'), may hold values from -0.21875 to 0.21875
- qv_bias: float32 [2, 768], P(None, 'tensor'), may hold values from -3 to 3
- out_weight: bfloat16 [768, 768], P('tensor'), may hold values from -0.875 to 0.875
- out_bias: float32 [2, 768], replicated, may hold values from -3 to 3
- fc_weight: bfloat16 [768, 3072], P(None, 'tensor'), may hold values from -0.21875 to 0.21875
- fc_bias: float32 [3072], P('tensor'), may hold values from -3 to 3
- proj_weight: bfloat16 [3072, 768], P('tensor'), may hold values from -0.109375 to 0.109375
- norm_gain: float32 [2, 768], replicated, may hold values from 0.5 to 1.5
- norm_shift: float32 [2, 768], replicated, may hold values from -3 to 3
Outputs:
- block_out: float32 [16, 1024, 768], P(None, 'dp', 'tensor')
- input_grad: float32 [16, 1024, 768], P(None, 'dp', 'tensor')
- grad_qkv_weight: float32 [3, 768, 768], P(None, None, 'tensor')
- grad_qv_bias: float32 [2, 768], P(None, 'tensor')
- grad_out_weight: float32 [768, 768], P('tensor')
- grad_out_bias: float32 [2, 768], replicated
- grad_fc_weight: float32 [768, 3072], P(None, 'tensor')
- grad_fc_bias: float32 [3072], P('tensor')
- grad_proj_weight: float32 [3072, 768], P('tensor')
- grad_norm_gain: float32 [2, 768], replicated
- grad_norm_shift: float32 [2, 768], replicated
Inputs may be any that keep to these rules, and one draw needn't show every extreme that they name: `lengths`: one sequence has exactly 1024 tokens and one exactly 64. `dealing`: dealt slot j belongs to data group j. `latent_pos`: each slot's 6 positions are consecutive and lie below every sequence's length.
All inputs are finite; a program needn't handle non-finite values.
Results may differ from a plain program's by a relative error of at most 0.012.
The roundings to bfloat16 on the way count: a program that leaves them out, or rounds other values in their place, can miss the bound.
Values may be sent and summed in bfloat16 or wider, within the bound.
No kernel may reach another device: no remote copies, remote signals or barrier semaphores. Data moves between devices by JAX's collectives and lax.ppermute only.
A program may use at most 192 MiB of HBM per device.

v0:
```python
import functools

import jax
import jax.numpy as jnp
from jax import lax
from jax.experimental import pallas as pl
from jax.experimental.pallas import tpu as pltpu
from jax.sharding import PartitionSpec as P

HEAD_DIM = 64
LANES = 128
AXES = ("dp", "tensor")
SCALE = HEAD_DIM ** (-0.5)
MASKED = -1e30
BF16 = jnp.bfloat16
F32 = jnp.float32


def dot_nn(left, right):
    return lax.dot_general(left, right, (((1,), (0,)), ((), ())), preferred_element_type=F32)


def dot_nt(left, right):
    return lax.dot_general(left, right, (((1,), (1,)), ((), ())), preferred_element_type=F32)


def dot_tn(left, right):
    return lax.dot_general(left, right, (((0,), (0,)), ((), ())), preferred_element_type=F32)


def own_mask(tile, start, core, length, block):
    key = lax.broadcasted_iota(jnp.int32, (tile, tile), 0)
    query = lax.broadcasted_iota(jnp.int32, (tile, tile), 1)
    key_row = start + key
    key_pos = (2 * (key_row // block) + core) * block + key_row % block
    return (key <= query) & (key_pos < length)


def other_mask(tile, start, core, length, block):
    key = lax.broadcasted_iota(jnp.int32, (tile, tile), 0)
    query = lax.broadcasted_iota(jnp.int32, (tile, tile), 1)
    key_row = start + key
    key_pos = (2 * (key_row // block) + 1 - core) * block + key_row % block
    return (key // block <= query // block - (1 - core)) & (key_pos < length)


def attend_forward_kernel(tile, block, info, q_ref, ko_ref, vo_ref, kx_ref, vx_ref, out_ref, lse_ref):
    core, length = info[0], info[1]
    rows = q_ref.shape[0]
    lane = lax.broadcasted_iota(jnp.int32, (1, LANES), 1)
    vo_t = vo_ref[...].T
    vx_t = vx_ref[...].T
    for start in range(0, rows, tile):
        stop = start + tile
        mask_own = own_mask(tile, start, core, length, block)
        mask_other = other_mask(tile, start, core, length, block)
        query = q_ref[start:stop, :] * jnp.asarray(SCALE, BF16)
        outs = []
        for half in range(2):
            picked = jnp.where(lane // HEAD_DIM == half, query, jnp.zeros_like(query))
            s_own = dot_nt(ko_ref[:stop, :], picked)
            s_other = dot_nt(kx_ref[:stop, :], picked)
            d_own = jnp.where(mask_own, s_own[start:], MASKED)
            d_other = jnp.where(mask_other, s_other[start:], MASKED)
            if start:
                s_own = jnp.concatenate([s_own[:start], d_own], axis=0)
                s_other = jnp.concatenate([s_other[:start], d_other], axis=0)
            else:
                s_own, s_other = d_own, d_other
            top = jnp.maximum(
                jnp.max(s_own, axis=0, keepdims=True), jnp.max(s_other, axis=0, keepdims=True)
            )
            e_own = jnp.exp(s_own - top)
            e_other = jnp.exp(s_other - top)
            total = jnp.sum(e_own, axis=0, keepdims=True) + jnp.sum(e_other, axis=0, keepdims=True)
            lanes = slice(half * HEAD_DIM, (half + 1) * HEAD_DIM)
            mixed = dot_nn(vo_t[lanes, :stop], e_own.astype(BF16)) + dot_nn(
                vx_t[lanes, :stop], e_other.astype(BF16)
            )
            outs.append(mixed / total)
            lse_ref[0, half : half + 1, start:stop] = top + jnp.log(total)
        out_ref[start:stop, :] = jnp.concatenate(outs, axis=0).T.astype(BF16)


def attend_backward_kernel(
    tile, block, info, q_ref, ko_ref, vo_ref, kx_ref, vx_ref, go_ref, out_ref, lse_ref,
    dq_ref, dko_ref, dvo_ref, dkx_ref, dvx_ref, ako, avo, akx, avx,
):
    core, length = info[0], info[1]
    rows = q_ref.shape[0]
    lane = lax.broadcasted_iota(jnp.int32, (1, LANES), 1)
    ko_t = ko_ref[...].T
    kx_t = kx_ref[...].T
    for acc in (ako, avo, akx, avx):
        acc[...] = jnp.zeros_like(acc)
    for start in range(0, rows, tile):
        stop = start + tile
        mask_own = own_mask(tile, start, core, length, block)
        mask_other = other_mask(tile, start, core, length, block)
        query = q_ref[start:stop, :] * jnp.asarray(SCALE, BF16)
        grad = go_ref[start:stop, :]
        product = grad.astype(F32) * out_ref[start:stop, :].astype(F32)
        parts = []
        for half in range(2):
            mine = lane // HEAD_DIM == half
            picked = jnp.where(mine, query, jnp.zeros_like(query))
            grad_half = jnp.where(mine, grad, jnp.zeros_like(grad))
            pick = jnp.broadcast_to(jnp.where(mine, 1.0, 0.0).astype(F32), (8, LANES))
            inner = lax.dot_general(
                pick, product, (((1,), (1,)), ((), ())),
                precision=lax.Precision.HIGHEST, preferred_element_type=F32,
            )[:1]
            lse = lse_ref[0, half : half + 1, start:stop]
            lanes = slice(half * HEAD_DIM, (half + 1) * HEAD_DIM)
            part = jnp.zeros((HEAD_DIM, tile), F32)
            for key_ref, value_ref, key_t, mask, acc_k, acc_v in (
                (ko_ref, vo_ref, ko_t, mask_own, ako, avo),
                (kx_ref, vx_ref, kx_t, mask_other, akx, avx),
            ):
                prob = jnp.exp(dot_nt(key_ref[:stop, :], picked) - lse)
                last = jnp.where(mask, prob[start:], 0.0)
                prob = jnp.concatenate([prob[:start], last], axis=0) if start else last
                grad_prob = dot_nt(value_ref[:stop, :], grad_half)
                grad_score = (prob * (grad_prob - inner)).astype(BF16)
                acc_v[:stop, :] += dot_nn(prob.astype(BF16), grad_half)
                acc_k[:stop, :] += dot_nn(grad_score, picked)
                part = part + dot_nn(key_t[lanes, :stop], grad_score)
            parts.append(part)
        dq_ref[start:stop, :] = (jnp.concatenate(parts, axis=0) * SCALE).T.astype(BF16)
    for acc, ref in ((ako, dko_ref), (avo, dvo_ref), (akx, dkx_ref), (avx, dvx_ref)):
        ref[...] = acc[...].astype(ref.dtype)


def attend_forward(info, block, queries, keys_own, values_own, keys_other, values_other):
    rows, width = queries.shape
    pairs = width // LANES
    tile = min(256, rows)
    column = pl.BlockSpec((rows, LANES), lambda pair, info: (0, pair))
    return pl.pallas_call(
        functools.partial(attend_forward_kernel, tile, block),
        grid_spec=pltpu.PrefetchScalarGridSpec(
            num_scalar_prefetch=1,
            grid=(pairs,),
            in_specs=[column] * 5,
            out_specs=[column, pl.BlockSpec((1, 2, rows), lambda pair, info: (pair, 0, 0))],
        ),
        out_shape=[
            jax.ShapeDtypeStruct((rows, width), BF16),
            jax.ShapeDtypeStruct((pairs, 2, rows), F32),
        ],
        name="attend_forward",
    )(info, queries, keys_own, values_own, keys_other, values_other)


def attend_backward(info, block, first, pairs, queries, keys_own, values_own, keys_other, values_other, grad_heads,
                    heads_out, lse):
    rows = queries.shape[0]
    tile = min(256, rows)
    column = pl.BlockSpec((rows, LANES), lambda pair, info: (0, first + pair))
    result = pl.BlockSpec((rows, LANES), lambda pair, info: (0, pair))
    dtypes = (BF16, F32, F32, BF16, BF16)
    return pl.pallas_call(
        functools.partial(attend_backward_kernel, tile, block),
        grid_spec=pltpu.PrefetchScalarGridSpec(
            num_scalar_prefetch=1,
            grid=(pairs,),
            in_specs=[column] * 7 + [pl.BlockSpec((1, 2, rows), lambda pair, info: (first + pair, 0, 0))],
            out_specs=[result] * 5,
            scratch_shapes=[pltpu.VMEM((rows, LANES), F32)] * 4,
        ),
        out_shape=[jax.ShapeDtypeStruct((rows, pairs * LANES), dtype) for dtype in dtypes],
        name="attend_backward",
    )(info, queries, keys_own, values_own, keys_other, values_other, grad_heads, heads_out, lse)


HALF = 384


def spec(shape, index):
    return pl.BlockSpec(shape, index)


def whole(shape):
    zeros = (0,) * len(shape)
    return pl.BlockSpec(shape, lambda *_: zeros)


def call(kernel, name, grid, in_specs, out_specs, out_shape, scratch=()):
    return pl.pallas_call(
        kernel,
        grid_spec=pltpu.PrefetchScalarGridSpec(
            num_scalar_prefetch=1, grid=grid, in_specs=in_specs, out_specs=out_specs, scratch_shapes=list(scratch)
        ),
        out_shape=out_shape,
        name=name,
    )


def like(shape, dtype):
    return jax.ShapeDtypeStruct(shape, dtype)


def gather_slots(index, array, dtype):
    slots, block, width = array.shape
    steps = 4
    per = slots // steps

    def kernel(index_ref, array_ref, out_ref):
        first = pl.program_id(0) * per

        def copy(i, carry):
            out_ref[i] = array_ref[index_ref[first + i]].astype(dtype)
            return carry

        lax.fori_loop(0, per, copy, 0, unroll=min(per, 4))

    return call(
        kernel, "gather_slots", (steps,), [whole(array.shape)],
        spec((per, block, width), lambda i, _: (i, 0, 0)), like(array.shape, dtype),
    )(index, array)


def statistics(features):
    mean = jnp.mean(features, axis=-1, keepdims=True)
    centred = features - mean
    variance = jnp.mean(centred * centred, axis=-1, keepdims=True)
    scale = lax.rsqrt(variance + 1e-05)
    return centred * scale, scale


def norm_rows_back(grad, gain, xhat, scale):
    scaled = grad * gain
    return scale * (
        scaled
        - jnp.mean(scaled, axis=-1, keepdims=True)
        - xhat * jnp.mean(scaled * xhat, axis=-1, keepdims=True)
    )


def sum_rows(value):
    return jnp.sum(value, axis=0, keepdims=True)


def row_positions(tile, block, core):
    row = pl.program_id(0) * tile + lax.broadcasted_iota(jnp.int32, (tile, 1), 0)
    return (2 * (row // block) + core) * block + row % block


def rows_of(pieces_ref, tile):
    halves = [pieces_ref[:, side].astype(F32).reshape(tile, HALF) for side in range(2)]
    return jnp.concatenate(halves, axis=1)


def cols(index):
    return pl.ds(pl.multiple_of(index * HALF, LANES), HALF)


def rows_at(index):
    return pl.ds(pl.multiple_of(index * HALF, LANES), HALF)


ROOT = 0.7978845608028654
CUBE = 0.044715


def gelu_and_slope(value):
    square = value * value
    turn = jnp.tanh(ROOT * value * (1.0 + CUBE * square))
    slope = 0.5 * (1.0 + turn) + 0.5 * value * (1.0 - turn * turn) * ROOT * (1.0 + 3.0 * CUBE * square)
    return 0.5 * value * (1.0 + turn), slope


def enter_kernel(tile, block, info, pieces, thoughts, norms, bias_own, bias_other, own_k, own_v, direct, partner,
                 inputs_ref, normed_ref, k_ref, v_ref):
    core = info[0]
    position = row_positions(tile, block, core)
    features = rows_of(pieces, tile)
    for index in range(6):
        features = jnp.where(position == info[2 + index], thoughts[index : index + 1, :], features)
    inputs_ref[...] = features
    xhat, _ = statistics(features)
    normed = (xhat * norms[0:1, :] + norms[1:2, :]).astype(BF16)
    normed_ref[...] = normed
    project(core, normed_ref, own_k[0], direct[0], partner[0], None, None, k_ref)
    project(core, normed_ref, own_v[0], direct[1], partner[1], bias_own[1:2, :], bias_other[1:2, :], v_ref)


def project(core, normed, own, direct, partner, bias_own, bias_other, ref):
    mine = dot_nn(normed[...], own)
    theirs = dot_nn(normed[:, cols(core)], direct) + dot_nn(normed[:, cols(1 - core)], partner)
    if bias_own is not None:
        mine = mine + bias_own
        theirs = theirs + bias_other
    ref[:, :HALF] = mine.astype(BF16)
    ref[:, HALF:] = theirs.astype(BF16)


def queries_kernel(info, normed, bias_own, bias_other, own, direct, partner, q_ref):
    project(info[0], normed, own[0], direct[0], partner[0], bias_own[0:1, :], bias_other[0:1, :], q_ref)


def cotangent_kernel(tile, block, info, pieces, grad_ref):
    position = row_positions(tile, block, info[0])
    grad_ref[...] = jnp.where(position < info[1], rows_of(pieces, tile), 0.0).astype(BF16)


def middle_kernel(info, heads, inputs, norms, own, direct, partner, residual_ref, normed_ref, mixed):
    core = info[0]
    mixed[...] = dot_nn(heads[:, :HALF], own[...]) + norms[2:3, :]
    mixed[:, cols(core)] += dot_nn(heads[:, HALF:], direct[...])
    mixed[:, cols(1 - core)] += dot_nn(heads[:, HALF:], partner[...])
    residual = inputs[...] + mixed[...]
    residual_ref[...] = residual
    xhat, _ = statistics(residual)
    normed_ref[...] = (xhat * norms[0:1, :] + norms[1:2, :]).astype(BF16)


def mlp_rows_kernel(info, normed, grad, fc, bias, proj, mlp_ref, back_ref, active_t_ref, pre_ref, fcb_ref, mlp_sum, back_sum):
    step = pl.program_id(1)
    active, slope = gelu_and_slope(dot_nn(normed[...], fc[...]) + bias[...])
    active = active.astype(BF16)
    active_t_ref[...] = active.T
    grad_pre = (dot_nt(grad[...], proj[...]) * slope).astype(BF16)
    pre_ref[...] = grad_pre
    fcb_ref[0] = sum_rows(grad_pre.astype(F32))
    mlp = dot_nn(active, proj[...])
    back = dot_nt(grad_pre, fc[...])

    @pl.when(step == 0)
    def _():
        mlp_sum[...] = mlp
        back_sum[...] = back

    @pl.when((step > 0) & (step < pl.num_programs(1) - 1))
    def _():
        mlp_sum[...] += mlp
        back_sum[...] += back

    @pl.when(step == pl.num_programs(1) - 1)
    def _():
        mlp_ref[...] = (mlp_sum[...] + mlp).astype(mlp_ref.dtype)
        back_ref[...] = (back_sum[...] + back).astype(back_ref.dtype)


def mlp_grads_kernel(info, normed0, normed1, grad0, grad1, active0, active1, pre0, pre1, keep, send, normed_t):
    core = info[0]

    @pl.when(pl.program_id(0) == 0)
    def _():
        normed_t[0] = normed0[...].T
        normed_t[1] = normed1[...].T

    for index, ref in ((core, keep), (1 - core, send)):
        fc = dot_nn(normed_t[0, rows_at(index), :], pre0[...]) + dot_nn(normed_t[1, rows_at(index), :], pre1[...])
        proj = dot_nn(active0[rows_at(index), :], grad0[...]) + dot_nn(active1[rows_at(index), :], grad1[...])
        ref[:, : 2 * HALF] = fc.astype(BF16)
        ref[:, 2 * HALF :] = proj.astype(BF16)


def back_kernel(info, back, back_far, residual, grad, norms, own, direct, partner,
                grad_residual_ref, grad_attn_ref, grad_heads_ref, small_ref):
    core = info[0]
    xhat, scale = statistics(residual[...])
    incoming = back[...] + back_far[...].astype(F32)
    grad_out = grad[...].astype(F32)
    grad_residual = grad_out + norm_rows_back(incoming, norms[0:1, :], xhat, scale)
    grad_residual_ref[...] = grad_residual
    grad_attn = grad_residual.astype(BF16)
    grad_attn_ref[...] = grad_attn
    grad_heads_ref[:, :HALF] = dot_nt(grad_attn, own[...]).astype(BF16)
    theirs = dot_nt(grad_attn_ref[:, cols(core)], direct[...])
    theirs = theirs + dot_nt(grad_attn_ref[:, cols(1 - core)], partner[...])
    grad_heads_ref[:, HALF:] = theirs.astype(BF16)
    sums = jnp.concatenate(
        [sum_rows(incoming * xhat), sum_rows(incoming), sum_rows(grad_out), sum_rows(grad_attn.astype(F32))], axis=0
    )

    @pl.when(pl.program_id(0) == 0)
    def _():
        small_ref[...] = sums

    @pl.when(pl.program_id(0) > 0)
    def _():
        small_ref[...] += sums


def block_kernel(tile, block, info, residual, mlp, mlp_far, bias, block_ref):
    position = row_positions(tile, block, info[0])
    result = residual[...] + (mlp[...] + mlp_far[...].astype(F32) + bias[...])
    result = jnp.where(position < info[1], result, 0.0)
    for side in range(2):
        half = result[:, side * HALF : (side + 1) * HALF].reshape(tile // block, block, HALF)
        block_ref[:, side] = half.astype(BF16)


def key_value_grads(dk, dk_far, dv, dv_far):
    return (
        (dk[...] + dk_far[...].astype(F32)).astype(BF16),
        (dv[...] + dv_far[...].astype(F32)).astype(BF16),
    )


def attention_grads_kernel(info, normed, heads, grad_attn, dq, dk, dk_far, dv, dv_far, keep, send, normed_t):
    core = info[0]
    normed_t[...] = normed[...].T
    grads = (dq[...], *key_value_grads(dk, dk_far, dv, dv_far))
    heads_t = heads[...].T
    for index, ref in ((1 - core, send), (core, keep)):
        left = normed_t[rows_at(index), :]
        for place, grad in enumerate(grads):
            ref[:, place * HALF : (place + 1) * HALF] = dot_nn(left, grad).astype(BF16)
        ref[:, 3 * HALF :] = dot_nn(heads_t, grad_attn[:, cols(index)]).astype(BF16)


def leave_kernel(tile, block, info, inputs, grad_residual, norms, dq0, dk0, dk_far0, dv0, dv_far0,
                 dq1, dk1, dk_far1, dv1, dv_far1, own, direct, partner, direct_q, partner_q, pieces_ref, small_ref, back):
    core = info[0]
    mine = (dq0[...], *key_value_grads(dk0, dk_far0, dv0, dv_far0))
    theirs = (dq1[...], *key_value_grads(dk1, dk_far1, dv1, dv_far1))
    back[...] = sum(dot_nt(grad, own[index]) for index, grad in enumerate(mine))
    far_q, far_k, far_v = theirs
    back[:, cols(core)] += dot_nt(far_q, direct_q[0]) + dot_nt(far_k, direct[0]) + dot_nt(far_v, direct[1])
    back[:, cols(1 - core)] += dot_nt(far_q, partner_q[0]) + dot_nt(far_k, partner[0]) + dot_nt(far_v, partner[1])
    incoming = back[...]
    xhat, scale = statistics(inputs[...])
    result = grad_residual[...] + norm_rows_back(incoming, norms[0:1, :], xhat, scale)
    blocks = tile // block
    for side in range(2):
        pieces_ref[:, side] = result[:, side * HALF : (side + 1) * HALF].reshape(blocks, block, HALF).astype(BF16)
    biases = [
        jnp.concatenate([sum_rows(mine[place].astype(F32)), sum_rows(theirs[place].astype(F32))], axis=1)
        for place in (0, 2)
    ]
    sums = jnp.concatenate([sum_rows(incoming * xhat), sum_rows(incoming), *biases], axis=0)

    @pl.when(pl.program_id(0) == 0)
    def _():
        small_ref[...] = sums

    @pl.when(pl.program_id(0) > 0)
    def _():
        small_ref[...] += sums


def finish_rows(info, refs):
    core, near = info[0], info[8]
    size = refs[0].shape[0]
    for index, ref in enumerate(refs):
        base = (core if index < 2 else 1 - core) * HALF
        yield base, (near if index % 2 == 0 else 1 - near) * size, ref


def finish_mlp_kernel(info, *refs):
    fc_ref, proj_ref = refs[4:]
    for base, offset, ref in finish_rows(info, refs[:4]):
        rows = pl.ds(pl.multiple_of(base + offset, 64), ref.shape[0])
        fc_ref[rows, :] = ref[:, : 2 * HALF].astype(F32)
        proj_ref[rows, :] = ref[:, 2 * HALF :].astype(F32)


def finish_attention_kernel(info, *refs):
    qkv_ref, out_ref = refs[4:]
    for base, offset, ref in finish_rows(info, refs[:4]):
        rows = pl.ds(pl.multiple_of(base + offset, 64), ref.shape[0])
        for place in range(3):
            qkv_ref[place, rows, :] = ref[:, place * HALF : (place + 1) * HALF].astype(F32)
        heads = pl.ds(pl.multiple_of(offset, 64), ref.shape[0])
        out_ref[heads, pl.ds(pl.multiple_of(base, LANES), HALF)] = ref[:, 3 * HALF :].astype(F32)


def solution(mesh):
    groups = mesh.shape["dp"]
    bits = groups.bit_length() - 1
    assert groups == 1 << bits and mesh.shape["tensor"] == 2

    def pairs_of(change):
        table = []
        for group in range(groups):
            for side in range(2):
                to_group, to_side = change(group, side)
                table.append((group * 2 + side, to_group * 2 + to_side))
        return table

    tensor_pairs = pairs_of(lambda group, side: (group, 1 - side))
    bit_pairs = [pairs_of(lambda group, side, k=k: (group ^ (1 << k), side)) for k in range(bits)]
    deal_groups = [
        [group * 2 + side for group in range(core, groups, 2) for side in range(2)] for core in range(2)
    ]

    def body(
        tokens, cotangent, thoughts, latent_pos, lengths, dealing, qkv_weight, qv_bias, out_weight,
        out_bias, fc_weight, fc_bias, proj_weight, norm_gain, norm_shift,
    ):
        group = lax.axis_index("dp")
        side = lax.axis_index("tensor")
        core = group % 2
        slot = group - core + side
        slots, block, half_width = tokens.shape
        width = 2 * half_width
        rows = slots * block // 2
        hidden_half = fc_weight.shape[1]
        assert half_width == HALF and hidden_half == 4 * HALF
        tile = 256
        blocks = tile // block

        def cross(value):
            return lax.ppermute(value, AXES, tensor_pairs)

        def flip(value, bit=0):
            return lax.ppermute(value, AXES, bit_pairs[bit])

        def part(value, index, axis=0):
            size = value.shape[axis] // 2
            return lax.dynamic_slice_in_dim(value, index * size, size, axis)

        def join(flag, mine, theirs, axis=0):
            return jnp.where(
                flag == 0,
                jnp.concatenate([mine, theirs], axis=axis),
                jnp.concatenate([theirs, mine], axis=axis),
            )

        def exchange(array):
            return lax.all_to_all(
                array, AXES, split_axis=0, concat_axis=0, tiled=True, axis_index_groups=deal_groups
            )

        def deal(array):
            return exchange(gather_slots(dealing, array, BF16)).reshape(slots // 2, 2, block, half_width)

        order = jnp.arange(slots, dtype=jnp.int32)
        restore = jnp.sum(jnp.where(dealing[None, :] == order[:, None], order[None, :], 0), axis=1)

        qkv_sent = part(qkv_weight, core, 1)
        thoughts_core = flip(thoughts[0])
        tokens, thoughts_core = lax.optimization_barrier((tokens, thoughts_core))
        dealt = deal(tokens)
        kv_direct = cross(qkv_sent[1:])
        kv_partner = flip(kv_direct)
        biases_other = cross(qv_bias)
        near = jnp.where(core == side, thoughts[0], thoughts_core)
        far = cross(jnp.where(core == side, thoughts_core, thoughts[0]))
        latent_core = flip(latent_pos)
        latent = jnp.where(core == side, latent_pos, latent_core)[0]
        length = lengths[dealing[slot]]
        info = jnp.concatenate(
            [jnp.stack([core, length]).astype(jnp.int32), latent, jnp.stack([(group >> 1) & 1, group >> 2]).astype(jnp.int32)]
        )

        cot_dealt = gather_slots(dealing, cotangent, BF16)
        out_sent = part(out_weight, core, 1)
        thought_rows = join(side, near, far, axis=1).astype(F32)
        norms_in = jnp.stack([norm_gain[0], norm_shift[0]])
        norms_mid = jnp.stack([norm_gain[1], norm_shift[1], out_bias[0]])
        q_sent, out_sent, kv_direct, cot_dealt, thought_rows, biases_other, info, norms_in, norms_mid = (
            lax.optimization_barrier(
                (qkv_sent[:1], out_sent, kv_direct, cot_dealt, thought_rows, biases_other, info, norms_in, norms_mid)
            )
        )
        q_direct = cross(q_sent)
        qv_other = biases_other
        out_direct = cross(out_sent)
        cot_pieces = exchange(cot_dealt).reshape(slots // 2, 2, block, half_width)

        steps = rows // tile
        rowwise = spec((tile, width), lambda i, _: (i, 0))
        pieces_spec = spec((blocks, 2, block, half_width), lambda i, _: (i, 0, 0, 0))
        one, two, three = (spec((1, width, half_width), lambda i, _, place=place: (place, 0, 0)) for place in range(3))
        kv_specs = [whole(kv_direct.shape)] * 2
        q_specs = [whole(q_direct.shape)] * 2
        out_specs = [whole(out_weight.shape), whole(out_sent.shape), whole(out_sent.shape)]
        rows_bf, rows_f = like((rows, width), BF16), like((rows, width), F32)

        inputs, normed, keys_own, values_own = call(
            functools.partial(enter_kernel, tile, block), "enter", (steps,),
            [pieces_spec, whole((6, width)), whole((2, width)), whole((2, half_width)), whole((2, half_width)), two, three, *kv_specs],
            [rowwise] * 4, [rows_f, rows_bf, rows_bf, rows_bf],
        )(info, dealt, thought_rows, norms_in, qv_bias, qv_other,
          qkv_weight, qkv_weight, kv_direct, kv_partner)
        keys_other, values_other = flip(keys_own), flip(values_own)
        grad_mlp = call(
            functools.partial(cotangent_kernel, tile, block), "cotangent", (steps,), [pieces_spec], rowwise, rows_bf
        )(info, cot_pieces)
        q_direct, grad_mlp = lax.optimization_barrier((q_direct, grad_mlp))
        q_partner = flip(q_direct)
        queries = call(
            queries_kernel, "queries", (steps,),
            [rowwise, whole((2, half_width)), whole((2, half_width)), one, *q_specs], rowwise, rows_bf,
        )(info, normed, qv_bias, qv_other, qkv_weight, q_direct, q_partner)
        queries, grad_mlp, keys_other, values_other, out_direct = lax.optimization_barrier(
            (queries, grad_mlp, keys_other, values_other, out_direct)
        )
        grad_far = cross(grad_mlp)
        out_partner = flip(out_direct)
        heads_out, lse = attend_forward(info, block, queries, keys_own, values_own, keys_other, values_other)
        heads_out, grad_far = lax.optimization_barrier((heads_out, grad_far))
        residual, normed_mlp = call(
            middle_kernel, "middle", (steps,),
            [rowwise, rowwise, whole((3, width)), *out_specs],
            [rowwise] * 2, [rows_f, rows_bf], [pltpu.VMEM((tile, width), F32)],
        )(info, heads_out, inputs, norms_mid,
          out_weight, out_direct, out_partner)
        normed_far = cross(normed_mlp)

        full = whole((rows, width))
        chunk = 2 * half_width

        def mlp_rows(normed_rows, grad_rows, dtype):
            units = hidden_half // 3
            by_row = spec((tile, width), lambda r, i, _: (r, 0))
            result = like((rows, width), dtype)
            return call(
                mlp_rows_kernel, "mlp_rows", (steps, 3),
                [by_row, by_row, spec((width, units), lambda r, i, _: (0, i)), spec((1, units), lambda r, i, _: (0, i)),
                 spec((units, width), lambda r, i, _: (i, 0))],
                [by_row, by_row, spec((units, tile), lambda r, i, _: (i, r)), spec((tile, units), lambda r, i, _: (r, i)),
                 spec((1, 1, units), lambda r, i, _: (r, 0, i))],
                [result, result, like((hidden_half, rows), BF16), like((rows, hidden_half), BF16),
                 like((steps, 1, hidden_half), F32)],
                [pltpu.VMEM((tile, width), F32)] * 2,
            )(info, normed_rows, grad_rows, fc_weight, fc_bias.reshape(1, hidden_half), proj_weight)

        mlp, back, active0, pre0, fcb0 = mlp_rows(normed_mlp, grad_mlp, F32)
        normed_far, mlp = lax.optimization_barrier((normed_far, mlp))
        mlp_sent, back_sent, active1, pre1, fcb1 = mlp_rows(normed_far, grad_far, BF16)
        back_far = cross(back_sent)
        quarter_spec = spec((half_width, 2 * chunk), lambda i, _: (0, i))
        by_unit = spec((rows, chunk), lambda i, _: (0, i))
        unit_rows = spec((chunk, rows), lambda i, _: (i, 0))
        mlp_keep, mlp_send = call(
            mlp_grads_kernel, "mlp_grads", (2,),
            [full] * 4 + [unit_rows] * 2 + [by_unit] * 2, [quarter_spec] * 2,
            [like((half_width, 4 * chunk), BF16)] * 2, [pltpu.VMEM((2, width, rows), BF16)],
        )(info, normed_mlp, normed_far, grad_mlp, grad_far, active0, active1, pre0, pre1)

        back_far, mlp_keep, mlp_send, mlp_sent = lax.optimization_barrier((back_far, mlp_keep, mlp_send, mlp_sent))
        mlp_far = cross(mlp_sent)
        near = (group >> 1) & 1
        half = half_width // 2
        upper = list(range(2, bits))
        levels = len(upper)
        flags = [(group >> link) & 1 for link in upper]
        sizes = [half >> (level + 1) for level in range(levels)]
        starts = [sum(flag * size for flag, size in zip(flags[:level], sizes)) for level in range(levels + 1)]

        def rows_sum(terms, start, size):
            total = 0.0
            for array, base in terms:
                total = total + lax.dynamic_slice_in_dim(array, base + start, size, 0).astype(F32)
            return total.astype(BF16)

        def section(level):
            if level == levels:
                return starts[level], sizes[-1]
            return starts[level] + (1 - flags[level]) * sizes[level], sizes[level]

        def widen(level, mine, theirs):
            return join(flags[level], mine, theirs)

        mlp_got = flip(mlp_send)
        grad_residual, grad_attn, grad_heads, small_mlp = call(
            back_kernel, "back", (steps,),
            [rowwise, rowwise, rowwise, rowwise, whole((1, width)), *out_specs],
            [rowwise, rowwise, rowwise, whole((4, width))],
            [rows_f, rows_bf, rows_bf, like((4, width), F32)],
        )(info, back, back_far, residual, grad_mlp, norm_gain[1:], out_weight, out_direct, out_partner)
        pairs = half_width // LANES
        grad_heads, mlp_got = lax.optimization_barrier((grad_heads, mlp_got))
        mlp_rows_kept = [(mlp_keep, near * half), (mlp_got, near * half)]
        mlp_rows_sent = [(mlp_keep, (1 - near) * half), (mlp_got, (1 - near) * half)]
        over_y = [rows_sum(mlp_rows_sent, *section(level)) for level in range(levels + 1)]
        grad_heads, *over_y = lax.optimization_barrier((grad_heads, *over_y))
        over_y[0] = flip(over_y[0], 1)

        def mlp_section(level):
            start, size = section(level)
            return rows_sum([*mlp_rows_kept, (over_y[level], -start)], start, size)

        def backward(first, grad):
            grad_q, grad_ko, grad_vo, grad_kx, grad_vx = attend_backward(
                info, block, first, pairs, queries, keys_own, values_own, keys_other, values_other, grad, heads_out, lse
            )
            return grad_q, grad_ko, grad_vo, grad_kx, grad_vx

        def with_far(grads, *ties):
            grad_q, grad_ko, grad_vo, grad_kx, grad_vx = grads
            far_k, far_v, *ties = lax.optimization_barrier((flip(grad_kx), flip(grad_vx), *ties))
            return (grad_q, grad_ko, far_k, grad_vo, far_v), ties

        other = backward(pairs, grad_heads)
        mlp_far, *tied = lax.optimization_barrier((mlp_far, *over_y, *other))
        over_y, other = tied[: levels + 1], tied[levels + 1 :]
        over_y[1] = flip(over_y[1], 1)
        block_pieces = call(
            functools.partial(block_kernel, tile, block), "block", (steps,),
            [rowwise, rowwise, rowwise, whole((1, width))], pieces_spec,
            like((slots // 2, 2, block, half_width), BF16),
        )(info, residual, mlp, mlp_far, out_bias[1:])
        other, (block_pieces,) = with_far(other, block_pieces)
        block_back = exchange(block_pieces.reshape(slots, block, half_width))

        def attention_grads(column, grads):
            shape = (half_width, 4 * half_width)
            return call(
                attention_grads_kernel, "attention_grads", (1,),
                [full, spec((rows, half_width), lambda i, _: (0, column)), full, *[whole((rows, half_width))] * 5],
                [whole(shape)] * 2, [like(shape, BF16)] * 2, [pltpu.VMEM((width, rows), BF16)],
            )(info, normed, heads_out, grad_attn, *grads)

        keep_other, send_other = attention_grads(1, other)
        keep_other, send_other, *over_y = lax.optimization_barrier((keep_other, send_other, *over_y))
        over_y[2:] = [flip(value, 1) for value in over_y[2:]]
        got_other = flip(send_other)
        mlp_stage = mlp_section(0)
        x_first, x_last = (
            rows_sum([(keep_other, place * half), (got_other, place * half)], 0, half) for place in (1 - near, near)
        )
        x_first, x_last, mlp_stage, grad_heads = lax.optimization_barrier((x_first, x_last, mlp_stage, grad_heads))
        x_first = cross(x_first)
        mlp_stage = flip(mlp_stage, upper[0])
        own = backward(0, grad_heads)
        x_first, x_last, mlp_stage, *tied = lax.optimization_barrier((x_first, x_last, mlp_stage, *over_y[2:], *own))
        over_y[2:], own = tied[: levels - 1], tied[levels - 1 :]
        x_last = cross(x_last)
        mlp_rows_kept.append((mlp_stage, -starts[1]))
        own, (mlp_stage,) = with_far(own, mlp_section(1))
        mlp_stage = flip(mlp_stage, upper[1])
        keep_own, send_own = attention_grads(0, own)
        keep_own, send_own, mlp_stage = lax.optimization_barrier((keep_own, send_own, mlp_stage))
        mlp_rows_kept.append((mlp_stage, -starts[2]))
        for level in range(2, levels):
            mlp_rows_kept.append((flip(mlp_section(level), upper[level]), -starts[level + 1]))
        mlp_piece = mlp_section(levels)
        for level in reversed(range(2, levels)):
            mlp_piece = widen(level, mlp_piece, flip(mlp_piece, upper[level]))
        block_out = gather_slots(restore, block_back, F32)
        mlp_piece, block_out, *own = lax.optimization_barrier((mlp_piece, block_out, *own))
        mlp_stage = flip(mlp_piece, upper[1])
        got_own = flip(send_own)
        half_rows = spec((tile, half_width), lambda i, _: (i, 0))
        input_pieces, small_attn = call(
            functools.partial(leave_kernel, tile, block), "leave", (steps,),
            [rowwise, rowwise, whole((1, width)), *[half_rows] * 10, whole(qkv_weight.shape), *kv_specs, *q_specs],
            [pieces_spec, whole((4, width))],
            [like((slots // 2, 2, block, half_width), BF16), like((4, width), F32)],
            [pltpu.VMEM((tile, width), F32)],
        )(info, inputs, grad_residual, norm_gain[:1], *own, *other, qkv_weight, kv_direct, kv_partner, q_direct, q_partner)
        input_pieces, small_attn, got_own, x_last, mlp_stage = lax.optimization_barrier(
            (input_pieces, small_attn, got_own, x_last, mlp_stage)
        )
        sent = rows_sum([(keep_own, (1 - near) * half), (got_own, (1 - near) * half), (x_first, 0)], 0, half)
        over_bit = flip(sent, 1)
        mlp_piece = widen(1, mlp_piece, mlp_stage)
        mlp_stage = flip(mlp_piece, upper[0])
        input_back = exchange(input_pieces.reshape(slots, block, half_width))

        def ordered(vectors):
            return join(side, vectors[:, :half_width], vectors[:, half_width:], axis=1)

        hidden = 2 * hidden_half
        fcb0 = jnp.sum(fcb0 + fcb1, axis=0)
        fcb = join(side, fcb0, jnp.zeros_like(fcb0), axis=1).reshape(hidden // width, width)
        small = jnp.concatenate([small_mlp, small_attn[:2], ordered(small_attn[2:]), fcb], axis=0)
        links = [flip, cross, *[functools.partial(flip, bit=bit) for bit in range(1, bits)]]

        def add_over(value):
            return value + links.pop(0)(value) if links else value

        small = add_over(small)
        over_bit, mlp_stage, small = lax.optimization_barrier((over_bit, mlp_stage, small))
        mlp_piece = widen(0, mlp_piece, mlp_stage)
        kept = [(keep_own, near * half), (got_own, near * half), (x_last, 0), (over_bit, 0)]
        for level in range(levels):
            stage = flip(rows_sum(kept, *section(level)), upper[level])
            if level == 0:
                mlp_over, mlp_core = flip(mlp_piece, 1), flip(mlp_piece)
            small = add_over(small)
            stage, small, input_back = lax.optimization_barrier((stage, small, input_back))
            kept.append((stage, -starts[level + 1]))
        piece = rows_sum(kept, *section(levels))
        for level in reversed(range(levels)):
            stage = flip(piece, upper[level])
            small = add_over(small)
            stage, small = lax.optimization_barrier((stage, small))
            piece = widen(level, piece, stage)
        while links:
            small = add_over(small)
        over, near_core = flip(piece, 1), flip(piece)
        mlp_over, mlp_core, piece = lax.optimization_barrier((mlp_over, mlp_core, piece))
        mlp_all = [mlp_piece, mlp_over, mlp_core, flip(mlp_over)]
        input_grad = gather_slots(restore, input_back, F32)
        fc_grad, proj_grad = call(
            finish_mlp_kernel, "finish_mlp", (2,), [spec((half, 2 * chunk), lambda i, _: (0, i))] * 4,
            [spec((width, chunk), lambda i, _: (0, i)), spec((chunk, width), lambda i, _: (i, 0))],
            [like(fc_weight.shape, F32), like(proj_weight.shape, F32)],
        )(info, *mlp_all)
        over, fc_grad, proj_grad, input_grad, small = lax.optimization_barrier((over, fc_grad, proj_grad, input_grad, small))
        qkv_grad, out_grad = call(
            finish_attention_kernel, "finish_attention", (1,), [whole((half, 2 * chunk))] * 4,
            [whole(qkv_weight.shape), whole(out_weight.shape)],
            [like(qkv_weight.shape, F32), like(out_weight.shape, F32)],
        )(info, piece, over, near_core, flip(over))

        gain_mlp, shift_mlp, bias_mlp, bias_attn, gain_attn, shift_attn = (small[i] for i in range(6))
        return (
            block_out,
            input_grad,
            qkv_grad,
            part(small[6:8], side, 1),
            out_grad,
            jnp.stack([bias_attn, bias_mlp]),
            fc_grad,
            part(small[8:].reshape(hidden), side),
            proj_grad,
            jnp.stack([gain_attn, gain_mlp]),
            jnp.stack([shift_attn, shift_mlp]),
        )

    return jax.shard_map(
        body,
        mesh=mesh,
        in_specs=(
            P(None, "dp", "tensor"),
            P(None, "dp", "tensor"),
            P("dp", None, "tensor"),
            P("dp", None),
            P(),
            P(),
            P(None, None, "tensor"),
            P(None, "tensor"),
            P("tensor", None),
            P(),
            P(None, "tensor"),
            P("tensor"),
            P("tensor", None),
            P(),
            P(),
        ),
        out_specs=(
            P(None, "dp", "tensor"),
            P(None, "dp", "tensor"),
            P(None, None, "tensor"),
            P(None, "tensor"),
            P("tensor", None),
            P(),
            P(None, "tensor"),
            P("tensor"),
            P("tensor", None),
            P(),
            P(),
        ),
        check_vma=False,
    )
```

profile of v0, /device:TPU:0, one launch (start us, length us, event | category | flops | bytes accessed | tf_op | source)
XLA Modules:
  0.0 357.1 jit_solution(10175912684578191690)
XLA Ops:
  1.2 2.6 collective-permute-start.3
  6.0 3.3 gather_slots.5
  9.3 7.3 %all-to-all-start = ((bf16[16,64,384]{2,1,0:T(8,128)(2,1)}), bf16[16,64,384]{2,1,0:T(8,128)(2,1)S(1)}, u32[]{:S(2)}, u32[]{:S(2)}) async-start(bf16[16,64,384]{2,1,0:T(8,128)(2,1)} %gather_slots.5), calls=%async_computation | async-start | bytes 1572864 | tf_op jit(solution)/shard_map/all_to_all | solution.py:524
  21.5 3.3 gather_slots.4
  30.4 6.0 %all-to-all-done = bf16[16,64,384]{2,1,0:T(8,128)(2,1)S(1)} async-done(((bf16[16,64,384]{2,1,0:T(8,128)(2,1)}), bf16[16,64,384]{2,1,0:T(8,128)(2,1)S(1)}, u32[]{:S(2)}, u32[]{:S(2)}) %all-to-all-start) | async-done | bytes 786464 | tf_op jit(solution)/shard_map/all_to_all | solution.py:524
  36.5 5.0 %all-to-all-start.1 = ((bf16[16,64,384]{2,1,0:T(8,128)(2,1)}), bf16[16,64,384]{2,1,0:T(8,128)(2,1)S(1)}, u32[]{:S(2)}, u32[]{:S(2)}) async-start(bf16[16,64,384]{2,1,0:T(8,128)(2,1)} %gather_slots.4), calls=%async_computation.1 | async-start | bytes 1572864 | tf_op jit(solution)/shard_map/all_to_all | solution.py:524
  44.3 6.9 %enter.1 = (f32[512,768]{1,0:T(8,128)}, bf16[512,768]{1,0:T(8,128)(2,1)}, bf16[512,768]{1,0:T(8,128)(2,1)}, bf16[512,768]{1,0:T(8,128)(2,1)}) custom-call(s32[10]{0:T(128)} %concatenate.50.info, bf16[8,2,64,384]{3,2,1,0:T(8,128)(2,1)} %bitcast.13, f32[6,768]{1,0:T(8,128)} %fusion.1.thoughts, f32[2,768]{1,0:T(2,128)} %pad_maximum_fusion.2.norms, ...), custom_call_target="tpu_custom_call" | custom-call | tf_op jit(solution)/shard_map/enter/pallas_call | solution.py:574
  53.6 6.5 %all-to-all-done.1 = bf16[16,64,384]{2,1,0:T(8,128)(2,1)S(1)} async-done(((bf16[16,64,384]{2,1,0:T(8,128)(2,1)}), bf16[16,64,384]{2,1,0:T(8,128)(2,1)S(1)}, u32[]{:S(2)}, u32[]{:S(2)}) %all-to-all-start.1) | async-done | bytes 786464 | tf_op jit(solution)/shard_map/all_to_all | solution.py:524
  60.9 2.8 cotangent.1.grad.grad0
  66.1 4.2 %queries.1.q_ref = bf16[512,768]{1,0:T(8,128)(2,1)} custom-call(s32[10]{0:T(128)} %concatenate.50.info, bf16[512,768]{1,0:T(8,128)(2,1)} %get-tuple-element.163.normed, f32[2,384]{1,0:T(2,128)} %bias_own.3, f32[2,384]{1,0:T(2,128)} %copy-done.34, bf16[3,768,384]{2,1,0:T(8,128)(2,1)} %own.7, bf16[1,384,384]{2,1,0:T(8,128)(2,1)} %copy-done.18, ...), custom_call_target="tpu_custom_call" | custom-call | tf_op jit(solution)/shard_map/queries/pallas_call | solution.py:586
  70.2 3.2 collective-permute-done.10.direct
  74.6 15.3 %attend_forward.1 = (bf16[512,768]{1,0:T(8,128)(2,1)}, f32[6,2,512]{2,1,0:T(2,128)}) custom-call(s32[10]{0:T(128)} %concatenate.50.info, bf16[512,768]{1,0:T(8,128)(2,1)} %queries.1.q_ref, bf16[512,768]{1,0:T(8,128)(2,1)} %get-tuple-element.168.ko_ref, bf16[512,768]{1,0:T(8,128)(2,1)} %get-tuple-element.169.vo_ref, bf16[512,768]{1,0:T(8,128)(2,1)} %copy-done.1, ...), custom_call_target="tpu_custom_call" | custom-call | tf_op jit(solution)/shard_map/attend_forward/pallas_call | solution.py:139
  89.9 2.7 collective-permute-done.11.grad.grad1
  92.5 5.1 %middle.1 = (f32[512,768]{1,0:T(8,128)}, bf16[512,768]{1,0:T(8,128)(2,1)}) custom-call(s32[10]{0:T(128)} %concatenate.50.info, bf16[512,768]{1,0:T(8,128)(2,1)} %get-tuple-element.176.heads.out_ref, f32[512,768]{1,0:T(8,128)} %get-tuple-element.177.inputs, f32[3,768]{1,0:T(4,128)} %pad_maximum_fusion.1.norms, bf16[384,768]{1,0:T(8,128)(2,1)} %own.6, ...), custom_call_target="tpu_custom_call" | custom-call | tf_op jit(solution)/shard_map/middle/pallas_call | solution.py:597
  99.1 12.7 %mlp_rows.2 = (f32[512,768]{1,0:T(8,128)}, f32[512,768]{1,0:T(8,128)}, bf16[1536,512]{1,0:T(8,128)(2,1)}, bf16[512,1536]{1,0:T(8,128)(2,1)}, f32[2,1,1536]{2,1,0:T(1,128)}) custom-call(s32[10]{0:T(128)} %concatenate.50.info, bf16[512,768]{1,0:T(8,128)(2,1)} %get-tuple-element.180.normed.normed0, bf16[512,768]{1,0:T(8,128)(2,1)} %cotangent.1.grad.grad0, ...), custom_call_target="tpu_custom_call" | custom-call | tf_op jit(solution)/shard_map/mlp_rows/pallas_call | solution.py:612
  111.9 4.2 %collective-permute-done.13.normed.normed1 = bf16[512,768]{1,0:T(8,128)(2,1)S(1)} collective-permute-done((bf16[512,768]{1,0:T(8,128)(2,1)}, bf16[512,768]{1,0:T(8,128)(2,1)S(1)}, u32[]{:S(2)}, u32[]{:S(2)}) %collective-permute-start.13) | collective-permute-done | bytes 786464 | tf_op jit(solution)/shard_map/ppermute | solution.py:507
  117.0 12.2 %mlp_rows.3 = (bf16[512,768]{1,0:T(8,128)(2,1)}, bf16[512,768]{1,0:T(8,128)(2,1)}, bf16[1536,512]{1,0:T(8,128)(2,1)}, bf16[512,1536]{1,0:T(8,128)(2,1)}, f32[2,1,1536]{2,1,0:T(1,128)}) custom-call(s32[10]{0:T(128)} %concatenate.50.info, bf16[512,768]{1,0:T(8,128)(2,1)} %copy-done.10, bf16[512,768]{1,0:T(8,128)(2,1)} %copy-done.9, bf16[768,1536]{1,0:T(8,128)(2,1)} %fc.3, ...), custom_call_target="tpu_custom_call" | custom-call | tf_op jit(solution)/shard_map/mlp_rows/pallas_call | solution.py:612
  130.1 10.5 %mlp_grads.1 = (bf16[384,3072]{1,0:T(8,128)(2,1)}, bf16[384,3072]{1,0:T(8,128)(2,1)}) custom-call(s32[10]{0:T(128)} %concatenate.50.info, bf16[512,768]{1,0:T(8,128)(2,1)} %get-tuple-element.180.normed.normed0, bf16[512,768]{1,0:T(8,128)(2,1)} %copy-done.10, bf16[512,768]{1,0:T(8,128)(2,1)} %cotangent.1.grad.grad0, bf16[512,768]{1,0:T(8,128)(2,1)} %copy-done.9, ...), custom_call_target="tpu_custom_call" | custom-call | tf_op jit(solution)/shard_map/mlp_grads/pallas_call | solution.py:630
  140.6 6.1 %collective-permute-done.14.back_far = bf16[512,768]{1,0:T(8,128)(2,1)S(1)} collective-permute-done((bf16[512,768]{1,0:T(8,128)(2,1)}, bf16[512,768]{1,0:T(8,128)(2,1)S(1)}, u32[]{:S(2)}, u32[]{:S(2)}) %collective-permute-start.14) | collective-permute-done | bytes 786464 | tf_op jit(solution)/shard_map/ppermute | solution.py:507
  147.7 6.7 %back.1 = (f32[512,768]{1,0:T(8,128)}, bf16[512,768]{1,0:T(8,128)(2,1)}, bf16[512,768]{1,0:T(8,128)(2,1)}, f32[4,768]{1,0:T(4,128)}) custom-call(s32[10]{0:T(128)} %concatenate.50.info, f32[512,768]{1,0:T(8,128)} %get-tuple-element.193.back, bf16[512,768]{1,0:T(8,128)(2,1)} %copy-done.25, f32[512,768]{1,0:T(8,128)} %get-tuple-element.195.residual, ...), custom_call_target="tpu_custom_call" | custom-call | tf_op jit(solution)/shard_map/back/pallas_call | solution.py:661
  159.2 11.9 %attend_backward.2 = (bf16[512,384]{1,0:T(8,128)(2,1)}, f32[512,384]{1,0:T(8,128)}, f32[512,384]{1,0:T(8,128)}, bf16[512,384]{1,0:T(8,128)(2,1)}, bf16[512,384]{1,0:T(8,128)(2,1)}) custom-call(s32[10]{0:T(128)} %concatenate.50.info, bf16[512,768]{1,0:T(8,128)(2,1)} %queries.1.q_ref, bf16[512,768]{1,0:T(8,128)(2,1)} %get-tuple-element.168.ko_ref, ...), custom_call_target="tpu_custom_call" | custom-call | tf_op jit(solution)/shard_map/attend_backward/pallas_call | solution.py:162
  175.0 3.8 %block.1 = bf16[8,2,64,384]{3,2,1,0:T(8,128)(2,1)} custom-call(s32[10]{0:T(128)} %concatenate.50.info, f32[512,768]{1,0:T(8,128)} %get-tuple-element.195.residual, f32[512,768]{1,0:T(8,128)} %get-tuple-element.216.mlp, bf16[512,768]{1,0:T(8,128)(2,1)} %collective-permute-done.16.mlp_far, f32[1,768]{1,0:T(1,128)} %get-tuple-element.317.bias), custom_call_target="tpu_custom_call" | custom-call | tf_op jit(solution)/shard_map/block/pallas_call | solution.py:694
  179.7 6.0 %attention_grads.2 = (bf16[384,1536]{1,0:T(8,128)(2,1)}, bf16[384,1536]{1,0:T(8,128)(2,1)}) custom-call(s32[10]{0:T(128)} %concatenate.50.info, bf16[512,768]{1,0:T(8,128)(2,1)} %get-tuple-element.163.normed, bf16[512,768]{1,0:T(8,128)(2,1)} %get-tuple-element.176.heads.out_ref, bf16[512,768]{1,0:T(8,128)(2,1)} %get-tuple-element.199.grad_attn, ...), custom_call_target="tpu_custom_call" | custom-call | tf_op jit(solution)/shard_map/attention_grads/pallas_call | solution.py:704
  185.8 2.4 add_convert_fusion.1
  188.9 2.5 add_convert_fusion.2
  194.7 3.9 %all-to-all-start.2 = ((bf16[16,64,384]{2,1,0:T(8,128)(2,1)}), bf16[16,64,384]{2,1,0:T(8,128)(2,1)S(1)}, u32[]{:S(2)}, u32[]{:S(2)}) async-start(bf16[16,64,384]{2,1,0:T(8,128)(2,1)} %bitcast.8), calls=%async_computation.2 | async-start | bytes 1572864 | tf_op jit(solution)/shard_map/all_to_all | solution.py:524
  200.6 11.9 %attend_backward.3 = (bf16[512,384]{1,0:T(8,128)(2,1)}, f32[512,384]{1,0:T(8,128)}, f32[512,384]{1,0:T(8,128)}, bf16[512,384]{1,0:T(8,128)(2,1)}, bf16[512,384]{1,0:T(8,128)(2,1)}) custom-call(s32[10]{0:T(128)} %concatenate.50.info, bf16[512,768]{1,0:T(8,128)(2,1)} %queries.1.q_ref, bf16[512,768]{1,0:T(8,128)(2,1)} %get-tuple-element.168.ko_ref, ...), custom_call_target="tpu_custom_call" | custom-call | tf_op jit(solution)/shard_map/attend_backward/pallas_call | solution.py:162
  212.5 3.9 %collective-permute-done.23 = bf16[96,3072]{1,0:T(8,128)(2,1)} collective-permute-done((bf16[96,3072]{1,0:T(8,128)(2,1)}, bf16[96,3072]{1,0:T(8,128)(2,1)}, u32[]{:S(2)}, u32[]{:S(2)}) %collective-permute-start.23) | collective-permute-done | bytes 589856 | tf_op jit(solution)/shard_map/ppermute | solution.py:510
  219.7 6.0 %attention_grads.3 = (bf16[384,1536]{1,0:T(8,128)(2,1)}, bf16[384,1536]{1,0:T(8,128)(2,1)}) custom-call(s32[10]{0:T(128)} %concatenate.50.info, bf16[512,768]{1,0:T(8,128)(2,1)} %get-tuple-element.163.normed, bf16[512,768]{1,0:T(8,128)(2,1)} %get-tuple-element.176.heads.out_ref, bf16[512,768]{1,0:T(8,128)(2,1)} %get-tuple-element.199.grad_attn, ...), custom_call_target="tpu_custom_call" | custom-call | tf_op jit(solution)/shard_map/attention_grads/pallas_call | solution.py:704
  225.7 9.4 %collective-permute-done.27 = bf16[48,3072]{1,0:T(8,128)(2,1)} collective-permute-done((bf16[48,3072]{1,0:T(8,128)(2,1)}, bf16[48,3072]{1,0:T(8,128)(2,1)}, u32[]{:S(2)}, u32[]{:S(2)}) %collective-permute-start.27) | collective-permute-done | bytes 294944 | tf_op jit(solution)/shard_map/ppermute | solution.py:510
  236.6 3.5 gather_slots.6
  242.2 9.4 %leave.1 = (bf16[8,2,64,384]{3,2,1,0:T(8,128)(2,1)}, f32[4,768]{1,0:T(4,128)}) custom-call(s32[10]{0:T(128)} %concatenate.50.info, f32[512,768]{1,0:T(8,128)} %get-tuple-element.177.inputs, f32[512,768]{1,0:T(8,128)} %get-tuple-element.256.grad_residual, f32[1,768]{1,0:T(1,128)} %copy-done.31, bf16[512,384]{1,0:T(8,128)(2,1)} %get-tuple-element.257.dq.dq0, ...), custom_call_target="tpu_custom_call" | custom-call | tf_op jit(solution)/shard_map/leave/pallas_call | solution.py:741
  251.6 4.4 %collective-permute-done.29 = bf16[192,1536]{1,0:T(8,128)(2,1)S(1)} collective-permute-done((bf16[192,1536]{1,0:T(8,128)(2,1)}, bf16[192,1536]{1,0:T(8,128)(2,1)S(1)}, u32[]{:S(2)}, u32[]{:S(2)}) %collective-permute-start.29) | collective-permute-done | bytes 589856 | tf_op jit(solution)/shard_map/ppermute | solution.py:507
  258.1 4.0 %all-to-all-start.3 = ((bf16[16,64,384]{2,1,0:T(8,128)(2,1)}), bf16[16,64,384]{2,1,0:T(8,128)(2,1)S(1)}, u32[]{:S(2)}, u32[]{:S(2)}) async-start(bf16[16,64,384]{2,1,0:T(8,128)(2,1)} %bitcast.15), calls=%async_computation.3 | async-start | bytes 1572864 | tf_op jit(solution)/shard_map/all_to_all | solution.py:524
  264.3 2.3 add_convert_fusion
  269.4 20.5 %collective-permute-done.32 = bf16[96,3072]{1,0:T(8,128)(2,1)S(1)} collective-permute-done((bf16[96,3072]{1,0:T(8,128)(2,1)S(1)}, bf16[96,3072]{1,0:T(8,128)(2,1)S(1)}, u32[]{:S(2)}, u32[]{:S(2)}) %collective-permute-start.32) | collective-permute-done | bytes 589856 | tf_op jit(solution)/shard_map/ppermute | solution.py:510
  293.3 2.5 collective-permute-done.35
  296.6 2.8 collective-permute-done.34
  302.1 2.4 collective-permute-start.36
  305.5 4.1 %collective-permute-done.36 = bf16[48,1536]{1,0:T(8,128)(2,1)S(1)} collective-permute-done((bf16[48,1536]{1,0:T(8,128)(2,1)S(1)}, bf16[48,1536]{1,0:T(8,128)(2,1)S(1)}, u32[]{:S(2)}, u32[]{:S(2)}) %collective-permute-start.36) | collective-permute-done | bytes 147488 | tf_op jit(solution)/shard_map/ppermute | solution.py:510
  316.1 2.5 collective-permute-done.38
  318.8 3.0 collective-permute-start.41
  321.8 2.2 collective-permute-done.41
  326.2 7.0 %collective-permute-done.43.refs_1_ = bf16[192,3072]{1,0:T(8,128)(2,1)S(1)} collective-permute-done((bf16[192,3072]{1,0:T(8,128)(2,1)S(1)}, bf16[192,3072]{1,0:T(8,128)(2,1)S(1)}, u32[]{:S(2)}, u32[]{:S(2)}) %collective-permute-start.43) | collective-permute-done | bytes 1179680 | tf_op jit(solution)/shard_map/ppermute | solution.py:510
  333.8 3.5 gather_slots.7
  337.5 6.2 %finish_mlp.1 = (f32[768,1536]{1,0:T(8,128)}, f32[1536,768]{1,0:T(8,128)}) custom-call(s32[10]{0:T(128)} %concatenate.50.info, bf16[192,3072]{1,0:T(8,128)(2,1)} %copy-done.3, bf16[192,3072]{1,0:T(8,128)(2,1)} %copy-done.22, bf16[192,3072]{1,0:T(8,128)(2,1)} %copy-done.21, bf16[192,3072]{1,0:T(8,128)(2,1)} %collective-permute-done.45.refs_3_), custom_call_target="tpu_custom_call" | custom-call | tf_op jit(solution)/shard_map/finish_mlp/pallas_call | solution.py:792
  343.7 5.3 %collective-permute-done.42.refs_1_ = bf16[192,1536]{1,0:T(8,128)(2,1)} collective-permute-done((bf16[192,1536]{1,0:T(8,128)(2,1)S(1)}, bf16[192,1536]{1,0:T(8,128)(2,1)}, u32[]{:S(2)}, u32[]{:S(2)}) %collective-permute-start.42) | collective-permute-done | bytes 589856 | tf_op jit(solution)/shard_map/ppermute | solution.py:510
  352.4 4.7 %finish_attention.1 = (f32[3,768,384]{2,1,0:T(8,128)}, f32[384,768]{1,0:T(8,128)}) custom-call(s32[10]{0:T(128)} %concatenate.50.info, bf16[192,1536]{1,0:T(8,128)(2,1)} %copy-done.11, bf16[192,1536]{1,0:T(8,128)(2,1)} %collective-permute-done.42.refs_1_, bf16[192,1536]{1,0:T(8,128)(2,1)} %collective-permute-done.46.refs_2_, bf16[192,1536]{1,0:T(8,128)(2,1)} %copy-done.26), custom_call_target="tpu_custom_call" | custom-call | tf_op jit(solution)/shard_map/finish_attention/pallas_call | solution.py:798
  (219 shorter events, 75.5 us)
Async XLA Ops:
  0.7 27.4 %collective-permute-start.4 = (s32[1,6]{1,0:T(1,128)}, s32[1,6]{1,0:T(1,128)S(1)}, u32[]{:S(2)}, u32[]{:S(2)}) collective-permute-start(s32[1,6]{1,0:T(1,128)} %param.18), channel_id=1, source_target_pairs={{0,2},{1,3},{2,0},{3,1},{4,6},{5,7},{6,4},{7,5},{8,10},{9,11},{10,... | collective-permute-start | bytes 80 | tf_op jit(solution)/shard_map/ppermute | solution.py:510
  1.2 29.2 %collective-permute-start.3 = (f32[2,384]{1,0:T(2,128)}, f32[2,384]{1,0:T(2,128)S(1)}, u32[]{:S(2)}, u32[]{:S(2)}) collective-permute-start(f32[2,384]{1,0:T(2,128)} %bias_own.3), channel_id=1, source_target_pairs={{0,1},{1,0},{2,3},{3,2},{4,5},{5,4},{6,7},{7,6},{8,9},{9,8},{10,11... | collective-permute-start | bytes 9224 | tf_op jit(solution)/shard_map/ppermute | solution.py:507
  5.0 25.4 %collective-permute-start = (bf16[2,384,384]{2,1,0:T(8,128)(2,1)S(1)}, bf16[2,384,384]{2,1,0:T(8,128)(2,1)S(1)}, u32[]{:S(2)}, u32[]{:S(2)}) collective-permute-start(bf16[2,384,384]{2,1,0:T(8,128)(2,1)S(1)} %constant_dynamic-slice_fusion.3), channel_id=1, source_target_pairs={{0,1},{1,0},{2,3},{3,2},{4,5},{5,4},{6,7},{7,6},{8,9},{9,8},{10,11... | collective-permute-start | bytes 1769480 | tf_op jit(solution)/shard_map/ppermute | solution.py:507
  9.3 27.2 %all-to-all-start = ((bf16[16,64,384]{2,1,0:T(8,128)(2,1)}), bf16[16,64,384]{2,1,0:T(8,128)(2,1)S(1)}, u32[]{:S(2)}, u32[]{:S(2)}) async-start(bf16[16,64,384]{2,1,0:T(8,128)(2,1)} %gather_slots.5), calls=%async_computation | async-start | bytes 1572864 | tf_op jit(solution)/shard_map/all_to_all | solution.py:524
  26.0 3.8 %collective-permute-start.2 = (bf16[6,384]{1,0:T(8,128)(2,1)S(1)}, bf16[6,384]{1,0:T(8,128)(2,1)S(1)}, u32[]{:S(2)}, u32[]{:S(2)}) collective-permute-start(bf16[6,384]{1,0:T(8,128)(2,1)S(1)} %get-tuple-element.316), channel_id=1, source_target_pairs={{0,1},{1,0},{2,3},{3,2},{4,5},{5,4},{6,7},{7,6},{8,9},{9,8},{10,11... | collective-permute-start | bytes 13832 | tf_op jit(solution)/shard_map/ppermute | solution.py:507
  36.5 23.6 %all-to-all-start.1 = ((bf16[16,64,384]{2,1,0:T(8,128)(2,1)}), bf16[16,64,384]{2,1,0:T(8,128)(2,1)S(1)}, u32[]{:S(2)}, u32[]{:S(2)}) async-start(bf16[16,64,384]{2,1,0:T(8,128)(2,1)} %gather_slots.4), calls=%async_computation.1 | async-start | bytes 1572864 | tf_op jit(solution)/shard_map/all_to_all | solution.py:524
  51.2 22.2 %collective-permute-start.8 = (bf16[512,768]{1,0:T(8,128)(2,1)}, bf16[512,768]{1,0:T(8,128)(2,1)S(1)}, u32[]{:S(2)}, u32[]{:S(2)}) collective-permute-start(bf16[512,768]{1,0:T(8,128)(2,1)} %get-tuple-element.168.ko_ref), channel_id=1, source_target_pairs={{0,2},{1,3},{2,0},{3,1},{4,6},{5,7},{6,4},{7,5},{8,10},{9,11},{10,... | collective-permute-start | bytes 2359304 | tf_op jit(solution)/shard_map/ppermute | solution.py:510
  51.3 22.1 %collective-permute-start.9 = (bf16[512,768]{1,0:T(8,128)(2,1)}, bf16[512,768]{1,0:T(8,128)(2,1)S(1)}, u32[]{:S(2)}, u32[]{:S(2)}) collective-permute-start(bf16[512,768]{1,0:T(8,128)(2,1)} %get-tuple-element.169.vo_ref), channel_id=1, source_target_pairs={{0,2},{1,3},{2,0},{3,1},{4,6},{5,7},{6,4},{7,5},{8,10},{9,11},{10,... | collective-permute-start | bytes 2359304 | tf_op jit(solution)/shard_map/ppermute | solution.py:510
  51.7 12.0 %collective-permute-start.6 = (bf16[1,384,384]{2,1,0:T(8,128)(2,1)S(1)}, bf16[1,384,384]{2,1,0:T(8,128)(2,1)S(1)}, u32[]{:S(2)}, u32[]{:S(2)}) collective-permute-start(bf16[1,384,384]{2,1,0:T(8,128)(2,1)S(1)} %constant_dynamic-slice_fusion), channel_id=1, source_target_pairs={{0,1},{1,0},{2,3},{3,2},{4,5},{5,4},{6,7},{7,6},{8,9},{9,8},{10,11... | collective-permute-start | bytes 884744 | tf_op jit(solution)/shard_map/ppermute | solution.py:507
  63.8 9.6 %collective-permute-start.10 = (bf16[384,384]{1,0:T(8,128)(2,1)}, bf16[384,384]{1,0:T(8,128)(2,1)S(1)}, u32[]{:S(2)}, u32[]{:S(2)}) collective-permute-start(bf16[384,384]{1,0:T(8,128)(2,1)} %constant_dynamic-slice_fusion.2), channel_id=1, source_target_pairs={{0,1},{1,0},{2,3},{3,2},{4,5},{5,4},{6,7},{7,6},{8,9},{9,8},{10,11... | collective-permute-start | bytes 884744 | tf_op jit(solution)/shard_map/ppermute | solution.py:507
  73.4 19.1 %collective-permute-start.11 = (bf16[512,768]{1,0:T(8,128)(2,1)S(1)}, bf16[512,768]{1,0:T(8,128)(2,1)S(1)}, u32[]{:S(2)}, u32[]{:S(2)}) collective-permute-start(bf16[512,768]{1,0:T(8,128)(2,1)S(1)} %copy-done), channel_id=1, source_target_pairs={{0,1},{1,0},{2,3},{3,2},{4,5},{5,4},{6,7},{7,6},{8,9},{9,8},{10,11... | collective-permute-start | bytes 2359304 | tf_op jit(solution)/shard_map/ppermute | solution.py:507
  74.3 18.3 %collective-permute-start.12 = (bf16[384,384]{1,0:T(8,128)(2,1)S(1)}, bf16[384,384]{1,0:T(8,128)(2,1)}, u32[]{:S(2)}, u32[]{:S(2)}) collective-permute-start(bf16[384,384]{1,0:T(8,128)(2,1)S(1)} %collective-permute-done.10.direct), channel_id=1, source_target_pairs={{0,2},{1,3},{2,0},{3,1},{4,6},{5,7},{6,4},{7,5},{8,10},{9,11},{10,... | collective-permute-start | bytes 884744 | tf_op jit(solution)/shard_map/ppermute | solution.py:510
  97.6 18.5 %collective-permute-start.13 = (bf16[512,768]{1,0:T(8,128)(2,1)}, bf16[512,768]{1,0:T(8,128)(2,1)S(1)}, u32[]{:S(2)}, u32[]{:S(2)}) collective-permute-start(bf16[512,768]{1,0:T(8,128)(2,1)} %get-tuple-element.180.normed.normed0), channel_id=1, source_target_pairs={{0,1},{1,0},{2,3},{3,2},{4,5},{5,4},{6,7},{7,6},{8,9},{9,8},{10,11... | collective-permute-start | bytes 2359304 | tf_op jit(solution)/shard_map/ppermute | solution.py:507
  129.1 17.6 %collective-permute-start.14 = (bf16[512,768]{1,0:T(8,128)(2,1)}, bf16[512,768]{1,0:T(8,128)(2,1)S(1)}, u32[]{:S(2)}, u32[]{:S(2)}) collective-permute-start(bf16[512,768]{1,0:T(8,128)(2,1)} %get-tuple-element.184), channel_id=1, source_target_pairs={{0,1},{1,0},{2,3},{3,2},{4,5},{5,4},{6,7},{7,6},{8,9},{9,8},{10,11... | collective-permute-start | bytes 2359304 | tf_op jit(solution)/shard_map/ppermute | solution.py:507
  146.8 7.7 %collective-permute-start.15 = (bf16[384,3072]{1,0:T(8,128)(2,1)}, bf16[384,3072]{1,0:T(8,128)(2,1)}, u32[]{:S(2)}, u32[]{:S(2)}) collective-permute-start(bf16[384,3072]{1,0:T(8,128)(2,1)} %get-tuple-element.197), channel_id=1, source_target_pairs={{0,2},{1,3},{2,0},{3,1},{4,6},{5,7},{6,4},{7,5},{8,10},{9,11},{10,... | collective-permute-start | bytes 7077896 | tf_op jit(solution)/shard_map/ppermute | solution.py:510
  146.8 24.4 %collective-permute-start.16 = (bf16[512,768]{1,0:T(8,128)(2,1)}, bf16[512,768]{1,0:T(8,128)(2,1)}, u32[]{:S(2)}, u32[]{:S(2)}) collective-permute-start(bf16[512,768]{1,0:T(8,128)(2,1)} %get-tuple-element.200), channel_id=1, source_target_pairs={{0,1},{1,0},{2,3},{3,2},{4,5},{5,4},{6,7},{7,6},{8,9},{9,8},{10,11... | collective-permute-start | bytes 2359304 | tf_op jit(solution)/shard_map/ppermute | solution.py:507
  157.7 15.6 %collective-permute-start.17 = (bf16[96,3072]{1,0:T(8,128)(2,1)S(1)}, bf16[96,3072]{1,0:T(8,128)(2,1)}, u32[]{:S(2)}, u32[]{:S(2)}) collective-permute-start(bf16[96,3072]{1,0:T(8,128)(2,1)S(1)} %add_convert_fusion.4), channel_id=1, source_target_pairs={{0,4},{1,5},{2,6},{3,7},{4,0},{5,1},{6,2},{7,3},{8,12},{9,13},{10,... | collective-permute-start | bytes 1769480 | tf_op jit(solution)/shard_map/ppermute | solution.py:510
  173.3 5.5 %collective-permute-start.18 = (bf16[512,384]{1,0:T(8,128)(2,1)}, bf16[512,384]{1,0:T(8,128)(2,1)S(1)}, u32[]{:S(2)}, u32[]{:S(2)}) collective-permute-start(bf16[512,384]{1,0:T(8,128)(2,1)} %get-tuple-element.214), channel_id=1, source_target_pairs={{0,2},{1,3},{2,0},{3,1},{4,6},{5,7},{6,4},{7,5},{8,10},{9,11},{10,... | collective-permute-start | bytes 1179656 | tf_op jit(solution)/shard_map/ppermute | solution.py:510
  173.3 5.5 %collective-permute-start.19 = (bf16[512,384]{1,0:T(8,128)(2,1)}, bf16[512,384]{1,0:T(8,128)(2,1)S(1)}, u32[]{:S(2)}, u32[]{:S(2)}) collective-permute-start(bf16[512,384]{1,0:T(8,128)(2,1)} %get-tuple-element.215), channel_id=1, source_target_pairs={{0,2},{1,3},{2,0},{3,1},{4,6},{5,7},{6,4},{7,5},{8,10},{9,11},{10,... | collective-permute-start | bytes 1179656 | tf_op jit(solution)/shard_map/ppermute | solution.py:510
  173.8 11.9 %collective-permute-start.20 = (bf16[48,3072]{1,0:T(8,128)(2,1)}, bf16[48,3072]{1,0:T(8,128)(2,1)S(1)}, u32[]{:S(2)}, u32[]{:S(2)}) collective-permute-start(bf16[48,3072]{1,0:T(8,128)(2,1)} %get-tuple-element.224), channel_id=1, source_target_pairs={{0,4},{1,5},{2,6},{3,7},{4,0},{5,1},{6,2},{7,3},{8,12},{9,13},{10,... | collective-permute-start | bytes 884744 | tf_op jit(solution)/shard_map/ppermute | solution.py:510
  185.7 3.3 collective-permute-start.21
  191.5 21.0 %collective-permute-start.22 = (bf16[192,1536]{1,0:T(8,128)(2,1)}, bf16[192,1536]{1,0:T(8,128)(2,1)}, u32[]{:S(2)}, u32[]{:S(2)}) collective-permute-start(bf16[192,1536]{1,0:T(8,128)(2,1)} %get-tuple-element.229), channel_id=1, source_target_pairs={{0,1},{1,0},{2,3},{3,2},{4,5},{5,4},{6,7},{7,6},{8,9},{9,8},{10,11... | collective-permute-start | bytes 1769480 | tf_op jit(solution)/shard_map/ppermute | solution.py:507
  192.9 23.4 %collective-permute-start.23 = (bf16[96,3072]{1,0:T(8,128)(2,1)}, bf16[96,3072]{1,0:T(8,128)(2,1)}, u32[]{:S(2)}, u32[]{:S(2)}) collective-permute-start(bf16[96,3072]{1,0:T(8,128)(2,1)} %add_convert_fusion.1), channel_id=1, source_target_pairs={{0,8},{1,9},{2,10},{3,11},{4,12},{5,13},{6,14},{7,15},{8,0},{9,1},... | collective-permute-start | bytes 1769480 | tf_op jit(solution)/shard_map/ppermute | solution.py:510
  194.7 41.0 %all-to-all-start.2 = ((bf16[16,64,384]{2,1,0:T(8,128)(2,1)}), bf16[16,64,384]{2,1,0:T(8,128)(2,1)S(1)}, u32[]{:S(2)}, u32[]{:S(2)}) async-start(bf16[16,64,384]{2,1,0:T(8,128)(2,1)} %bitcast.8), calls=%async_computation.2 | async-start | bytes 1572864 | tf_op jit(solution)/shard_map/all_to_all | solution.py:524
  198.6 13.8 %collective-permute-start.24 = (bf16[48,3072]{1,0:T(8,128)(2,1)S(1)}, bf16[48,3072]{1,0:T(8,128)(2,1)}, u32[]{:S(2)}, u32[]{:S(2)}) collective-permute-start(bf16[48,3072]{1,0:T(8,128)(2,1)S(1)} %copy-done.29), channel_id=1, source_target_pairs={{0,4},{1,5},{2,6},{3,7},{4,0},{5,1},{6,2},{7,3},{8,12},{9,13},{10,... | collective-permute-start | bytes 884744 | tf_op jit(solution)/shard_map/ppermute | solution.py:510
  216.4 2.5 collective-permute-start.25
  216.4 2.6 collective-permute-start.26
  219.0 16.1 %collective-permute-start.27 = (bf16[48,3072]{1,0:T(8,128)(2,1)}, bf16[48,3072]{1,0:T(8,128)(2,1)}, u32[]{:S(2)}, u32[]{:S(2)}) collective-permute-start(bf16[48,3072]{1,0:T(8,128)(2,1)} %add_convert_fusion.7), channel_id=1, source_target_pairs={{0,16},{1,17},{2,18},{3,19},{4,20},{5,21},{6,22},{7,23},{8,24},{9,... | collective-permute-start | bytes 884744 | tf_op jit(solution)/shard_map/ppermute | solution.py:510
  235.1 23.0 %collective-permute-start.28 = (bf16[384,1536]{1,0:T(8,128)(2,1)}, bf16[384,1536]{1,0:T(8,128)(2,1)}, u32[]{:S(2)}, u32[]{:S(2)}) collective-permute-start(bf16[384,1536]{1,0:T(8,128)(2,1)} %get-tuple-element.264), channel_id=1, source_target_pairs={{0,2},{1,3},{2,0},{3,1},{4,6},{5,7},{6,4},{7,5},{8,10},{9,11},{10,... | collective-permute-start | bytes 3538952 | tf_op jit(solution)/shard_map/ppermute | solution.py:510
  240.1 15.9 %collective-permute-start.29 = (bf16[192,1536]{1,0:T(8,128)(2,1)}, bf16[192,1536]{1,0:T(8,128)(2,1)S(1)}, u32[]{:S(2)}, u32[]{:S(2)}) collective-permute-start(bf16[192,1536]{1,0:T(8,128)(2,1)} %get-tuple-element.265), channel_id=1, source_target_pairs={{0,1},{1,0},{2,3},{3,2},{4,5},{5,4},{6,7},{7,6},{8,9},{9,8},{10,11... | collective-permute-start | bytes 1769480 | tf_op jit(solution)/shard_map/ppermute | solution.py:507
  242.0 16.1 %collective-permute-start.30 = (bf16[48,3072]{1,0:T(8,128)(2,1)S(1)}, bf16[48,3072]{1,0:T(8,128)(2,1)S(1)}, u32[]{:S(2)}, u32[]{:S(2)}) collective-permute-start(bf16[48,3072]{1,0:T(8,128)(2,1)S(1)} %add_convert_fusion.6), channel_id=1, source_target_pairs={{0,16},{1,17},{2,18},{3,19},{4,20},{5,21},{6,22},{7,23},{8,24},{9,... | collective-permute-start | bytes 884744 | tf_op jit(solution)/shard_map/ppermute | solution.py:510
  258.1 41.3 %all-to-all-start.3 = ((bf16[16,64,384]{2,1,0:T(8,128)(2,1)}), bf16[16,64,384]{2,1,0:T(8,128)(2,1)S(1)}, u32[]{:S(2)}, u32[]{:S(2)}) async-start(bf16[16,64,384]{2,1,0:T(8,128)(2,1)} %bitcast.15), calls=%async_computation.3 | async-start | bytes 1572864 | tf_op jit(solution)/shard_map/all_to_all | solution.py:524
  262.3 27.6 %collective-permute-start.32 = (bf16[96,3072]{1,0:T(8,128)(2,1)S(1)}, bf16[96,3072]{1,0:T(8,128)(2,1)S(1)}, u32[]{:S(2)}, u32[]{:S(2)}) collective-permute-start(bf16[96,3072]{1,0:T(8,128)(2,1)S(1)} %maximum_select_fusion.1), channel_id=1, source_target_pairs={{0,8},{1,9},{2,10},{3,11},{4,12},{5,13},{6,14},{7,15},{8,0},{9,1},... | collective-permute-start | bytes 1769480 | tf_op jit(solution)/shard_map/ppermute | solution.py:510
  266.5 23.3 %collective-permute-start.31 = (bf16[192,1536]{1,0:T(8,128)(2,1)}, bf16[192,1536]{1,0:T(8,128)(2,1)}, u32[]{:S(2)}, u32[]{:S(2)}) collective-permute-start(bf16[192,1536]{1,0:T(8,128)(2,1)} %add_convert_fusion), channel_id=1, source_target_pairs={{0,4},{1,5},{2,6},{3,7},{4,0},{5,1},{6,2},{7,3},{8,12},{9,13},{10,... | collective-permute-start | bytes 1769480 | tf_op jit(solution)/shard_map/ppermute | solution.py:510
  291.2 8.2 %collective-permute-start.34 = (bf16[96,1536]{1,0:T(8,128)(2,1)S(1)}, bf16[96,1536]{1,0:T(8,128)(2,1)}, u32[]{:S(2)}, u32[]{:S(2)}) collective-permute-start(bf16[96,1536]{1,0:T(8,128)(2,1)S(1)} %add_convert_fusion.5), channel_id=1, source_target_pairs={{0,8},{1,9},{2,10},{3,11},{4,12},{5,13},{6,14},{7,15},{8,0},{9,1},... | collective-permute-start | bytes 884744 | tf_op jit(solution)/shard_map/ppermute | solution.py:510
  291.6 4.2 %collective-permute-start.35 = (f32[12,768]{1,0:T(8,128)S(1)}, f32[12,768]{1,0:T(8,128)}, u32[]{:S(2)}, u32[]{:S(2)}) collective-permute-start(f32[12,768]{1,0:T(8,128)S(1)} %fusion.3), channel_id=1, source_target_pairs={{0,1},{1,0},{2,3},{3,2},{4,5},{5,4},{6,7},{7,6},{8,9},{9,8},{10,11... | collective-permute-start | bytes 110600 | tf_op jit(solution)/shard_map/ppermute | solution.py:507
  299.4 6.1 %collective-permute-start.37 = (f32[12,768]{1,0:T(8,128)S(1)}, f32[12,768]{1,0:T(8,128)S(1)}, u32[]{:S(2)}, u32[]{:S(2)}) collective-permute-start(f32[12,768]{1,0:T(8,128)S(1)} %add.296), channel_id=1, source_target_pairs={{0,4},{1,5},{2,6},{3,7},{4,0},{5,1},{6,2},{7,3},{8,12},{9,13},{10,... | collective-permute-start | bytes 110600 | tf_op jit(solution)/shard_map/ppermute | solution.py:510
  302.1 7.5 %collective-permute-start.36 = (bf16[48,1536]{1,0:T(8,128)(2,1)S(1)}, bf16[48,1536]{1,0:T(8,128)(2,1)S(1)}, u32[]{:S(2)}, u32[]{:S(2)}) collective-permute-start(bf16[48,1536]{1,0:T(8,128)(2,1)S(1)} %add_convert_fusion.11), channel_id=1, source_target_pairs={{0,16},{1,17},{2,18},{3,19},{4,20},{5,21},{6,22},{7,23},{8,24},{9,... | collective-permute-start | bytes 442376 | tf_op jit(solution)/shard_map/ppermute | solution.py:510
  304.7 21.4 %collective-permute-start.44 = (bf16[192,3072]{1,0:T(8,128)(2,1)S(1)}, bf16[192,3072]{1,0:T(8,128)(2,1)S(1)}, u32[]{:S(2)}, u32[]{:S(2)}) collective-permute-start(bf16[192,3072]{1,0:T(8,128)(2,1)S(1)} %maximum_select_fusion.refs_0_), channel_id=1, source_target_pairs={{0,2},{1,3},{2,0},{3,1},{4,6},{5,7},{6,4},{7,5},{8,10},{9,11},{10,... | collective-permute-start | bytes 3538952 | tf_op jit(solution)/shard_map/ppermute | solution.py:510
  304.8 28.4 %collective-permute-start.43 = (bf16[192,3072]{1,0:T(8,128)(2,1)S(1)}, bf16[192,3072]{1,0:T(8,128)(2,1)S(1)}, u32[]{:S(2)}, u32[]{:S(2)}) collective-permute-start(bf16[192,3072]{1,0:T(8,128)(2,1)S(1)} %maximum_select_fusion.refs_0_), channel_id=1, source_target_pairs={{0,4},{1,5},{2,6},{3,7},{4,0},{5,1},{6,2},{7,3},{8,12},{9,13},{10,... | collective-permute-start | bytes 3538952 | tf_op jit(solution)/shard_map/ppermute | solution.py:510
  310.8 7.8 %collective-permute-start.38 = (bf16[48,1536]{1,0:T(8,128)(2,1)S(1)}, bf16[48,1536]{1,0:T(8,128)(2,1)S(1)}, u32[]{:S(2)}, u32[]{:S(2)}) collective-permute-start(bf16[48,1536]{1,0:T(8,128)(2,1)S(1)} %add_convert_fusion.10), channel_id=1, source_target_pairs={{0,16},{1,17},{2,18},{3,19},{4,20},{5,21},{6,22},{7,23},{8,24},{9,... | collective-permute-start | bytes 442376 | tf_op jit(solution)/shard_map/ppermute | solution.py:510
  312.0 4.1 %collective-permute-start.39 = (f32[12,768]{1,0:T(8,128)S(1)}, f32[12,768]{1,0:T(8,128)S(1)}, u32[]{:S(2)}, u32[]{:S(2)}) collective-permute-start(f32[12,768]{1,0:T(8,128)S(1)} %add.303), channel_id=1, source_target_pairs={{0,8},{1,9},{2,10},{3,11},{4,12},{5,13},{6,14},{7,15},{8,0},{9,1},... | collective-permute-start | bytes 110600 | tf_op jit(solution)/shard_map/ppermute | solution.py:510
  318.7 7.3 %collective-permute-start.40 = (bf16[96,1536]{1,0:T(8,128)(2,1)S(1)}, bf16[96,1536]{1,0:T(8,128)(2,1)S(1)}, u32[]{:S(2)}, u32[]{:S(2)}) collective-permute-start(bf16[96,1536]{1,0:T(8,128)(2,1)S(1)} %maximum_select_fusion.3), channel_id=1, source_target_pairs={{0,8},{1,9},{2,10},{3,11},{4,12},{5,13},{6,14},{7,15},{8,0},{9,1},... | collective-permute-start | bytes 884744 | tf_op jit(solution)/shard_map/ppermute | solution.py:510
  318.8 5.2 %collective-permute-start.41 = (f32[12,768]{1,0:T(8,128)S(1)}, f32[12,768]{1,0:T(8,128)S(1)}, u32[]{:S(2)}, u32[]{:S(2)}) collective-permute-start(f32[12,768]{1,0:T(8,128)S(1)} %add.305), channel_id=1, source_target_pairs={{0,16},{1,17},{2,18},{3,19},{4,20},{5,21},{6,22},{7,23},{8,24},{9,... | collective-permute-start | bytes 110600 | tf_op jit(solution)/shard_map/ppermute | solution.py:510
  333.2 4.3 %collective-permute-start.45 = (bf16[192,3072]{1,0:T(8,128)(2,1)S(1)}, bf16[192,3072]{1,0:T(8,128)(2,1)}, u32[]{:S(2)}, u32[]{:S(2)}) collective-permute-start(bf16[192,3072]{1,0:T(8,128)(2,1)S(1)} %collective-permute-done.43.refs_1_), channel_id=1, source_target_pairs={{0,2},{1,3},{2,0},{3,1},{4,6},{5,7},{6,4},{7,5},{8,10},{9,11},{10,... | collective-permute-start | bytes 3538952 | tf_op jit(solution)/shard_map/ppermute | solution.py:510
  333.2 15.8 %collective-permute-start.42 = (bf16[192,1536]{1,0:T(8,128)(2,1)S(1)}, bf16[192,1536]{1,0:T(8,128)(2,1)}, u32[]{:S(2)}, u32[]{:S(2)}) collective-permute-start(bf16[192,1536]{1,0:T(8,128)(2,1)S(1)} %maximum_select_fusion.2.refs_0_), channel_id=1, source_target_pairs={{0,4},{1,5},{2,6},{3,7},{4,0},{5,1},{6,2},{7,3},{8,12},{9,13},{10,... | collective-permute-start | bytes 1769480 | tf_op jit(solution)/shard_map/ppermute | solution.py:510
  337.2 14.3 %collective-permute-start.46 = (bf16[192,1536]{1,0:T(8,128)(2,1)S(1)}, bf16[192,1536]{1,0:T(8,128)(2,1)}, u32[]{:S(2)}, u32[]{:S(2)}) collective-permute-start(bf16[192,1536]{1,0:T(8,128)(2,1)S(1)} %maximum_select_fusion.2.refs_0_), channel_id=1, source_target_pairs={{0,2},{1,3},{2,0},{3,1},{4,6},{5,7},{6,4},{7,5},{8,10},{9,11},{10,... | collective-permute-start | bytes 1769480 | tf_op jit(solution)/shard_map/ppermute | solution.py:510
  349.0 2.5 collective-permute-start.47
  (50 other events, 282.6 us)
where the time goes:
time: 359 us; the launch traced here: 357 us
  Pallas kernels  150 us (42%)
  waiting for transfers between devices  107 us (30%)
  starting transfers between devices  59.4 us (17%)
  other arithmetic  22.8 us (6%)
  local copies, waits for them, and re-layouts  14.8 us (4%)
    ppermute x36, waiting for transfers between devices, flip(): return lax.ppermute(value, AXES, bit_pairs[bit])  71 us
    pallas_call x2, Pallas kernels, mlp_rows(): call(mlp_rows_kernel, 'mlp_rows', (steps, 3), [by_row, by_row, spec((widt...  24.9 us
    ppermute x36, starting transfers between devices, flip(): return lax.ppermute(value, AXES, bit_pairs[bit])  24.5 us
    pallas_call x2, Pallas kernels, attend_backward(): pl.pallas_call(functools.partial(attend_backward_kernel, tile, block), gr...  23.7 us
    ppermute x12, waiting for transfers between devices, cross(): return lax.ppermute(value, AXES, tensor_pairs)  23.6 us
    all_to_all x4, starting transfers between devices, exchange(): lax.all_to_all(array, AXES, split_axis=0, concat_axis=0, tiled=True, axis...  20.1 us
    convert_element_type x10, other arithmetic, rows_sum(): return total.astype(BF16)  17.7 us
    pallas_call x1, Pallas kernels, attend_forward(): pl.pallas_call(functools.partial(attend_forward_kernel, tile, block), gri...  15.3 us
  transfers between devices with their start and end apart: 52, of which 27 were waited for; matrix products, arithmetic and copies ran while one was open for 8% of the time, Pallas kernels for 36%

commit v1 on v0

--- a/solution.py
+++ b/solution.py
@@ -577,18 +577,19 @@
             [rowwise] * 4, [rows_f, rows_bf, rows_bf, rows_bf],
         )(info, dealt, thought_rows, norms_in, qv_bias, qv_other,
           qkv_weight, qkv_weight, kv_direct, kv_partner)
+        q_direct, keys_own, values_own, normed = lax.optimization_barrier((q_direct, keys_own, values_own, normed))
+        q_partner = flip(q_direct)
         keys_other, values_other = flip(keys_own), flip(values_own)
-        grad_mlp = call(
-            functools.partial(cotangent_kernel, tile, block), "cotangent", (steps,), [pieces_spec], rowwise, rows_bf
-        )(info, cot_pieces)
-        q_direct, grad_mlp = lax.optimization_barrier((q_direct, grad_mlp))
-        q_partner = flip(q_direct)
         queries = call(
             queries_kernel, "queries", (steps,),
             [rowwise, whole((2, half_width)), whole((2, half_width)), one, *q_specs], rowwise, rows_bf,
         )(info, normed, qv_bias, qv_other, qkv_weight, q_direct, q_partner)
-        queries, grad_mlp, keys_other, values_other, out_direct = lax.optimization_barrier(
-            (queries, grad_mlp, keys_other, values_other, out_direct)
+        queries, out_direct, cot_pieces = lax.optimization_barrier((queries, out_direct, cot_pieces))
+        grad_mlp = call(
+            functools.partial(cotangent_kernel, tile, block), "cotangent", (steps,), [pieces_spec], rowwise, rows_bf
+        )(info, cot_pieces)
+        queries, grad_mlp, keys_other, values_other = lax.optimization_barrier(
+            (queries, grad_mlp, keys_other, values_other)
         )
         grad_far = cross(grad_mlp)
         out_partner = flip(out_direct)
@@ -719,24 +720,27 @@
         x_first = cross(x_first)
         mlp_stage = flip(mlp_stage, upper[0])
         own = backward(0, grad_heads)
-        x_first, x_last, mlp_stage, *tied = lax.optimization_barrier((x_first, x_last, mlp_stage, *over_y[2:], *own))
+        x_first, x_last, mlp_stage, block_back, *tied = lax.optimization_barrier(
+            (x_first, x_last, mlp_stage, block_back, *over_y[2:], *own)
+        )
         over_y[2:], own = tied[: levels - 1], tied[levels - 1 :]
         x_last = cross(x_last)
         mlp_rows_kept.append((mlp_stage, -starts[1]))
         own, (mlp_stage,) = with_far(own, mlp_section(1))
         mlp_stage = flip(mlp_stage, upper[1])
         keep_own, send_own = attention_grads(0, own)
-        keep_own, send_own, mlp_stage = lax.optimization_barrier((keep_own, send_own, mlp_stage))
+        block_out = gather_slots(restore, block_back, F32)
+        got_own, mlp_stage, block_out = lax.optimization_barrier((flip(send_own), mlp_stage, block_out))
         mlp_rows_kept.append((mlp_stage, -starts[2]))
         for level in range(2, levels):
             mlp_rows_kept.append((flip(mlp_section(level), upper[level]), -starts[level + 1]))
         mlp_piece = mlp_section(levels)
         for level in reversed(range(2, levels)):
             mlp_piece = widen(level, mlp_piece, flip(mlp_piece, upper[level]))
-        block_out = gather_slots(restore, block_back, F32)
-        mlp_piece, block_out, *own = lax.optimization_barrier((mlp_piece, block_out, *own))
+        sent = rows_sum([(keep_own, (1 - near) * half), (got_own, (1 - near) * half), (x_first, 0)], 0, half)
+        sent, mlp_piece, *own = lax.optimization_barrier((sent, mlp_piece, *own))
+        over_bit = flip(sent, 1)
         mlp_stage = flip(mlp_piece, upper[1])
-        got_own = flip(send_own)
         half_rows = spec((tile, half_width), lambda i, _: (i, 0))
         input_pieces, small_attn = call(
             functools.partial(leave_kernel, tile, block), "leave", (steps,),
@@ -745,14 +749,9 @@
             [like((slots // 2, 2, block, half_width), BF16), like((4, width), F32)],
             [pltpu.VMEM((tile, width), F32)],
         )(info, inputs, grad_residual, norm_gain[:1], *own, *other, qkv_weight, kv_direct, kv_partner, q_direct, q_partner)
-        input_pieces, small_attn, got_own, x_last, mlp_stage = lax.optimization_barrier(
-            (input_pieces, small_attn, got_own, x_last, mlp_stage)
+        input_pieces, small_attn, over_bit, mlp_stage, x_last = lax.optimization_barrier(
+            (input_pieces, small_attn, over_bit, mlp_stage, x_last)
         )
-        sent = rows_sum([(keep_own, (1 - near) * half), (got_own, (1 - near) * half), (x_first, 0)], 0, half)
-        over_bit = flip(sent, 1)
-        mlp_piece = widen(1, mlp_piece, mlp_stage)
-        mlp_stage = flip(mlp_piece, upper[0])
-        input_back = exchange(input_pieces.reshape(slots, block, half_width))
 
         def ordered(vectors):
             return join(side, vectors[:, :half_width], vectors[:, half_width:], axis=1)
@@ -761,27 +760,34 @@
         fcb0 = jnp.sum(fcb0 + fcb1, axis=0)
         fcb = join(side, fcb0, jnp.zeros_like(fcb0), axis=1).reshape(hidden // width, width)
         small = jnp.concatenate([small_mlp, small_attn[:2], ordered(small_attn[2:]), fcb], axis=0)
-        links = [flip, cross, *[functools.partial(flip, bit=bit) for bit in range(1, bits)]]
+        links = [functools.partial(flip, bit=1), flip, cross, *[functools.partial(flip, bit=bit) for bit in upper]]
 
         def add_over(value):
             return value + links.pop(0)(value) if links else value
 
-        small = add_over(small)
-        over_bit, mlp_stage, small = lax.optimization_barrier((over_bit, mlp_stage, small))
-        mlp_piece = widen(0, mlp_piece, mlp_stage)
         kept = [(keep_own, near * half), (got_own, near * half), (x_last, 0), (over_bit, 0)]
         for level in range(levels):
             stage = flip(rows_sum(kept, *section(level)), upper[level])
             if level == 0:
+                mlp_piece = widen(1, mlp_piece, mlp_stage)
+                mlp_stage = flip(mlp_piece, upper[0])
+            small = add_over(small)
+            stage, small = lax.optimization_barrier((stage, small))
+            if level == 1:
+                stage, mlp_stage, input_pieces = lax.optimization_barrier((stage, mlp_stage, input_pieces))
+                mlp_piece = widen(0, mlp_piece, mlp_stage)
                 mlp_over, mlp_core = flip(mlp_piece, 1), flip(mlp_piece)
-            small = add_over(small)
-            stage, small, input_back = lax.optimization_barrier((stage, small, input_back))
+                input_back = exchange(input_pieces.reshape(slots, block, half_width))
             kept.append((stage, -starts[level + 1]))
         piece = rows_sum(kept, *section(levels))
         for level in reversed(range(levels)):
             stage = flip(piece, upper[level])
             small = add_over(small)
             stage, small = lax.optimization_barrier((stage, small))
+            if level == levels - 1:
+                stage, mlp_core = lax.optimization_barrier((stage, mlp_core))
+            if level == 0:
+                stage, mlp_over, input_back = lax.optimization_barrier((stage, mlp_over, input_back))
             piece = widen(level, piece, stage)
         while links:
             small = add_over(small)

time: 359 us -> 365 us (1.017)
  starting transfers between devices: 59.4 us -> 64.1 us
  waiting for transfers between devices: 107 us -> 103 us
  local copies, waits for them, and re-layouts: 14.8 us -> 18.7 us
    all_to_all x4, waiting for transfers between devices: 12.5 us -> 6.05 us  [exchange(): lax.all_to_all(array, AXES, split_axis=0, concat_axis=0, tiled=True, axis...]
    ppermute x12, waiting for transfers between devices: 23.6 us -> 28.6 us  [cross(): return lax.ppermute(value, AXES, tensor_pairs)]
    unnamed x92 -> x102, local copies, waits for them, and re-layouts: 6.96 us -> 10 us
  transfers between devices with their start and end apart: 52 -> 52, of which waited for: 27 -> 24; matrix products, arithmetic and copies ran while one was open for 8% -> 8% of each run, Pallas kernels for 36% -> 33%
where the time goes in v1:
time: 365 us; the launch traced here: 363 us
  Pallas kernels  150 us (41%)
  waiting for transfers between devices  103 us (28%)
  starting transfers between devices  64.1 us (18%)
  other arithmetic  24.4 us (7%)
  local copies, waits for them, and re-layouts  18.7 us (5%)
    ppermute x36, waiting for transfers between devices, flip(): return lax.ppermute(value, AXES, bit_pairs[bit])  68.6 us
    ppermute x12, waiting for transfers between devices, cross(): return lax.ppermute(value, AXES, tensor_pairs)  28.6 us
    ppermute x36, starting transfers between devices, flip(): return lax.ppermute(value, AXES, bit_pairs[bit])  25.9 us
    pallas_call x2, Pallas kernels, mlp_rows(): call(mlp_rows_kernel, 'mlp_rows', (steps, 3), [by_row, by_row, spec((widt...  24.9 us
    pallas_call x2, Pallas kernels, attend_backward(): pl.pallas_call(functools.partial(attend_backward_kernel, tile, block), gr...  23.8 us
    all_to_all x4, starting transfers between devices, exchange(): lax.all_to_all(array, AXES, split_axis=0, concat_axis=0, tiled=True, axis...  22.9 us
    convert_element_type x10, other arithmetic, rows_sum(): return total.astype(BF16)  17.9 us
    pallas_call x1, Pallas kernels, attend_forward(): pl.pallas_call(functools.partial(attend_forward_kernel, tile, block), gri...  15.3 us
  transfers between devices with their start and end apart: 52, of which 24 were waited for; matrix products, arithmetic and copies ran while one was open for 8% of the time, Pallas kernels for 33%

profile of v1, /device:TPU:0, one launch (start us, length us, event | category | flops | bytes accessed | tf_op | source)
XLA Modules:
  0.0 363.2 jit_solution(10652645413510772325)
XLA Ops:
  1.2 2.6 collective-permute-start.3
  6.0 3.3 gather_slots.5
  9.3 7.3 %all-to-all-start = ((bf16[16,64,384]{2,1,0:T(8,128)(2,1)}), bf16[16,64,384]{2,1,0:T(8,128)(2,1)S(1)}, u32[]{:S(2)}, u32[]{:S(2)}) async-start(bf16[16,64,384]{2,1,0:T(8,128)(2,1)} %gather_slots.5), calls=%async_computation | async-start | bytes 1572864 | tf_op jit(solution)/shard_map/all_to_all | solution.py:524
  21.5 3.3 gather_slots.4
  30.4 6.0 %all-to-all-done = bf16[16,64,384]{2,1,0:T(8,128)(2,1)S(1)} async-done(((bf16[16,64,384]{2,1,0:T(8,128)(2,1)}), bf16[16,64,384]{2,1,0:T(8,128)(2,1)S(1)}, u32[]{:S(2)}, u32[]{:S(2)}) %all-to-all-start) | async-done | bytes 786464 | tf_op jit(solution)/shard_map/all_to_all | solution.py:524
  36.5 5.0 %all-to-all-start.1 = ((bf16[16,64,384]{2,1,0:T(8,128)(2,1)}), bf16[16,64,384]{2,1,0:T(8,128)(2,1)S(1)}, u32[]{:S(2)}, u32[]{:S(2)}) async-start(bf16[16,64,384]{2,1,0:T(8,128)(2,1)} %gather_slots.4), calls=%async_computation.1 | async-start | bytes 1572864 | tf_op jit(solution)/shard_map/all_to_all | solution.py:524
  44.3 6.9 %enter.1 = (f32[512,768]{1,0:T(8,128)}, bf16[512,768]{1,0:T(8,128)(2,1)}, bf16[512,768]{1,0:T(8,128)(2,1)}, bf16[512,768]{1,0:T(8,128)(2,1)}) custom-call(s32[10]{0:T(128)} %concatenate.50.info, bf16[8,2,64,384]{3,2,1,0:T(8,128)(2,1)} %bitcast.13, f32[6,768]{1,0:T(8,128)} %fusion.1.thoughts, f32[2,768]{1,0:T(2,128)} %pad_maximum_fusion.2.norms, ...), custom_call_target="tpu_custom_call" | custom-call | tf_op jit(solution)/shard_map/enter/pallas_call | solution.py:574
  51.2 5.6 %collective-permute-done.5.direct.direct_q = bf16[1,384,384]{2,1,0:T(8,128)(2,1)S(1)} collective-permute-done((bf16[1,384,384]{2,1,0:T(8,128)(2,1)S(1)}, bf16[1,384,384]{2,1,0:T(8,128)(2,1)S(1)}, u32[]{:S(2)}, u32[]{:S(2)}) %collective-permute-start.5) | collective-permute-done | bytes 294944 | tf_op jit(solution)/shard_map/ppermute | solution.py:507
  58.0 2.8 collective-permute-done.7.partner.partner_q
  61.6 4.0 %queries.1.q_ref = bf16[512,768]{1,0:T(8,128)(2,1)} custom-call(s32[10]{0:T(128)} %concatenate.50.info, bf16[512,768]{1,0:T(8,128)(2,1)} %get-tuple-element.175.normed, f32[2,384]{1,0:T(2,128)} %bias_own.3, f32[2,384]{1,0:T(2,128)} %copy-done.39, bf16[3,768,384]{2,1,0:T(8,128)(2,1)} %own.7, bf16[1,384,384]{2,1,0:T(8,128)(2,1)} %copy-done.17, ...), custom_call_target="tpu_custom_call" | custom-call | tf_op jit(solution)/shard_map/queries/pallas_call | solution.py:583
  67.9 2.8 cotangent.1.grad.grad0
  71.9 15.3 %attend_forward.1 = (bf16[512,768]{1,0:T(8,128)(2,1)}, f32[6,2,512]{2,1,0:T(2,128)}) custom-call(s32[10]{0:T(128)} %concatenate.50.info, bf16[512,768]{1,0:T(8,128)(2,1)} %queries.1.q_ref, bf16[512,768]{1,0:T(8,128)(2,1)} %get-tuple-element.181.ko_ref, bf16[512,768]{1,0:T(8,128)(2,1)} %get-tuple-element.182.vo_ref, bf16[512,768]{1,0:T(8,128)(2,1)} %copy-done, ...), custom_call_target="tpu_custom_call" | custom-call | tf_op jit(solution)/shard_map/attend_forward/pallas_call | solution.py:139
  87.2 2.9 collective-permute-done.11.grad.grad1
  90.8 5.1 %middle.1 = (f32[512,768]{1,0:T(8,128)}, bf16[512,768]{1,0:T(8,128)(2,1)}) custom-call(s32[10]{0:T(128)} %concatenate.50.info, bf16[512,768]{1,0:T(8,128)(2,1)} %get-tuple-element.188.heads.out_ref, f32[512,768]{1,0:T(8,128)} %get-tuple-element.189.inputs, f32[3,768]{1,0:T(4,128)} %pad_maximum_fusion.1.norms, bf16[384,768]{1,0:T(8,128)(2,1)} %own.6, ...), custom_call_target="tpu_custom_call" | custom-call | tf_op jit(solution)/shard_map/middle/pallas_call | solution.py:598
  97.3 12.7 %mlp_rows.2 = (f32[512,768]{1,0:T(8,128)}, f32[512,768]{1,0:T(8,128)}, bf16[1536,512]{1,0:T(8,128)(2,1)}, bf16[512,1536]{1,0:T(8,128)(2,1)}, f32[2,1,1536]{2,1,0:T(1,128)}) custom-call(s32[10]{0:T(128)} %concatenate.50.info, bf16[512,768]{1,0:T(8,128)(2,1)} %get-tuple-element.192.normed.normed0, bf16[512,768]{1,0:T(8,128)(2,1)} %cotangent.1.grad.grad0, ...), custom_call_target="tpu_custom_call" | custom-call | tf_op jit(solution)/shard_map/mlp_rows/pallas_call | solution.py:613
  110.0 4.4 %collective-permute-done.13.normed.normed1 = bf16[512,768]{1,0:T(8,128)(2,1)S(1)} collective-permute-done((bf16[512,768]{1,0:T(8,128)(2,1)}, bf16[512,768]{1,0:T(8,128)(2,1)S(1)}, u32[]{:S(2)}, u32[]{:S(2)}) %collective-permute-start.13) | collective-permute-done | bytes 786464 | tf_op jit(solution)/shard_map/ppermute | solution.py:507
  115.3 12.2 %mlp_rows.3 = (bf16[512,768]{1,0:T(8,128)(2,1)}, bf16[512,768]{1,0:T(8,128)(2,1)}, bf16[1536,512]{1,0:T(8,128)(2,1)}, bf16[512,1536]{1,0:T(8,128)(2,1)}, f32[2,1,1536]{2,1,0:T(1,128)}) custom-call(s32[10]{0:T(128)} %concatenate.50.info, bf16[512,768]{1,0:T(8,128)(2,1)} %copy-done.9, bf16[512,768]{1,0:T(8,128)(2,1)} %copy-done.8, bf16[768,1536]{1,0:T(8,128)(2,1)} %fc.3, ...), custom_call_target="tpu_custom_call" | custom-call | tf_op jit(solution)/shard_map/mlp_rows/pallas_call | solution.py:613
  128.3 10.5 %mlp_grads.1 = (bf16[384,3072]{1,0:T(8,128)(2,1)}, bf16[384,3072]{1,0:T(8,128)(2,1)}) custom-call(s32[10]{0:T(128)} %concatenate.50.info, bf16[512,768]{1,0:T(8,128)(2,1)} %get-tuple-element.192.normed.normed0, bf16[512,768]{1,0:T(8,128)(2,1)} %copy-done.9, bf16[512,768]{1,0:T(8,128)(2,1)} %cotangent.1.grad.grad0, bf16[512,768]{1,0:T(8,128)(2,1)} %copy-done.8, ...), custom_call_target="tpu_custom_call" | custom-call | tf_op jit(solution)/shard_map/mlp_grads/pallas_call | solution.py:631
  138.7 6.5 %collective-permute-done.14.back_far = bf16[512,768]{1,0:T(8,128)(2,1)S(1)} collective-permute-done((bf16[512,768]{1,0:T(8,128)(2,1)}, bf16[512,768]{1,0:T(8,128)(2,1)S(1)}, u32[]{:S(2)}, u32[]{:S(2)}) %collective-permute-start.14) | collective-permute-done | bytes 786464 | tf_op jit(solution)/shard_map/ppermute | solution.py:507
  146.1 6.7 %back.1 = (f32[512,768]{1,0:T(8,128)}, bf16[512,768]{1,0:T(8,128)(2,1)}, bf16[512,768]{1,0:T(8,128)(2,1)}, f32[4,768]{1,0:T(4,128)}) custom-call(s32[10]{0:T(128)} %concatenate.50.info, f32[512,768]{1,0:T(8,128)} %get-tuple-element.193.back, bf16[512,768]{1,0:T(8,128)(2,1)} %copy-done.23, f32[512,768]{1,0:T(8,128)} %get-tuple-element.206.residual, ...), custom_call_target="tpu_custom_call" | custom-call | tf_op jit(solution)/shard_map/back/pallas_call | solution.py:662
  156.9 2.3 collective-permute-start.17
  159.1 11.9 %attend_backward.2 = (bf16[512,384]{1,0:T(8,128)(2,1)}, f32[512,384]{1,0:T(8,128)}, f32[512,384]{1,0:T(8,128)}, bf16[512,384]{1,0:T(8,128)(2,1)}, bf16[512,384]{1,0:T(8,128)(2,1)}) custom-call(s32[10]{0:T(128)} %concatenate.50.info, bf16[512,768]{1,0:T(8,128)(2,1)} %queries.1.q_ref, bf16[512,768]{1,0:T(8,128)(2,1)} %get-tuple-element.181.ko_ref, ...), custom_call_target="tpu_custom_call" | custom-call | tf_op jit(solution)/shard_map/attend_backward/pallas_call | solution.py:162
  176.0 3.8 %block.1 = bf16[8,2,64,384]{3,2,1,0:T(8,128)(2,1)} custom-call(s32[10]{0:T(128)} %concatenate.50.info, f32[512,768]{1,0:T(8,128)} %get-tuple-element.206.residual, f32[512,768]{1,0:T(8,128)} %get-tuple-element.228.mlp, bf16[512,768]{1,0:T(8,128)(2,1)} %collective-permute-done.15.mlp_far, f32[1,768]{1,0:T(1,128)} %get-tuple-element.333.bias), custom_call_target="tpu_custom_call" | custom-call | tf_op jit(solution)/shard_map/block/pallas_call | solution.py:695
  180.7 6.0 %attention_grads.2 = (bf16[384,1536]{1,0:T(8,128)(2,1)}, bf16[384,1536]{1,0:T(8,128)(2,1)}) custom-call(s32[10]{0:T(128)} %concatenate.50.info, bf16[512,768]{1,0:T(8,128)(2,1)} %get-tuple-element.175.normed, bf16[512,768]{1,0:T(8,128)(2,1)} %get-tuple-element.188.heads.out_ref, bf16[512,768]{1,0:T(8,128)(2,1)} %get-tuple-element.207.grad_attn, ...), custom_call_target="tpu_custom_call" | custom-call | tf_op jit(solution)/shard_map/attention_grads/pallas_call | solution.py:705
  187.4 5.5 %all-to-all-start.2 = ((bf16[16,64,384]{2,1,0:T(8,128)(2,1)}), bf16[16,64,384]{2,1,0:T(8,128)(2,1)S(1)}, u32[]{:S(2)}, u32[]{:S(2)}) async-start(bf16[16,64,384]{2,1,0:T(8,128)(2,1)} %bitcast.8), calls=%async_computation.2 | async-start | bytes 1572864 | tf_op jit(solution)/shard_map/all_to_all | solution.py:524
  192.9 2.4 add_convert_fusion.1
  195.3 2.6 add_convert_fusion.2
  202.8 11.9 %attend_backward.3 = (bf16[512,384]{1,0:T(8,128)(2,1)}, f32[512,384]{1,0:T(8,128)}, f32[512,384]{1,0:T(8,128)}, bf16[512,384]{1,0:T(8,128)(2,1)}, bf16[512,384]{1,0:T(8,128)(2,1)}) custom-call(s32[10]{0:T(128)} %concatenate.50.info, bf16[512,768]{1,0:T(8,128)(2,1)} %queries.1.q_ref, bf16[512,768]{1,0:T(8,128)(2,1)} %get-tuple-element.181.ko_ref, ...), custom_call_target="tpu_custom_call" | custom-call | tf_op jit(solution)/shard_map/attend_backward/pallas_call | solution.py:162
  214.7 4.5 %collective-permute-done.22 = bf16[192,1536]{1,0:T(8,128)(2,1)} collective-permute-done((bf16[192,1536]{1,0:T(8,128)(2,1)}, bf16[192,1536]{1,0:T(8,128)(2,1)}, u32[]{:S(2)}, u32[]{:S(2)}) %collective-permute-start.22) | collective-permute-done | bytes 589856 | tf_op jit(solution)/shard_map/ppermute | solution.py:507
  223.9 6.0 %attention_grads.3 = (bf16[384,1536]{1,0:T(8,128)(2,1)}, bf16[384,1536]{1,0:T(8,128)(2,1)}) custom-call(s32[10]{0:T(128)} %concatenate.50.info, bf16[512,768]{1,0:T(8,128)(2,1)} %get-tuple-element.175.normed, bf16[512,768]{1,0:T(8,128)(2,1)} %get-tuple-element.188.heads.out_ref, bf16[512,768]{1,0:T(8,128)(2,1)} %get-tuple-element.207.grad_attn, ...), custom_call_target="tpu_custom_call" | custom-call | tf_op jit(solution)/shard_map/attention_grads/pallas_call | solution.py:705
  229.9 2.5 collective-permute-start.28
  234.5 3.5 gather_slots.6
  238.0 8.5 %collective-permute-done.28 = bf16[48,3072]{1,0:T(8,128)(2,1)S(1)} collective-permute-done((bf16[48,3072]{1,0:T(8,128)(2,1)}, bf16[48,3072]{1,0:T(8,128)(2,1)S(1)}, u32[]{:S(2)}, u32[]{:S(2)}) %collective-permute-start.28) | collective-permute-done | bytes 294944 | tf_op jit(solution)/shard_map/ppermute | solution.py:510
  252.2 9.4 %leave.1 = (bf16[8,2,64,384]{3,2,1,0:T(8,128)(2,1)}, f32[4,768]{1,0:T(4,128)}) custom-call(s32[10]{0:T(128)} %concatenate.50.info, f32[512,768]{1,0:T(8,128)} %get-tuple-element.189.inputs, f32[512,768]{1,0:T(8,128)} %get-tuple-element.267.grad_residual, f32[1,768]{1,0:T(1,128)} %copy-done.37, bf16[512,384]{1,0:T(8,128)(2,1)} %get-tuple-element.271.dq.dq0, ...), custom_call_target="tpu_custom_call" | custom-call | tf_op jit(solution)/shard_map/leave/pallas_call | solution.py:745
  261.6 5.6 %collective-permute-done.30 = bf16[48,3072]{1,0:T(8,128)(2,1)S(1)} collective-permute-done((bf16[48,3072]{1,0:T(8,128)(2,1)S(1)}, bf16[48,3072]{1,0:T(8,128)(2,1)S(1)}, u32[]{:S(2)}, u32[]{:S(2)}) %collective-permute-start.30) | collective-permute-done | bytes 294944 | tf_op jit(solution)/shard_map/ppermute | solution.py:510
  271.0 2.1 collective-permute-start.36
  273.1 7.6 %collective-permute-done.32 = bf16[96,1536]{1,0:T(8,128)(2,1)S(1)} collective-permute-done((bf16[96,1536]{1,0:T(8,128)(2,1)S(1)}, bf16[96,1536]{1,0:T(8,128)(2,1)S(1)}, u32[]{:S(2)}, u32[]{:S(2)}) %collective-permute-start.32) | collective-permute-done | bytes 294944 | tf_op jit(solution)/shard_map/ppermute | solution.py:510
  283.5 9.6 %collective-permute-done.34 = bf16[48,1536]{1,0:T(8,128)(2,1)S(1)} collective-permute-done((bf16[48,1536]{1,0:T(8,128)(2,1)S(1)}, bf16[48,1536]{1,0:T(8,128)(2,1)S(1)}, u32[]{:S(2)}, u32[]{:S(2)}) %collective-permute-start.34) | collective-permute-done | bytes 147488 | tf_op jit(solution)/shard_map/ppermute | solution.py:510
  293.1 2.2 collective-permute-done.36
  295.6 5.2 %all-to-all-start.3 = ((bf16[16,64,384]{2,1,0:T(8,128)(2,1)}), bf16[16,64,384]{2,1,0:T(8,128)(2,1)S(1)}, u32[]{:S(2)}, u32[]{:S(2)}) async-start(bf16[16,64,384]{2,1,0:T(8,128)(2,1)} %bitcast.15), calls=%async_computation.3 | async-start | bytes 1572864 | tf_op jit(solution)/shard_map/all_to_all | solution.py:524
  304.1 2.4 collective-permute-start.37
  308.0 2.9 collective-permute-done.38
  310.9 16.8 %collective-permute-done.37 = bf16[48,1536]{1,0:T(8,128)(2,1)S(1)} collective-permute-done((bf16[48,1536]{1,0:T(8,128)(2,1)S(1)}, bf16[48,1536]{1,0:T(8,128)(2,1)S(1)}, u32[]{:S(2)}, u32[]{:S(2)}) %collective-permute-start.37) | collective-permute-done | bytes 147488 | tf_op jit(solution)/shard_map/ppermute | solution.py:510
  329.9 7.2 %collective-permute-done.41 = f32[12,768]{1,0:T(8,128)S(1)} collective-permute-done((f32[12,768]{1,0:T(8,128)S(1)}, f32[12,768]{1,0:T(8,128)S(1)}, u32[]{:S(2)}, u32[]{:S(2)}) %collective-permute-start.41) | collective-permute-done | bytes 36896 | tf_op jit(solution)/shard_map/ppermute | solution.py:510
  342.0 3.5 gather_slots.7
  346.4 6.2 %finish_mlp.1 = (f32[768,1536]{1,0:T(8,128)}, f32[1536,768]{1,0:T(8,128)}) custom-call(s32[10]{0:T(128)} %concatenate.50.info, bf16[192,3072]{1,0:T(8,128)(2,1)} %copy-done.2, bf16[192,3072]{1,0:T(8,128)(2,1)} %collective-permute-done.42.refs_1_, bf16[192,3072]{1,0:T(8,128)(2,1)} %copy-done.21, bf16[192,3072]{1,0:T(8,128)(2,1)} %collective-permute-done.44.refs_3_), custom_call_target="tpu_custom_call" | custom-call | tf_op jit(solution)/shard_map/finish_mlp/pallas_call | solution.py:798
  352.6 2.5 collective-permute-done.43.refs_1_
  358.5 4.7 %finish_attention.1 = (f32[3,768,384]{2,1,0:T(8,128)}, f32[384,768]{1,0:T(8,128)}) custom-call(s32[10]{0:T(128)} %concatenate.50.info, bf16[192,1536]{1,0:T(8,128)(2,1)} %copy-done.10, bf16[192,1536]{1,0:T(8,128)(2,1)} %copy-done.24, bf16[192,1536]{1,0:T(8,128)(2,1)} %collective-permute-done.46.refs_2_, bf16[192,1536]{1,0:T(8,128)(2,1)} %copy-done.26), custom_call_target="tpu_custom_call" | custom-call | tf_op jit(solution)/shard_map/finish_attention/pallas_call | solution.py:804
  (229 shorter events, 75.0 us)
Async XLA Ops:
  0.7 27.4 %collective-permute-start.4 = (s32[1,6]{1,0:T(1,128)}, s32[1,6]{1,0:T(1,128)S(1)}, u32[]{:S(2)}, u32[]{:S(2)}) collective-permute-start(s32[1,6]{1,0:T(1,128)} %param.18), channel_id=1, source_target_pairs={{0,2},{1,3},{2,0},{3,1},{4,6},{5,7},{6,4},{7,5},{8,10},{9,11},{10,... | collective-permute-start | bytes 80 | tf_op jit(solution)/shard_map/ppermute | solution.py:510
  1.2 29.2 %collective-permute-start.3 = (f32[2,384]{1,0:T(2,128)}, f32[2,384]{1,0:T(2,128)S(1)}, u32[]{:S(2)}, u32[]{:S(2)}) collective-permute-start(f32[2,384]{1,0:T(2,128)} %bias_own.3), channel_id=1, source_target_pairs={{0,1},{1,0},{2,3},{3,2},{4,5},{5,4},{6,7},{7,6},{8,9},{9,8},{10,11... | collective-permute-start | bytes 9224 | tf_op jit(solution)/shard_map/ppermute | solution.py:507
  5.0 25.4 %collective-permute-start = (bf16[2,384,384]{2,1,0:T(8,128)(2,1)S(1)}, bf16[2,384,384]{2,1,0:T(8,128)(2,1)S(1)}, u32[]{:S(2)}, u32[]{:S(2)}) collective-permute-start(bf16[2,384,384]{2,1,0:T(8,128)(2,1)S(1)} %constant_dynamic-slice_fusion.3), channel_id=1, source_target_pairs={{0,1},{1,0},{2,3},{3,2},{4,5},{5,4},{6,7},{7,6},{8,9},{9,8},{10,11... | collective-permute-start | bytes 1769480 | tf_op jit(solution)/shard_map/ppermute | solution.py:507
  9.3 27.2 %all-to-all-start = ((bf16[16,64,384]{2,1,0:T(8,128)(2,1)}), bf16[16,64,384]{2,1,0:T(8,128)(2,1)S(1)}, u32[]{:S(2)}, u32[]{:S(2)}) async-start(bf16[16,64,384]{2,1,0:T(8,128)(2,1)} %gather_slots.5), calls=%async_computation | async-start | bytes 1572864 | tf_op jit(solution)/shard_map/all_to_all | solution.py:524
  26.0 3.8 %collective-permute-start.2 = (bf16[6,384]{1,0:T(8,128)(2,1)S(1)}, bf16[6,384]{1,0:T(8,128)(2,1)S(1)}, u32[]{:S(2)}, u32[]{:S(2)}) collective-permute-start(bf16[6,384]{1,0:T(8,128)(2,1)S(1)} %get-tuple-element.332), channel_id=1, source_target_pairs={{0,1},{1,0},{2,3},{3,2},{4,5},{5,4},{6,7},{7,6},{8,9},{9,8},{10,11... | collective-permute-start | bytes 13832 | tf_op jit(solution)/shard_map/ppermute | solution.py:507
  36.5 30.5 %all-to-all-start.1 = ((bf16[16,64,384]{2,1,0:T(8,128)(2,1)}), bf16[16,64,384]{2,1,0:T(8,128)(2,1)S(1)}, u32[]{:S(2)}, u32[]{:S(2)}) async-start(bf16[16,64,384]{2,1,0:T(8,128)(2,1)} %gather_slots.4), calls=%async_computation.1 | async-start | bytes 1572864 | tf_op jit(solution)/shard_map/all_to_all | solution.py:524
  41.5 15.3 %collective-permute-start.5 = (bf16[1,384,384]{2,1,0:T(8,128)(2,1)S(1)}, bf16[1,384,384]{2,1,0:T(8,128)(2,1)S(1)}, u32[]{:S(2)}, u32[]{:S(2)}) collective-permute-start(bf16[1,384,384]{2,1,0:T(8,128)(2,1)S(1)} %constant_dynamic-slice_fusion), channel_id=1, source_target_pairs={{0,1},{1,0},{2,3},{3,2},{4,5},{5,4},{6,7},{7,6},{8,9},{9,8},{10,11... | collective-permute-start | bytes 884744 | tf_op jit(solution)/shard_map/ppermute | solution.py:507
  56.8 13.9 %collective-permute-start.9 = (bf16[512,768]{1,0:T(8,128)(2,1)}, bf16[512,768]{1,0:T(8,128)(2,1)S(1)}, u32[]{:S(2)}, u32[]{:S(2)}) collective-permute-start(bf16[512,768]{1,0:T(8,128)(2,1)} %get-tuple-element.181.ko_ref), channel_id=1, source_target_pairs={{0,2},{1,3},{2,0},{3,1},{4,6},{5,7},{6,4},{7,5},{8,10},{9,11},{10,... | collective-permute-start | bytes 2359304 | tf_op jit(solution)/shard_map/ppermute | solution.py:510
  56.8 13.9 %collective-permute-start.10 = (bf16[512,768]{1,0:T(8,128)(2,1)}, bf16[512,768]{1,0:T(8,128)(2,1)S(1)}, u32[]{:S(2)}, u32[]{:S(2)}) collective-permute-start(bf16[512,768]{1,0:T(8,128)(2,1)} %get-tuple-element.182.vo_ref), channel_id=1, source_target_pairs={{0,2},{1,3},{2,0},{3,1},{4,6},{5,7},{6,4},{7,5},{8,10},{9,11},{10,... | collective-permute-start | bytes 2359304 | tf_op jit(solution)/shard_map/ppermute | solution.py:510
  57.3 3.5 collective-permute-start.7
  57.3 9.6 %collective-permute-start.8 = (bf16[384,384]{1,0:T(8,128)(2,1)}, bf16[384,384]{1,0:T(8,128)(2,1)S(1)}, u32[]{:S(2)}, u32[]{:S(2)}) collective-permute-start(bf16[384,384]{1,0:T(8,128)(2,1)} %constant_dynamic-slice_fusion.2), channel_id=1, source_target_pairs={{0,1},{1,0},{2,3},{3,2},{4,5},{5,4},{6,7},{7,6},{8,9},{9,8},{10,11... | collective-permute-start | bytes 884744 | tf_op jit(solution)/shard_map/ppermute | solution.py:507
  70.7 19.4 %collective-permute-start.11 = (bf16[512,768]{1,0:T(8,128)(2,1)}, bf16[512,768]{1,0:T(8,128)(2,1)S(1)}, u32[]{:S(2)}, u32[]{:S(2)}) collective-permute-start(bf16[512,768]{1,0:T(8,128)(2,1)} %cotangent.1.grad.grad0), channel_id=1, source_target_pairs={{0,1},{1,0},{2,3},{3,2},{4,5},{5,4},{6,7},{7,6},{8,9},{9,8},{10,11... | collective-permute-start | bytes 2359304 | tf_op jit(solution)/shard_map/ppermute | solution.py:507
  71.5 18.6 %collective-permute-start.12 = (bf16[384,384]{1,0:T(8,128)(2,1)S(1)}, bf16[384,384]{1,0:T(8,128)(2,1)S(1)}, u32[]{:S(2)}, u32[]{:S(2)}) collective-permute-start(bf16[384,384]{1,0:T(8,128)(2,1)S(1)} %collective-permute-done.8.direct), channel_id=1, source_target_pairs={{0,2},{1,3},{2,0},{3,1},{4,6},{5,7},{6,4},{7,5},{8,10},{9,11},{10,... | collective-permute-start | bytes 884744 | tf_op jit(solution)/shard_map/ppermute | solution.py:510
  95.9 18.5 %collective-permute-start.13 = (bf16[512,768]{1,0:T(8,128)(2,1)}, bf16[512,768]{1,0:T(8,128)(2,1)S(1)}, u32[]{:S(2)}, u32[]{:S(2)}) collective-permute-start(bf16[512,768]{1,0:T(8,128)(2,1)} %get-tuple-element.192.normed.normed0), channel_id=1, source_target_pairs={{0,1},{1,0},{2,3},{3,2},{4,5},{5,4},{6,7},{7,6},{8,9},{9,8},{10,11... | collective-permute-start | bytes 2359304 | tf_op jit(solution)/shard_map/ppermute | solution.py:507
  127.5 17.7 %collective-permute-start.14 = (bf16[512,768]{1,0:T(8,128)(2,1)}, bf16[512,768]{1,0:T(8,128)(2,1)S(1)}, u32[]{:S(2)}, u32[]{:S(2)}) collective-permute-start(bf16[512,768]{1,0:T(8,128)(2,1)} %get-tuple-element.197), channel_id=1, source_target_pairs={{0,1},{1,0},{2,3},{3,2},{4,5},{5,4},{6,7},{7,6},{8,9},{9,8},{10,11... | collective-permute-start | bytes 2359304 | tf_op jit(solution)/shard_map/ppermute | solution.py:507
  145.2 7.6 %collective-permute-start.16 = (bf16[384,3072]{1,0:T(8,128)(2,1)}, bf16[384,3072]{1,0:T(8,128)(2,1)}, u32[]{:S(2)}, u32[]{:S(2)}) collective-permute-start(bf16[384,3072]{1,0:T(8,128)(2,1)} %get-tuple-element.210), channel_id=1, source_target_pairs={{0,2},{1,3},{2,0},{3,1},{4,6},{5,7},{6,4},{7,5},{8,10},{9,11},{10,... | collective-permute-start | bytes 7077896 | tf_op jit(solution)/shard_map/ppermute | solution.py:510
  145.2 25.8 %collective-permute-start.15 = (bf16[512,768]{1,0:T(8,128)(2,1)}, bf16[512,768]{1,0:T(8,128)(2,1)}, u32[]{:S(2)}, u32[]{:S(2)}) collective-permute-start(bf16[512,768]{1,0:T(8,128)(2,1)} %get-tuple-element.208), channel_id=1, source_target_pairs={{0,1},{1,0},{2,3},{3,2},{4,5},{5,4},{6,7},{7,6},{8,9},{9,8},{10,11... | collective-permute-start | bytes 2359304 | tf_op jit(solution)/shard_map/ppermute | solution.py:507
  156.9 16.1 %collective-permute-start.17 = (bf16[96,3072]{1,0:T(8,128)(2,1)}, bf16[96,3072]{1,0:T(8,128)(2,1)S(1)}, u32[]{:S(2)}, u32[]{:S(2)}) collective-permute-start(bf16[96,3072]{1,0:T(8,128)(2,1)} %add_convert_fusion.4), channel_id=1, source_target_pairs={{0,4},{1,5},{2,6},{3,7},{4,0},{5,1},{6,2},{7,3},{8,12},{9,13},{10,... | collective-permute-start | bytes 1769480 | tf_op jit(solution)/shard_map/ppermute | solution.py:510
  173.8 6.0 %collective-permute-start.18 = (bf16[512,384]{1,0:T(8,128)(2,1)}, bf16[512,384]{1,0:T(8,128)(2,1)S(1)}, u32[]{:S(2)}, u32[]{:S(2)}) collective-permute-start(bf16[512,384]{1,0:T(8,128)(2,1)} %get-tuple-element.226), channel_id=1, source_target_pairs={{0,2},{1,3},{2,0},{3,1},{4,6},{5,7},{6,4},{7,5},{8,10},{9,11},{10,... | collective-permute-start | bytes 1179656 | tf_op jit(solution)/shard_map/ppermute | solution.py:510
  173.8 6.0 %collective-permute-start.19 = (bf16[512,384]{1,0:T(8,128)(2,1)}, bf16[512,384]{1,0:T(8,128)(2,1)S(1)}, u32[]{:S(2)}, u32[]{:S(2)}) collective-permute-start(bf16[512,384]{1,0:T(8,128)(2,1)} %get-tuple-element.227), channel_id=1, source_target_pairs={{0,2},{1,3},{2,0},{3,1},{4,6},{5,7},{6,4},{7,5},{8,10},{9,11},{10,... | collective-permute-start | bytes 1179656 | tf_op jit(solution)/shard_map/ppermute | solution.py:510
  174.3 12.4 %collective-permute-start.20 = (bf16[48,3072]{1,0:T(8,128)(2,1)}, bf16[48,3072]{1,0:T(8,128)(2,1)S(1)}, u32[]{:S(2)}, u32[]{:S(2)}) collective-permute-start(bf16[48,3072]{1,0:T(8,128)(2,1)} %get-tuple-element.236), channel_id=1, source_target_pairs={{0,4},{1,5},{2,6},{3,7},{4,0},{5,1},{6,2},{7,3},{8,12},{9,13},{10,... | collective-permute-start | bytes 884744 | tf_op jit(solution)/shard_map/ppermute | solution.py:510
  186.7 8.6 %collective-permute-start.21 = (bf16[384,1536]{1,0:T(8,128)(2,1)}, bf16[384,1536]{1,0:T(8,128)(2,1)}, u32[]{:S(2)}, u32[]{:S(2)}) collective-permute-start(bf16[384,1536]{1,0:T(8,128)(2,1)} %get-tuple-element.239), channel_id=1, source_target_pairs={{0,2},{1,3},{2,0},{3,1},{4,6},{5,7},{6,4},{7,5},{8,10},{9,11},{10,... | collective-permute-start | bytes 3538952 | tf_op jit(solution)/shard_map/ppermute | solution.py:510
  187.4 27.2 %all-to-all-start.2 = ((bf16[16,64,384]{2,1,0:T(8,128)(2,1)}), bf16[16,64,384]{2,1,0:T(8,128)(2,1)S(1)}, u32[]{:S(2)}, u32[]{:S(2)}) async-start(bf16[16,64,384]{2,1,0:T(8,128)(2,1)} %bitcast.8), calls=%async_computation.2 | async-start | bytes 1572864 | tf_op jit(solution)/shard_map/all_to_all | solution.py:524
  197.9 21.2 %collective-permute-start.22 = (bf16[192,1536]{1,0:T(8,128)(2,1)}, bf16[192,1536]{1,0:T(8,128)(2,1)}, u32[]{:S(2)}, u32[]{:S(2)}) collective-permute-start(bf16[192,1536]{1,0:T(8,128)(2,1)} %get-tuple-element.241), channel_id=1, source_target_pairs={{0,1},{1,0},{2,3},{3,2},{4,5},{5,4},{6,7},{7,6},{8,9},{9,8},{10,11... | collective-permute-start | bytes 1769480 | tf_op jit(solution)/shard_map/ppermute | solution.py:507
  199.8 20.8 %collective-permute-start.23 = (bf16[96,3072]{1,0:T(8,128)(2,1)}, bf16[96,3072]{1,0:T(8,128)(2,1)}, u32[]{:S(2)}, u32[]{:S(2)}) collective-permute-start(bf16[96,3072]{1,0:T(8,128)(2,1)} %add_convert_fusion.1), channel_id=1, source_target_pairs={{0,8},{1,9},{2,10},{3,11},{4,12},{5,13},{6,14},{7,15},{8,0},{9,1},... | collective-permute-start | bytes 1769480 | tf_op jit(solution)/shard_map/ppermute | solution.py:510
  201.3 13.3 %collective-permute-start.24 = (bf16[48,3072]{1,0:T(8,128)(2,1)S(1)}, bf16[48,3072]{1,0:T(8,128)(2,1)}, u32[]{:S(2)}, u32[]{:S(2)}) collective-permute-start(bf16[48,3072]{1,0:T(8,128)(2,1)S(1)} %copy-done.31), channel_id=1, source_target_pairs={{0,4},{1,5},{2,6},{3,7},{4,0},{5,1},{6,2},{7,3},{8,12},{9,13},{10,... | collective-permute-start | bytes 884744 | tf_op jit(solution)/shard_map/ppermute | solution.py:510
  220.6 2.6 collective-permute-start.26
  229.9 16.6 %collective-permute-start.27 = (bf16[384,1536]{1,0:T(8,128)(2,1)}, bf16[384,1536]{1,0:T(8,128)(2,1)}, u32[]{:S(2)}, u32[]{:S(2)}) collective-permute-start(bf16[384,1536]{1,0:T(8,128)(2,1)} %get-tuple-element.261), channel_id=1, source_target_pairs={{0,2},{1,3},{2,0},{3,1},{4,6},{5,7},{6,4},{7,5},{8,10},{9,11},{10,... | collective-permute-start | bytes 3538952 | tf_op jit(solution)/shard_map/ppermute | solution.py:510
  229.9 16.6 %collective-permute-start.28 = (bf16[48,3072]{1,0:T(8,128)(2,1)}, bf16[48,3072]{1,0:T(8,128)(2,1)S(1)}, u32[]{:S(2)}, u32[]{:S(2)}) collective-permute-start(bf16[48,3072]{1,0:T(8,128)(2,1)} %add_convert_fusion.7), channel_id=1, source_target_pairs={{0,16},{1,17},{2,18},{3,19},{4,20},{5,21},{6,22},{7,23},{8,24},{9,... | collective-permute-start | bytes 884744 | tf_op jit(solution)/shard_map/ppermute | solution.py:510
  233.1 28.5 %collective-permute-start.31 = (bf16[192,1536]{1,0:T(8,128)(2,1)}, bf16[192,1536]{1,0:T(8,128)(2,1)}, u32[]{:S(2)}, u32[]{:S(2)}) collective-permute-start(bf16[192,1536]{1,0:T(8,128)(2,1)} %get-tuple-element.280), channel_id=1, source_target_pairs={{0,1},{1,0},{2,3},{3,2},{4,5},{5,4},{6,7},{7,6},{8,9},{9,8},{10,11... | collective-permute-start | bytes 1769480 | tf_op jit(solution)/shard_map/ppermute | solution.py:507
  250.3 16.9 %collective-permute-start.29 = (bf16[192,1536]{1,0:T(8,128)(2,1)S(1)}, bf16[192,1536]{1,0:T(8,128)(2,1)S(1)}, u32[]{:S(2)}, u32[]{:S(2)}) collective-permute-start(bf16[192,1536]{1,0:T(8,128)(2,1)S(1)} %add_convert_fusion), channel_id=1, source_target_pairs={{0,4},{1,5},{2,6},{3,7},{4,0},{5,1},{6,2},{7,3},{8,12},{9,13},{10,... | collective-permute-start | bytes 1769480 | tf_op jit(solution)/shard_map/ppermute | solution.py:510
  252.0 15.2 %collective-permute-start.30 = (bf16[48,3072]{1,0:T(8,128)(2,1)S(1)}, bf16[48,3072]{1,0:T(8,128)(2,1)S(1)}, u32[]{:S(2)}, u32[]{:S(2)}) collective-permute-start(bf16[48,3072]{1,0:T(8,128)(2,1)S(1)} %add_convert_fusion.6), channel_id=1, source_target_pairs={{0,16},{1,17},{2,18},{3,19},{4,20},{5,21},{6,22},{7,23},{8,24},{9,... | collective-permute-start | bytes 884744 | tf_op jit(solution)/shard_map/ppermute | solution.py:510
  268.8 4.3 %collective-permute-start.33 = (f32[12,768]{1,0:T(8,128)S(1)}, f32[12,768]{1,0:T(8,128)S(1)}, u32[]{:S(2)}, u32[]{:S(2)}) collective-permute-start(f32[12,768]{1,0:T(8,128)S(1)} %pad_maximum_fusion), channel_id=1, source_target_pairs={{0,4},{1,5},{2,6},{3,7},{4,0},{5,1},{6,2},{7,3},{8,12},{9,13},{10,... | collective-permute-start | bytes 110600 | tf_op jit(solution)/shard_map/ppermute | solution.py:510
  270.8 9.9 %collective-permute-start.32 = (bf16[96,1536]{1,0:T(8,128)(2,1)S(1)}, bf16[96,1536]{1,0:T(8,128)(2,1)S(1)}, u32[]{:S(2)}, u32[]{:S(2)}) collective-permute-start(bf16[96,1536]{1,0:T(8,128)(2,1)S(1)} %add_convert_fusion.5), channel_id=1, source_target_pairs={{0,8},{1,9},{2,10},{3,11},{4,12},{5,13},{6,14},{7,15},{8,0},{9,1},... | collective-permute-start | bytes 884744 | tf_op jit(solution)/shard_map/ppermute | solution.py:510
  271.0 24.3 %collective-permute-start.36 = (bf16[96,3072]{1,0:T(8,128)(2,1)S(1)}, bf16[96,3072]{1,0:T(8,128)(2,1)S(1)}, u32[]{:S(2)}, u32[]{:S(2)}) collective-permute-start(bf16[96,3072]{1,0:T(8,128)(2,1)S(1)} %maximum_select_fusion.1), channel_id=1, source_target_pairs={{0,8},{1,9},{2,10},{3,11},{4,12},{5,13},{6,14},{7,15},{8,0},{9,1},... | collective-permute-start | bytes 1769480 | tf_op jit(solution)/shard_map/ppermute | solution.py:510
  282.0 11.1 %collective-permute-start.34 = (bf16[48,1536]{1,0:T(8,128)(2,1)S(1)}, bf16[48,1536]{1,0:T(8,128)(2,1)S(1)}, u32[]{:S(2)}, u32[]{:S(2)}) collective-permute-start(bf16[48,1536]{1,0:T(8,128)(2,1)S(1)} %add_convert_fusion.11), channel_id=1, source_target_pairs={{0,16},{1,17},{2,18},{3,19},{4,20},{5,21},{6,22},{7,23},{8,24},{9,... | collective-permute-start | bytes 442376 | tf_op jit(solution)/shard_map/ppermute | solution.py:510
  295.6 32.2 %collective-permute-start.39 = (bf16[192,3072]{1,0:T(8,128)(2,1)S(1)}, bf16[192,3072]{1,0:T(8,128)(2,1)S(1)}, u32[]{:S(2)}, u32[]{:S(2)}) collective-permute-start(bf16[192,3072]{1,0:T(8,128)(2,1)S(1)} %maximum_select_fusion.refs_0_), channel_id=1, source_target_pairs={{0,2},{1,3},{2,0},{3,1},{4,6},{5,7},{6,4},{7,5},{8,10},{9,11},{10,... | collective-permute-start | bytes 3538952 | tf_op jit(solution)/shard_map/ppermute | solution.py:510
  295.6 42.1 %all-to-all-start.3 = ((bf16[16,64,384]{2,1,0:T(8,128)(2,1)}), bf16[16,64,384]{2,1,0:T(8,128)(2,1)S(1)}, u32[]{:S(2)}, u32[]{:S(2)}) async-start(bf16[16,64,384]{2,1,0:T(8,128)(2,1)} %bitcast.15), calls=%async_computation.3 | async-start | bytes 1572864 | tf_op jit(solution)/shard_map/all_to_all | solution.py:524
  300.9 36.9 %collective-permute-start.42 = (bf16[192,3072]{1,0:T(8,128)(2,1)S(1)}, bf16[192,3072]{1,0:T(8,128)(2,1)}, u32[]{:S(2)}, u32[]{:S(2)}) collective-permute-start(bf16[192,3072]{1,0:T(8,128)(2,1)S(1)} %maximum_select_fusion.refs_0_), channel_id=1, source_target_pairs={{0,4},{1,5},{2,6},{3,7},{4,0},{5,1},{6,2},{7,3},{8,12},{9,13},{10,... | collective-permute-start | bytes 3538952 | tf_op jit(solution)/shard_map/ppermute | solution.py:510
  304.1 23.6 %collective-permute-start.37 = (bf16[48,1536]{1,0:T(8,128)(2,1)S(1)}, bf16[48,1536]{1,0:T(8,128)(2,1)S(1)}, u32[]{:S(2)}, u32[]{:S(2)}) collective-permute-start(bf16[48,1536]{1,0:T(8,128)(2,1)S(1)} %add_convert_fusion.10), channel_id=1, source_target_pairs={{0,16},{1,17},{2,18},{3,19},{4,20},{5,21},{6,22},{7,23},{8,24},{9,... | collective-permute-start | bytes 442376 | tf_op jit(solution)/shard_map/ppermute | solution.py:510
  306.5 4.4 %collective-permute-start.38 = (f32[12,768]{1,0:T(8,128)S(1)}, f32[12,768]{1,0:T(8,128)S(1)}, u32[]{:S(2)}, u32[]{:S(2)}) collective-permute-start(f32[12,768]{1,0:T(8,128)S(1)} %add.302), channel_id=1, source_target_pairs={{0,1},{1,0},{2,3},{3,2},{4,5},{5,4},{6,7},{7,6},{8,9},{9,8},{10,11... | collective-permute-start | bytes 110600 | tf_op jit(solution)/shard_map/ppermute | solution.py:507
  327.8 9.3 %collective-permute-start.40 = (bf16[96,1536]{1,0:T(8,128)(2,1)S(1)}, bf16[96,1536]{1,0:T(8,128)(2,1)S(1)}, u32[]{:S(2)}, u32[]{:S(2)}) collective-permute-start(bf16[96,1536]{1,0:T(8,128)(2,1)S(1)} %maximum_select_fusion.3), channel_id=1, source_target_pairs={{0,8},{1,9},{2,10},{3,11},{4,12},{5,13},{6,14},{7,15},{8,0},{9,1},... | collective-permute-start | bytes 884744 | tf_op jit(solution)/shard_map/ppermute | solution.py:510
  327.9 9.2 %collective-permute-start.41 = (f32[12,768]{1,0:T(8,128)S(1)}, f32[12,768]{1,0:T(8,128)S(1)}, u32[]{:S(2)}, u32[]{:S(2)}) collective-permute-start(f32[12,768]{1,0:T(8,128)S(1)} %add.304), channel_id=1, source_target_pairs={{0,8},{1,9},{2,10},{3,11},{4,12},{5,13},{6,14},{7,15},{8,0},{9,1},... | collective-permute-start | bytes 110600 | tf_op jit(solution)/shard_map/ppermute | solution.py:510
  339.3 7.1 %collective-permute-start.44 = (bf16[192,3072]{1,0:T(8,128)(2,1)}, bf16[192,3072]{1,0:T(8,128)(2,1)}, u32[]{:S(2)}, u32[]{:S(2)}) collective-permute-start(bf16[192,3072]{1,0:T(8,128)(2,1)} %collective-permute-done.42.refs_1_), channel_id=1, source_target_pairs={{0,2},{1,3},{2,0},{3,1},{4,6},{5,7},{6,4},{7,5},{8,10},{9,11},{10,... | collective-permute-start | bytes 3538952 | tf_op jit(solution)/shard_map/ppermute | solution.py:510
  339.3 15.7 %collective-permute-start.43 = (bf16[192,1536]{1,0:T(8,128)(2,1)S(1)}, bf16[192,1536]{1,0:T(8,128)(2,1)S(1)}, u32[]{:S(2)}, u32[]{:S(2)}) collective-permute-start(bf16[192,1536]{1,0:T(8,128)(2,1)S(1)} %maximum_select_fusion.2.refs_0_), channel_id=1, source_target_pairs={{0,4},{1,5},{2,6},{3,7},{4,0},{5,1},{6,2},{7,3},{8,12},{9,13},{10,... | collective-permute-start | bytes 1769480 | tf_op jit(solution)/shard_map/ppermute | solution.py:510
  340.9 5.5 %collective-permute-start.45 = (f32[12,768]{1,0:T(8,128)S(1)}, f32[12,768]{1,0:T(8,128)S(1)}, u32[]{:S(2)}, u32[]{:S(2)}) collective-permute-start(f32[12,768]{1,0:T(8,128)S(1)} %add.305), channel_id=1, source_target_pairs={{0,16},{1,17},{2,18},{3,19},{4,20},{5,21},{6,22},{7,23},{8,24},{9,... | collective-permute-start | bytes 110600 | tf_op jit(solution)/shard_map/ppermute | solution.py:510
  342.0 15.7 %collective-permute-start.46 = (bf16[192,1536]{1,0:T(8,128)(2,1)S(1)}, bf16[192,1536]{1,0:T(8,128)(2,1)}, u32[]{:S(2)}, u32[]{:S(2)}) collective-permute-start(bf16[192,1536]{1,0:T(8,128)(2,1)S(1)} %maximum_select_fusion.2.refs_0_), channel_id=1, source_target_pairs={{0,2},{1,3},{2,0},{3,1},{4,6},{5,7},{6,4},{7,5},{8,10},{9,11},{10,... | collective-permute-start | bytes 1769480 | tf_op jit(solution)/shard_map/ppermute | solution.py:510
  355.1 2.6 collective-permute-start.47
  (55 other events, 313.1 us)

commit v2 on v1

--- a/solution.py
+++ b/solution.py
@@ -729,8 +729,9 @@
         own, (mlp_stage,) = with_far(own, mlp_section(1))
         mlp_stage = flip(mlp_stage, upper[1])
         keep_own, send_own = attention_grads(0, own)
+        keep_own, send_own, mlp_stage, x_last = lax.optimization_barrier((keep_own, send_own, mlp_stage, x_last))
         block_out = gather_slots(restore, block_back, F32)
-        got_own, mlp_stage, block_out = lax.optimization_barrier((flip(send_own), mlp_stage, block_out))
+        got_own, block_out = lax.optimization_barrier((flip(send_own), block_out))
         mlp_rows_kept.append((mlp_stage, -starts[2]))
         for level in range(2, levels):
             mlp_rows_kept.append((flip(mlp_section(level), upper[level]), -starts[level + 1]))
@@ -749,9 +750,10 @@
             [like((slots // 2, 2, block, half_width), BF16), like((4, width), F32)],
             [pltpu.VMEM((tile, width), F32)],
         )(info, inputs, grad_residual, norm_gain[:1], *own, *other, qkv_weight, kv_direct, kv_partner, q_direct, q_partner)
-        input_pieces, small_attn, over_bit, mlp_stage, x_last = lax.optimization_barrier(
-            (input_pieces, small_attn, over_bit, mlp_stage, x_last)
+        input_pieces, small_attn, over_bit, mlp_stage = lax.optimization_barrier(
+            (input_pieces, small_attn, over_bit, mlp_stage)
         )
+        input_back = exchange(input_pieces.reshape(slots, block, half_width))
 
         def ordered(vectors):
             return join(side, vectors[:, :half_width], vectors[:, half_width:], axis=1)
@@ -765,19 +767,19 @@
         def add_over(value):
             return value + links.pop(0)(value) if links else value
 
+        mlp_piece = widen(1, mlp_piece, mlp_stage)
+        mlp_stage = flip(mlp_piece, upper[0])
+        small = add_over(small)
+        mlp_stage, small, over_bit = lax.optimization_barrier((mlp_stage, small, over_bit))
+        mlp_piece = widen(0, mlp_piece, mlp_stage)
+        mlp_over, mlp_core = flip(mlp_piece, 1), flip(mlp_piece)
         kept = [(keep_own, near * half), (got_own, near * half), (x_last, 0), (over_bit, 0)]
         for level in range(levels):
             stage = flip(rows_sum(kept, *section(level)), upper[level])
-            if level == 0:
-                mlp_piece = widen(1, mlp_piece, mlp_stage)
-                mlp_stage = flip(mlp_piece, upper[0])
             small = add_over(small)
             stage, small = lax.optimization_barrier((stage, small))
-            if level == 1:
-                stage, mlp_stage, input_pieces = lax.optimization_barrier((stage, mlp_stage, input_pieces))
-                mlp_piece = widen(0, mlp_piece, mlp_stage)
-                mlp_over, mlp_core = flip(mlp_piece, 1), flip(mlp_piece)
-                input_back = exchange(input_pieces.reshape(slots, block, half_width))
+            if level == 0:
+                stage, mlp_core = lax.optimization_barrier((stage, mlp_core))
             kept.append((stage, -starts[level + 1]))
         piece = rows_sum(kept, *section(levels))
         for level in reversed(range(levels)):
@@ -785,9 +787,9 @@
             small = add_over(small)
             stage, small = lax.optimization_barrier((stage, small))
             if level == levels - 1:
-                stage, mlp_core = lax.optimization_barrier((stage, mlp_core))
+                stage, input_back = lax.optimization_barrier((stage, input_back))
             if level == 0:
-                stage, mlp_over, input_back = lax.optimization_barrier((stage, mlp_over, input_back))
+                stage, mlp_over = lax.optimization_barrier((stage, mlp_over))
             piece = widen(level, piece, stage)
         while links:
             small = add_over(small)

time: 365 us -> 371 us (1.016)
  other arithmetic: 24.4 us -> 28.2 us
    ppermute x12, waiting for transfers between devices: 28.6 us -> 32.9 us  [cross(): return lax.ppermute(value, AXES, tensor_pairs)]
    ppermute x36, waiting for transfers between devices: 68.6 us -> 64.6 us  [flip(): return lax.ppermute(value, AXES, bit_pairs[bit])]
    unnamed x102 -> x104, local copies, waits for them, and re-layouts: 10 us -> 9.15 us
  transfers between devices with their start and end apart: 52 -> 52, of which waited for: 24 -> 26; matrix products, arithmetic and copies ran while one was open for 8% -> 10% of each run, Pallas kernels for 33% -> 35%
where the time goes in v2:
time: 371 us; the launch traced here: 369 us
  Pallas kernels  150 us (40%)
  waiting for transfers between devices  103 us (28%)
  starting transfers between devices  64.5 us (17%)
  other arithmetic  28.2 us (8%)
  local copies, waits for them, and re-layouts  20.2 us (5%)
    ppermute x36, waiting for transfers between devices, flip(): return lax.ppermute(value, AXES, bit_pairs[bit])  64.6 us
    ppermute x12, waiting for transfers between devices, cross(): return lax.ppermute(value, AXES, tensor_pairs)  32.9 us
    ppermute x36, starting transfers between devices, flip(): return lax.ppermute(value, AXES, bit_pairs[bit])  27.4 us
    pallas_call x2, Pallas kernels, mlp_rows(): call(mlp_rows_kernel, 'mlp_rows', (steps, 3), [by_row, by_row, spec((widt...  25 us
    pallas_call x2, Pallas kernels, attend_backward(): pl.pallas_call(functools.partial(attend_backward_kernel, tile, block), gr...  23.7 us
    all_to_all x4, starting transfers between devices, exchange(): lax.all_to_all(array, AXES, split_axis=0, concat_axis=0, tiled=True, axis...  21.9 us
    convert_element_type x10, other arithmetic, rows_sum(): return total.astype(BF16)  18.6 us
    pallas_call x1, Pallas kernels, attend_forward(): pl.pallas_call(functools.partial(attend_forward_kernel, tile, block), gri...  15.3 us
  transfers between devices with their start and end apart: 52, of which 26 were waited for; matrix products, arithmetic and copies ran while one was open for 10% of the time, Pallas kernels for 35%

profile of v2, /device:TPU:0, one launch (start us, length us, event | category | flops | bytes accessed | tf_op | source)
XLA Modules:
  0.0 368.8 jit_solution(6641483306452329967)
XLA Ops:
  1.2 2.6 collective-permute-start.3
  6.0 3.3 gather_slots.5
  9.3 7.3 %all-to-all-start = ((bf16[16,64,384]{2,1,0:T(8,128)(2,1)}), bf16[16,64,384]{2,1,0:T(8,128)(2,1)S(1)}, u32[]{:S(2)}, u32[]{:S(2)}) async-start(bf16[16,64,384]{2,1,0:T(8,128)(2,1)} %gather_slots.5), calls=%async_computation | async-start | bytes 1572864 | tf_op jit(solution)/shard_map/all_to_all | solution.py:524
  22.2 3.3 gather_slots.4
  31.1 5.4 %all-to-all-done = bf16[16,64,384]{2,1,0:T(8,128)(2,1)S(1)} async-done(((bf16[16,64,384]{2,1,0:T(8,128)(2,1)}), bf16[16,64,384]{2,1,0:T(8,128)(2,1)S(1)}, u32[]{:S(2)}, u32[]{:S(2)}) %all-to-all-start) | async-done | bytes 786464 | tf_op jit(solution)/shard_map/all_to_all | solution.py:524
  36.5 5.0 %all-to-all-start.1 = ((bf16[16,64,384]{2,1,0:T(8,128)(2,1)}), bf16[16,64,384]{2,1,0:T(8,128)(2,1)S(1)}, u32[]{:S(2)}, u32[]{:S(2)}) async-start(bf16[16,64,384]{2,1,0:T(8,128)(2,1)} %gather_slots.4), calls=%async_computation.1 | async-start | bytes 1572864 | tf_op jit(solution)/shard_map/all_to_all | solution.py:524
  44.3 6.9 %enter.1 = (f32[512,768]{1,0:T(8,128)}, bf16[512,768]{1,0:T(8,128)(2,1)}, bf16[512,768]{1,0:T(8,128)(2,1)}, bf16[512,768]{1,0:T(8,128)(2,1)}) custom-call(s32[10]{0:T(128)} %concatenate.50.info, bf16[8,2,64,384]{3,2,1,0:T(8,128)(2,1)} %bitcast.13, f32[6,768]{1,0:T(8,128)} %fusion.1.thoughts, f32[2,768]{1,0:T(2,128)} %pad_maximum_fusion.2.norms, ...), custom_call_target="tpu_custom_call" | custom-call | tf_op jit(solution)/shard_map/enter/pallas_call | solution.py:574
  51.2 5.8 %collective-permute-done.5.direct.direct_q = bf16[1,384,384]{2,1,0:T(8,128)(2,1)S(1)} collective-permute-done((bf16[1,384,384]{2,1,0:T(8,128)(2,1)}, bf16[1,384,384]{2,1,0:T(8,128)(2,1)S(1)}, u32[]{:S(2)}, u32[]{:S(2)}) %collective-permute-start.5) | collective-permute-done | bytes 294944 | tf_op jit(solution)/shard_map/ppermute | solution.py:507
  58.3 2.8 collective-permute-done.7.partner.partner_q
  61.8 4.1 %queries.1.q_ref = bf16[512,768]{1,0:T(8,128)(2,1)} custom-call(s32[10]{0:T(128)} %concatenate.50.info, bf16[512,768]{1,0:T(8,128)(2,1)} %get-tuple-element.178.normed, f32[2,384]{1,0:T(2,128)} %bias_own.3, f32[2,384]{1,0:T(2,128)} %copy-done.40, bf16[3,768,384]{2,1,0:T(8,128)(2,1)} %own.7, bf16[1,384,384]{2,1,0:T(8,128)(2,1)} %copy-done.17, ...), custom_call_target="tpu_custom_call" | custom-call | tf_op jit(solution)/shard_map/queries/pallas_call | solution.py:583
  68.1 2.8 cotangent.1.grad.grad0
  72.1 15.3 %attend_forward.1 = (bf16[512,768]{1,0:T(8,128)(2,1)}, f32[6,2,512]{2,1,0:T(2,128)}) custom-call(s32[10]{0:T(128)} %concatenate.50.info, bf16[512,768]{1,0:T(8,128)(2,1)} %queries.1.q_ref, bf16[512,768]{1,0:T(8,128)(2,1)} %get-tuple-element.184.ko_ref, bf16[512,768]{1,0:T(8,128)(2,1)} %get-tuple-element.185.vo_ref, bf16[512,768]{1,0:T(8,128)(2,1)} %copy-done, ...), custom_call_target="tpu_custom_call" | custom-call | tf_op jit(solution)/shard_map/attend_forward/pallas_call | solution.py:139
  87.4 2.9 collective-permute-done.11.grad.grad1
  91.1 5.1 %middle.1 = (f32[512,768]{1,0:T(8,128)}, bf16[512,768]{1,0:T(8,128)(2,1)}) custom-call(s32[10]{0:T(128)} %concatenate.50.info, bf16[512,768]{1,0:T(8,128)(2,1)} %get-tuple-element.191.heads.out_ref, f32[512,768]{1,0:T(8,128)} %get-tuple-element.192.inputs, f32[3,768]{1,0:T(4,128)} %pad_maximum_fusion.1.norms, bf16[384,768]{1,0:T(8,128)(2,1)} %own.6, ...), custom_call_target="tpu_custom_call" | custom-call | tf_op jit(solution)/shard_map/middle/pallas_call | solution.py:598
  97.5 12.8 %mlp_rows.2 = (f32[512,768]{1,0:T(8,128)}, f32[512,768]{1,0:T(8,128)}, bf16[1536,512]{1,0:T(8,128)(2,1)}, bf16[512,1536]{1,0:T(8,128)(2,1)}, f32[2,1,1536]{2,1,0:T(1,128)}) custom-call(s32[10]{0:T(128)} %concatenate.50.info, bf16[512,768]{1,0:T(8,128)(2,1)} %get-tuple-element.195.normed.normed0, bf16[512,768]{1,0:T(8,128)(2,1)} %cotangent.1.grad.grad0, ...), custom_call_target="tpu_custom_call" | custom-call | tf_op jit(solution)/shard_map/mlp_rows/pallas_call | solution.py:613
  110.3 4.4 %collective-permute-done.13.normed.normed1 = bf16[512,768]{1,0:T(8,128)(2,1)S(1)} collective-permute-done((bf16[512,768]{1,0:T(8,128)(2,1)}, bf16[512,768]{1,0:T(8,128)(2,1)S(1)}, u32[]{:S(2)}, u32[]{:S(2)}) %collective-permute-start.13) | collective-permute-done | bytes 786464 | tf_op jit(solution)/shard_map/ppermute | solution.py:507
  115.6 12.3 %mlp_rows.3 = (bf16[512,768]{1,0:T(8,128)(2,1)}, bf16[512,768]{1,0:T(8,128)(2,1)}, bf16[1536,512]{1,0:T(8,128)(2,1)}, bf16[512,1536]{1,0:T(8,128)(2,1)}, f32[2,1,1536]{2,1,0:T(1,128)}) custom-call(s32[10]{0:T(128)} %concatenate.50.info, bf16[512,768]{1,0:T(8,128)(2,1)} %copy-done.9, bf16[512,768]{1,0:T(8,128)(2,1)} %copy-done.8, bf16[768,1536]{1,0:T(8,128)(2,1)} %fc.3, ...), custom_call_target="tpu_custom_call" | custom-call | tf_op jit(solution)/shard_map/mlp_rows/pallas_call | solution.py:613
  128.6 10.5 %mlp_grads.1 = (bf16[384,3072]{1,0:T(8,128)(2,1)}, bf16[384,3072]{1,0:T(8,128)(2,1)}) custom-call(s32[10]{0:T(128)} %concatenate.50.info, bf16[512,768]{1,0:T(8,128)(2,1)} %get-tuple-element.195.normed.normed0, bf16[512,768]{1,0:T(8,128)(2,1)} %copy-done.9, bf16[512,768]{1,0:T(8,128)(2,1)} %cotangent.1.grad.grad0, bf16[512,768]{1,0:T(8,128)(2,1)} %copy-done.8, ...), custom_call_target="tpu_custom_call" | custom-call | tf_op jit(solution)/shard_map/mlp_grads/pallas_call | solution.py:631
  139.1 6.4 %collective-permute-done.14.back_far = bf16[512,768]{1,0:T(8,128)(2,1)S(1)} collective-permute-done((bf16[512,768]{1,0:T(8,128)(2,1)}, bf16[512,768]{1,0:T(8,128)(2,1)S(1)}, u32[]{:S(2)}, u32[]{:S(2)}) %collective-permute-start.14) | collective-permute-done | bytes 786464 | tf_op jit(solution)/shard_map/ppermute | solution.py:507
  146.4 6.7 %back.1 = (f32[512,768]{1,0:T(8,128)}, bf16[512,768]{1,0:T(8,128)(2,1)}, bf16[512,768]{1,0:T(8,128)(2,1)}, f32[4,768]{1,0:T(4,128)}) custom-call(s32[10]{0:T(128)} %concatenate.50.info, f32[512,768]{1,0:T(8,128)} %get-tuple-element.196.back, bf16[512,768]{1,0:T(8,128)(2,1)} %copy-done.26, f32[512,768]{1,0:T(8,128)} %get-tuple-element.209.residual, ...), custom_call_target="tpu_custom_call" | custom-call | tf_op jit(solution)/shard_map/back/pallas_call | solution.py:662
  158.7 11.9 %attend_backward.2 = (bf16[512,384]{1,0:T(8,128)(2,1)}, f32[512,384]{1,0:T(8,128)}, f32[512,384]{1,0:T(8,128)}, bf16[512,384]{1,0:T(8,128)(2,1)}, bf16[512,384]{1,0:T(8,128)(2,1)}) custom-call(s32[10]{0:T(128)} %concatenate.50.info, bf16[512,768]{1,0:T(8,128)(2,1)} %queries.1.q_ref, bf16[512,768]{1,0:T(8,128)(2,1)} %get-tuple-element.184.ko_ref, ...), custom_call_target="tpu_custom_call" | custom-call | tf_op jit(solution)/shard_map/attend_backward/pallas_call | solution.py:162
  175.2 3.8 %block.1 = bf16[8,2,64,384]{3,2,1,0:T(8,128)(2,1)} custom-call(s32[10]{0:T(128)} %concatenate.50.info, f32[512,768]{1,0:T(8,128)} %get-tuple-element.209.residual, f32[512,768]{1,0:T(8,128)} %get-tuple-element.231.mlp, bf16[512,768]{1,0:T(8,128)(2,1)} %collective-permute-done.15.mlp_far, f32[1,768]{1,0:T(1,128)} %get-tuple-element.339.bias), custom_call_target="tpu_custom_call" | custom-call | tf_op jit(solution)/shard_map/block/pallas_call | solution.py:695
  179.9 6.0 %attention_grads.2 = (bf16[384,1536]{1,0:T(8,128)(2,1)}, bf16[384,1536]{1,0:T(8,128)(2,1)}) custom-call(s32[10]{0:T(128)} %concatenate.50.info, bf16[512,768]{1,0:T(8,128)(2,1)} %get-tuple-element.178.normed, bf16[512,768]{1,0:T(8,128)(2,1)} %get-tuple-element.191.heads.out_ref, bf16[512,768]{1,0:T(8,128)(2,1)} %get-tuple-element.210.grad_attn, ...), custom_call_target="tpu_custom_call" | custom-call | tf_op jit(solution)/shard_map/attention_grads/pallas_call | solution.py:705
  186.0 5.6 %all-to-all-start.2 = ((bf16[16,64,384]{2,1,0:T(8,128)(2,1)}), bf16[16,64,384]{2,1,0:T(8,128)(2,1)S(1)}, u32[]{:S(2)}, u32[]{:S(2)}) async-start(bf16[16,64,384]{2,1,0:T(8,128)(2,1)} %bitcast.8), calls=%async_computation.2 | async-start | bytes 1572864 | tf_op jit(solution)/shard_map/all_to_all | solution.py:524
  194.0 2.6 add_convert_fusion.2
  201.4 11.9 %attend_backward.3 = (bf16[512,384]{1,0:T(8,128)(2,1)}, f32[512,384]{1,0:T(8,128)}, f32[512,384]{1,0:T(8,128)}, bf16[512,384]{1,0:T(8,128)(2,1)}, bf16[512,384]{1,0:T(8,128)(2,1)}) custom-call(s32[10]{0:T(128)} %concatenate.50.info, bf16[512,768]{1,0:T(8,128)(2,1)} %queries.1.q_ref, bf16[512,768]{1,0:T(8,128)(2,1)} %get-tuple-element.184.ko_ref, ...), custom_call_target="tpu_custom_call" | custom-call | tf_op jit(solution)/shard_map/attend_backward/pallas_call | solution.py:162
  213.4 5.3 %collective-permute-done.22 = bf16[192,1536]{1,0:T(8,128)(2,1)} collective-permute-done((bf16[192,1536]{1,0:T(8,128)(2,1)}, bf16[192,1536]{1,0:T(8,128)(2,1)}, u32[]{:S(2)}, u32[]{:S(2)}) %collective-permute-start.22) | collective-permute-done | bytes 589856 | tf_op jit(solution)/shard_map/ppermute | solution.py:507
  223.9 2.6 collective-permute-start.27
  226.5 6.0 %attention_grads.3 = (bf16[384,1536]{1,0:T(8,128)(2,1)}, bf16[384,1536]{1,0:T(8,128)(2,1)}) custom-call(s32[10]{0:T(128)} %concatenate.50.info, bf16[512,768]{1,0:T(8,128)(2,1)} %get-tuple-element.178.normed, bf16[512,768]{1,0:T(8,128)(2,1)} %get-tuple-element.191.heads.out_ref, bf16[512,768]{1,0:T(8,128)(2,1)} %get-tuple-element.210.grad_attn, ...), custom_call_target="tpu_custom_call" | custom-call | tf_op jit(solution)/shard_map/attention_grads/pallas_call | solution.py:705
  232.5 3.5 collective-permute-done.28
  236.0 4.2 %collective-permute-done.27 = bf16[48,3072]{1,0:T(8,128)(2,1)} collective-permute-done((bf16[48,3072]{1,0:T(8,128)(2,1)}, bf16[48,3072]{1,0:T(8,128)(2,1)}, u32[]{:S(2)}, u32[]{:S(2)}) %collective-permute-start.27) | collective-permute-done | bytes 294944 | tf_op jit(solution)/shard_map/ppermute | solution.py:510
  240.8 3.5 gather_slots.6
  249.9 9.4 %leave.1 = (bf16[8,2,64,384]{3,2,1,0:T(8,128)(2,1)}, f32[4,768]{1,0:T(4,128)}) custom-call(s32[10]{0:T(128)} %concatenate.50.info, f32[512,768]{1,0:T(8,128)} %get-tuple-element.192.inputs, f32[512,768]{1,0:T(8,128)} %get-tuple-element.278.grad_residual, f32[1,768]{1,0:T(1,128)} %copy-done.37, bf16[512,384]{1,0:T(8,128)(2,1)} %get-tuple-element.279.dq.dq0, ...), custom_call_target="tpu_custom_call" | custom-call | tf_op jit(solution)/shard_map/leave/pallas_call | solution.py:746
  259.3 6.8 %collective-permute-done.31 = bf16[48,3072]{1,0:T(8,128)(2,1)S(1)} collective-permute-done((bf16[48,3072]{1,0:T(8,128)(2,1)}, bf16[48,3072]{1,0:T(8,128)(2,1)S(1)}, u32[]{:S(2)}, u32[]{:S(2)}) %collective-permute-start.31) | collective-permute-done | bytes 294944 | tf_op jit(solution)/shard_map/ppermute | solution.py:510
  268.8 3.5 collective-permute-done.33
  273.0 10.4 %collective-permute-done.32 = bf16[96,3072]{1,0:T(8,128)(2,1)S(1)} collective-permute-done((bf16[96,3072]{1,0:T(8,128)(2,1)S(1)}, bf16[96,3072]{1,0:T(8,128)(2,1)S(1)}, u32[]{:S(2)}, u32[]{:S(2)}) %collective-permute-start.32) | collective-permute-done | bytes 589856 | tf_op jit(solution)/shard_map/ppermute | solution.py:510
  283.7 4.0 %all-to-all-start.3 = ((bf16[16,64,384]{2,1,0:T(8,128)(2,1)}), bf16[16,64,384]{2,1,0:T(8,128)(2,1)S(1)}, u32[]{:S(2)}, u32[]{:S(2)}) async-start(bf16[16,64,384]{2,1,0:T(8,128)(2,1)} %bitcast.15), calls=%async_computation.3 | async-start | bytes 1572864 | tf_op jit(solution)/shard_map/all_to_all | solution.py:524
  292.9 16.7 %collective-permute-done.34 = bf16[96,1536]{1,0:T(8,128)(2,1)} collective-permute-done((bf16[96,1536]{1,0:T(8,128)(2,1)S(1)}, bf16[96,1536]{1,0:T(8,128)(2,1)}, u32[]{:S(2)}, u32[]{:S(2)}) %collective-permute-start.34) | collective-permute-done | bytes 294944 | tf_op jit(solution)/shard_map/ppermute | solution.py:510
  311.4 2.6 collective-permute-start.37
  316.9 2.9 collective-permute-done.38
  322.4 2.8 collective-permute-start.40
  327.7 3.2 collective-permute-done.39
  332.4 2.6 collective-permute-start.42
  335.1 5.0 %collective-permute-done.42 = f32[12,768]{1,0:T(8,128)S(1)} collective-permute-done((f32[12,768]{1,0:T(8,128)S(1)}, f32[12,768]{1,0:T(8,128)S(1)}, u32[]{:S(2)}, u32[]{:S(2)}) %collective-permute-start.42) | collective-permute-done | bytes 36896 | tf_op jit(solution)/shard_map/ppermute | solution.py:510
  343.7 3.5 gather_slots.7
  348.4 6.2 %finish_mlp.1 = (f32[768,1536]{1,0:T(8,128)}, f32[1536,768]{1,0:T(8,128)}) custom-call(s32[10]{0:T(128)} %concatenate.50.info, bf16[192,3072]{1,0:T(8,128)(2,1)} %copy-done.2, bf16[192,3072]{1,0:T(8,128)(2,1)} %collective-permute-done.43.refs_1_, bf16[192,3072]{1,0:T(8,128)(2,1)} %copy-done.21, bf16[192,3072]{1,0:T(8,128)(2,1)} %copy-done.22), custom_call_target="tpu_custom_call" | custom-call | tf_op jit(solution)/shard_map/finish_mlp/pallas_call | solution.py:800
  354.6 3.6 collective-permute-done.44.refs_1_
  364.0 4.7 %finish_attention.1 = (f32[3,768,384]{2,1,0:T(8,128)}, f32[384,768]{1,0:T(8,128)}) custom-call(s32[10]{0:T(128)} %concatenate.50.info, bf16[192,1536]{1,0:T(8,128)(2,1)} %copy-done.10, bf16[192,1536]{1,0:T(8,128)(2,1)} %copy-done.27, bf16[192,1536]{1,0:T(8,128)(2,1)} %copy-done.29, bf16[192,1536]{1,0:T(8,128)(2,1)} %copy-done.30), custom_call_target="tpu_custom_call" | custom-call | tf_op jit(solution)/shard_map/finish_attention/pallas_call | solution.py:806
  (232 shorter events, 85.6 us)
Async XLA Ops:
  0.7 28.1 %collective-permute-start.4 = (s32[1,6]{1,0:T(1,128)}, s32[1,6]{1,0:T(1,128)S(1)}, u32[]{:S(2)}, u32[]{:S(2)}) collective-permute-start(s32[1,6]{1,0:T(1,128)} %param.18), channel_id=1, source_target_pairs={{0,2},{1,3},{2,0},{3,1},{4,6},{5,7},{6,4},{7,5},{8,10},{9,11},{10,... | collective-permute-start | bytes 80 | tf_op jit(solution)/shard_map/ppermute | solution.py:510
  1.2 29.9 %collective-permute-start.3 = (f32[2,384]{1,0:T(2,128)}, f32[2,384]{1,0:T(2,128)S(1)}, u32[]{:S(2)}, u32[]{:S(2)}) collective-permute-start(f32[2,384]{1,0:T(2,128)} %bias_own.3), channel_id=1, source_target_pairs={{0,1},{1,0},{2,3},{3,2},{4,5},{5,4},{6,7},{7,6},{8,9},{9,8},{10,11... | collective-permute-start | bytes 9224 | tf_op jit(solution)/shard_map/ppermute | solution.py:507
  5.0 26.1 %collective-permute-start = (bf16[2,384,384]{2,1,0:T(8,128)(2,1)S(1)}, bf16[2,384,384]{2,1,0:T(8,128)(2,1)S(1)}, u32[]{:S(2)}, u32[]{:S(2)}) collective-permute-start(bf16[2,384,384]{2,1,0:T(8,128)(2,1)S(1)} %constant_dynamic-slice_fusion.3), channel_id=1, source_target_pairs={{0,1},{1,0},{2,3},{3,2},{4,5},{5,4},{6,7},{7,6},{8,9},{9,8},{10,11... | collective-permute-start | bytes 1769480 | tf_op jit(solution)/shard_map/ppermute | solution.py:507
  9.3 27.2 %all-to-all-start = ((bf16[16,64,384]{2,1,0:T(8,128)(2,1)}), bf16[16,64,384]{2,1,0:T(8,128)(2,1)S(1)}, u32[]{:S(2)}, u32[]{:S(2)}) async-start(bf16[16,64,384]{2,1,0:T(8,128)(2,1)} %gather_slots.5), calls=%async_computation | async-start | bytes 1572864 | tf_op jit(solution)/shard_map/all_to_all | solution.py:524
  26.7 3.7 %collective-permute-start.2 = (bf16[6,384]{1,0:T(8,128)(2,1)S(1)}, bf16[6,384]{1,0:T(8,128)(2,1)S(1)}, u32[]{:S(2)}, u32[]{:S(2)}) collective-permute-start(bf16[6,384]{1,0:T(8,128)(2,1)S(1)} %get-tuple-element.338), channel_id=1, source_target_pairs={{0,1},{1,0},{2,3},{3,2},{4,5},{5,4},{6,7},{7,6},{8,9},{9,8},{10,11... | collective-permute-start | bytes 13832 | tf_op jit(solution)/shard_map/ppermute | solution.py:507
  36.5 30.7 %all-to-all-start.1 = ((bf16[16,64,384]{2,1,0:T(8,128)(2,1)}), bf16[16,64,384]{2,1,0:T(8,128)(2,1)S(1)}, u32[]{:S(2)}, u32[]{:S(2)}) async-start(bf16[16,64,384]{2,1,0:T(8,128)(2,1)} %gather_slots.4), calls=%async_computation.1 | async-start | bytes 1572864 | tf_op jit(solution)/shard_map/all_to_all | solution.py:524
  41.5 15.5 %collective-permute-start.5 = (bf16[1,384,384]{2,1,0:T(8,128)(2,1)}, bf16[1,384,384]{2,1,0:T(8,128)(2,1)S(1)}, u32[]{:S(2)}, u32[]{:S(2)}) collective-permute-start(bf16[1,384,384]{2,1,0:T(8,128)(2,1)} %constant_dynamic-slice_fusion), channel_id=1, source_target_pairs={{0,1},{1,0},{2,3},{3,2},{4,5},{5,4},{6,7},{7,6},{8,9},{9,8},{10,11... | collective-permute-start | bytes 884744 | tf_op jit(solution)/shard_map/ppermute | solution.py:507
  57.0 13.9 %collective-permute-start.9 = (bf16[512,768]{1,0:T(8,128)(2,1)}, bf16[512,768]{1,0:T(8,128)(2,1)S(1)}, u32[]{:S(2)}, u32[]{:S(2)}) collective-permute-start(bf16[512,768]{1,0:T(8,128)(2,1)} %get-tuple-element.184.ko_ref), channel_id=1, source_target_pairs={{0,2},{1,3},{2,0},{3,1},{4,6},{5,7},{6,4},{7,5},{8,10},{9,11},{10,... | collective-permute-start | bytes 2359304 | tf_op jit(solution)/shard_map/ppermute | solution.py:510
  57.0 13.9 %collective-permute-start.10 = (bf16[512,768]{1,0:T(8,128)(2,1)}, bf16[512,768]{1,0:T(8,128)(2,1)S(1)}, u32[]{:S(2)}, u32[]{:S(2)}) collective-permute-start(bf16[512,768]{1,0:T(8,128)(2,1)} %get-tuple-element.185.vo_ref), channel_id=1, source_target_pairs={{0,2},{1,3},{2,0},{3,1},{4,6},{5,7},{6,4},{7,5},{8,10},{9,11},{10,... | collective-permute-start | bytes 2359304 | tf_op jit(solution)/shard_map/ppermute | solution.py:510
  57.5 9.6 %collective-permute-start.8 = (bf16[384,384]{1,0:T(8,128)(2,1)}, bf16[384,384]{1,0:T(8,128)(2,1)S(1)}, u32[]{:S(2)}, u32[]{:S(2)}) collective-permute-start(bf16[384,384]{1,0:T(8,128)(2,1)} %constant_dynamic-slice_fusion.2), channel_id=1, source_target_pairs={{0,1},{1,0},{2,3},{3,2},{4,5},{5,4},{6,7},{7,6},{8,9},{9,8},{10,11... | collective-permute-start | bytes 884744 | tf_op jit(solution)/shard_map/ppermute | solution.py:507
  70.9 19.4 %collective-permute-start.11 = (bf16[512,768]{1,0:T(8,128)(2,1)}, bf16[512,768]{1,0:T(8,128)(2,1)S(1)}, u32[]{:S(2)}, u32[]{:S(2)}) collective-permute-start(bf16[512,768]{1,0:T(8,128)(2,1)} %cotangent.1.grad.grad0), channel_id=1, source_target_pairs={{0,1},{1,0},{2,3},{3,2},{4,5},{5,4},{6,7},{7,6},{8,9},{9,8},{10,11... | collective-permute-start | bytes 2359304 | tf_op jit(solution)/shard_map/ppermute | solution.py:507
  71.7 18.6 %collective-permute-start.12 = (bf16[384,384]{1,0:T(8,128)(2,1)S(1)}, bf16[384,384]{1,0:T(8,128)(2,1)S(1)}, u32[]{:S(2)}, u32[]{:S(2)}) collective-permute-start(bf16[384,384]{1,0:T(8,128)(2,1)S(1)} %collective-permute-done.8.direct), channel_id=1, source_target_pairs={{0,2},{1,3},{2,0},{3,1},{4,6},{5,7},{6,4},{7,5},{8,10},{9,11},{10,... | collective-permute-start | bytes 884744 | tf_op jit(solution)/shard_map/ppermute | solution.py:510
  96.1 18.5 %collective-permute-start.13 = (bf16[512,768]{1,0:T(8,128)(2,1)}, bf16[512,768]{1,0:T(8,128)(2,1)S(1)}, u32[]{:S(2)}, u32[]{:S(2)}) collective-permute-start(bf16[512,768]{1,0:T(8,128)(2,1)} %get-tuple-element.195.normed.normed0), channel_id=1, source_target_pairs={{0,1},{1,0},{2,3},{3,2},{4,5},{5,4},{6,7},{7,6},{8,9},{9,8},{10,11... | collective-permute-start | bytes 2359304 | tf_op jit(solution)/shard_map/ppermute | solution.py:507
  127.8 17.7 %collective-permute-start.14 = (bf16[512,768]{1,0:T(8,128)(2,1)}, bf16[512,768]{1,0:T(8,128)(2,1)S(1)}, u32[]{:S(2)}, u32[]{:S(2)}) collective-permute-start(bf16[512,768]{1,0:T(8,128)(2,1)} %get-tuple-element.200), channel_id=1, source_target_pairs={{0,1},{1,0},{2,3},{3,2},{4,5},{5,4},{6,7},{7,6},{8,9},{9,8},{10,11... | collective-permute-start | bytes 2359304 | tf_op jit(solution)/shard_map/ppermute | solution.py:507
  145.5 7.6 %collective-permute-start.16 = (bf16[384,3072]{1,0:T(8,128)(2,1)}, bf16[384,3072]{1,0:T(8,128)(2,1)}, u32[]{:S(2)}, u32[]{:S(2)}) collective-permute-start(bf16[384,3072]{1,0:T(8,128)(2,1)} %get-tuple-element.213), channel_id=1, source_target_pairs={{0,2},{1,3},{2,0},{3,1},{4,6},{5,7},{6,4},{7,5},{8,10},{9,11},{10,... | collective-permute-start | bytes 7077896 | tf_op jit(solution)/shard_map/ppermute | solution.py:510
  145.5 25.1 %collective-permute-start.15 = (bf16[512,768]{1,0:T(8,128)(2,1)}, bf16[512,768]{1,0:T(8,128)(2,1)}, u32[]{:S(2)}, u32[]{:S(2)}) collective-permute-start(bf16[512,768]{1,0:T(8,128)(2,1)} %get-tuple-element.211), channel_id=1, source_target_pairs={{0,1},{1,0},{2,3},{3,2},{4,5},{5,4},{6,7},{7,6},{8,9},{9,8},{10,11... | collective-permute-start | bytes 2359304 | tf_op jit(solution)/shard_map/ppermute | solution.py:507
  156.4 15.7 %collective-permute-start.17 = (bf16[96,3072]{1,0:T(8,128)(2,1)S(1)}, bf16[96,3072]{1,0:T(8,128)(2,1)S(1)}, u32[]{:S(2)}, u32[]{:S(2)}) collective-permute-start(bf16[96,3072]{1,0:T(8,128)(2,1)S(1)} %add_convert_fusion.4), channel_id=1, source_target_pairs={{0,4},{1,5},{2,6},{3,7},{4,0},{5,1},{6,2},{7,3},{8,12},{9,13},{10,... | collective-permute-start | bytes 1769480 | tf_op jit(solution)/shard_map/ppermute | solution.py:510
  172.9 6.0 %collective-permute-start.18 = (bf16[512,384]{1,0:T(8,128)(2,1)}, bf16[512,384]{1,0:T(8,128)(2,1)S(1)}, u32[]{:S(2)}, u32[]{:S(2)}) collective-permute-start(bf16[512,384]{1,0:T(8,128)(2,1)} %get-tuple-element.229), channel_id=1, source_target_pairs={{0,2},{1,3},{2,0},{3,1},{4,6},{5,7},{6,4},{7,5},{8,10},{9,11},{10,... | collective-permute-start | bytes 1179656 | tf_op jit(solution)/shard_map/ppermute | solution.py:510
  173.0 6.0 %collective-permute-start.19 = (bf16[512,384]{1,0:T(8,128)(2,1)}, bf16[512,384]{1,0:T(8,128)(2,1)S(1)}, u32[]{:S(2)}, u32[]{:S(2)}) collective-permute-start(bf16[512,384]{1,0:T(8,128)(2,1)} %get-tuple-element.230), channel_id=1, source_target_pairs={{0,2},{1,3},{2,0},{3,1},{4,6},{5,7},{6,4},{7,5},{8,10},{9,11},{10,... | collective-permute-start | bytes 1179656 | tf_op jit(solution)/shard_map/ppermute | solution.py:510
  173.5 12.4 %collective-permute-start.20 = (bf16[48,3072]{1,0:T(8,128)(2,1)}, bf16[48,3072]{1,0:T(8,128)(2,1)S(1)}, u32[]{:S(2)}, u32[]{:S(2)}) collective-permute-start(bf16[48,3072]{1,0:T(8,128)(2,1)} %get-tuple-element.239), channel_id=1, source_target_pairs={{0,4},{1,5},{2,6},{3,7},{4,0},{5,1},{6,2},{7,3},{8,12},{9,13},{10,... | collective-permute-start | bytes 884744 | tf_op jit(solution)/shard_map/ppermute | solution.py:510
  185.9 8.1 %collective-permute-start.21 = (bf16[384,1536]{1,0:T(8,128)(2,1)}, bf16[384,1536]{1,0:T(8,128)(2,1)}, u32[]{:S(2)}, u32[]{:S(2)}) collective-permute-start(bf16[384,1536]{1,0:T(8,128)(2,1)} %get-tuple-element.242), channel_id=1, source_target_pairs={{0,2},{1,3},{2,0},{3,1},{4,6},{5,7},{6,4},{7,5},{8,10},{9,11},{10,... | collective-permute-start | bytes 3538952 | tf_op jit(solution)/shard_map/ppermute | solution.py:510
  186.0 27.3 %all-to-all-start.2 = ((bf16[16,64,384]{2,1,0:T(8,128)(2,1)}), bf16[16,64,384]{2,1,0:T(8,128)(2,1)S(1)}, u32[]{:S(2)}, u32[]{:S(2)}) async-start(bf16[16,64,384]{2,1,0:T(8,128)(2,1)} %bitcast.8), calls=%async_computation.2 | async-start | bytes 1572864 | tf_op jit(solution)/shard_map/all_to_all | solution.py:524
  196.6 22.0 %collective-permute-start.22 = (bf16[192,1536]{1,0:T(8,128)(2,1)}, bf16[192,1536]{1,0:T(8,128)(2,1)}, u32[]{:S(2)}, u32[]{:S(2)}) collective-permute-start(bf16[192,1536]{1,0:T(8,128)(2,1)} %get-tuple-element.244), channel_id=1, source_target_pairs={{0,1},{1,0},{2,3},{3,2},{4,5},{5,4},{6,7},{7,6},{8,9},{9,8},{10,11... | collective-permute-start | bytes 1769480 | tf_op jit(solution)/shard_map/ppermute | solution.py:507
  198.5 21.4 %collective-permute-start.23 = (bf16[96,3072]{1,0:T(8,128)(2,1)}, bf16[96,3072]{1,0:T(8,128)(2,1)}, u32[]{:S(2)}, u32[]{:S(2)}) collective-permute-start(bf16[96,3072]{1,0:T(8,128)(2,1)} %add_convert_fusion.1), channel_id=1, source_target_pairs={{0,8},{1,9},{2,10},{3,11},{4,12},{5,13},{6,14},{7,15},{8,0},{9,1},... | collective-permute-start | bytes 1769480 | tf_op jit(solution)/shard_map/ppermute | solution.py:510
  200.0 13.3 %collective-permute-start.24 = (bf16[48,3072]{1,0:T(8,128)(2,1)}, bf16[48,3072]{1,0:T(8,128)(2,1)S(1)}, u32[]{:S(2)}, u32[]{:S(2)}) collective-permute-start(bf16[48,3072]{1,0:T(8,128)(2,1)} %get-tuple-element.248), channel_id=1, source_target_pairs={{0,4},{1,5},{2,6},{3,7},{4,0},{5,1},{6,2},{7,3},{8,12},{9,13},{10,... | collective-permute-start | bytes 884744 | tf_op jit(solution)/shard_map/ppermute | solution.py:510
  219.9 4.0 %collective-permute-start.25 = (bf16[512,384]{1,0:T(8,128)(2,1)}, bf16[512,384]{1,0:T(8,128)(2,1)S(1)}, u32[]{:S(2)}, u32[]{:S(2)}) collective-permute-start(bf16[512,384]{1,0:T(8,128)(2,1)} %get-tuple-element.257), channel_id=1, source_target_pairs={{0,2},{1,3},{2,0},{3,1},{4,6},{5,7},{6,4},{7,5},{8,10},{9,11},{10,... | collective-permute-start | bytes 1179656 | tf_op jit(solution)/shard_map/ppermute | solution.py:510
  219.9 4.0 %collective-permute-start.26 = (bf16[512,384]{1,0:T(8,128)(2,1)}, bf16[512,384]{1,0:T(8,128)(2,1)}, u32[]{:S(2)}, u32[]{:S(2)}) collective-permute-start(bf16[512,384]{1,0:T(8,128)(2,1)} %get-tuple-element.258), channel_id=1, source_target_pairs={{0,2},{1,3},{2,0},{3,1},{4,6},{5,7},{6,4},{7,5},{8,10},{9,11},{10,... | collective-permute-start | bytes 1179656 | tf_op jit(solution)/shard_map/ppermute | solution.py:510
  220.4 15.6 %collective-permute-start.28 = (bf16[192,1536]{1,0:T(8,128)(2,1)}, bf16[192,1536]{1,0:T(8,128)(2,1)}, u32[]{:S(2)}, u32[]{:S(2)}) collective-permute-start(bf16[192,1536]{1,0:T(8,128)(2,1)} %get-tuple-element.267), channel_id=1, source_target_pairs={{0,1},{1,0},{2,3},{3,2},{4,5},{5,4},{6,7},{7,6},{8,9},{9,8},{10,11... | collective-permute-start | bytes 1769480 | tf_op jit(solution)/shard_map/ppermute | solution.py:507
  223.9 16.2 %collective-permute-start.27 = (bf16[48,3072]{1,0:T(8,128)(2,1)}, bf16[48,3072]{1,0:T(8,128)(2,1)}, u32[]{:S(2)}, u32[]{:S(2)}) collective-permute-start(bf16[48,3072]{1,0:T(8,128)(2,1)} %add_convert_fusion.7), channel_id=1, source_target_pairs={{0,16},{1,17},{2,18},{3,19},{4,20},{5,21},{6,22},{7,23},{8,24},{9,... | collective-permute-start | bytes 884744 | tf_op jit(solution)/shard_map/ppermute | solution.py:510
  240.1 6.4 %collective-permute-start.29 = (bf16[384,1536]{1,0:T(8,128)(2,1)}, bf16[384,1536]{1,0:T(8,128)(2,1)S(1)}, u32[]{:S(2)}, u32[]{:S(2)}) collective-permute-start(bf16[384,1536]{1,0:T(8,128)(2,1)} %get-tuple-element.268), channel_id=1, source_target_pairs={{0,2},{1,3},{2,0},{3,1},{4,6},{5,7},{6,4},{7,5},{8,10},{9,11},{10,... | collective-permute-start | bytes 3538952 | tf_op jit(solution)/shard_map/ppermute | solution.py:510
  248.3 17.8 %collective-permute-start.30 = (bf16[192,1536]{1,0:T(8,128)(2,1)S(1)}, bf16[192,1536]{1,0:T(8,128)(2,1)S(1)}, u32[]{:S(2)}, u32[]{:S(2)}) collective-permute-start(bf16[192,1536]{1,0:T(8,128)(2,1)S(1)} %add_convert_fusion), channel_id=1, source_target_pairs={{0,4},{1,5},{2,6},{3,7},{4,0},{5,1},{6,2},{7,3},{8,12},{9,13},{10,... | collective-permute-start | bytes 1769480 | tf_op jit(solution)/shard_map/ppermute | solution.py:510
  249.8 16.3 %collective-permute-start.31 = (bf16[48,3072]{1,0:T(8,128)(2,1)}, bf16[48,3072]{1,0:T(8,128)(2,1)S(1)}, u32[]{:S(2)}, u32[]{:S(2)}) collective-permute-start(bf16[48,3072]{1,0:T(8,128)(2,1)} %add_convert_fusion.6), channel_id=1, source_target_pairs={{0,16},{1,17},{2,18},{3,19},{4,20},{5,21},{6,22},{7,23},{8,24},{9,... | collective-permute-start | bytes 884744 | tf_op jit(solution)/shard_map/ppermute | solution.py:510
  268.0 15.3 %collective-permute-start.32 = (bf16[96,3072]{1,0:T(8,128)(2,1)S(1)}, bf16[96,3072]{1,0:T(8,128)(2,1)S(1)}, u32[]{:S(2)}, u32[]{:S(2)}) collective-permute-start(bf16[96,3072]{1,0:T(8,128)(2,1)S(1)} %maximum_select_fusion.1), channel_id=1, source_target_pairs={{0,8},{1,9},{2,10},{3,11},{4,12},{5,13},{6,14},{7,15},{8,0},{9,1},... | collective-permute-start | bytes 1769480 | tf_op jit(solution)/shard_map/ppermute | solution.py:510
  268.2 4.2 %collective-permute-start.33 = (f32[12,768]{1,0:T(8,128)S(1)}, f32[12,768]{1,0:T(8,128)S(1)}, u32[]{:S(2)}, u32[]{:S(2)}) collective-permute-start(f32[12,768]{1,0:T(8,128)S(1)} %pad_maximum_fusion), channel_id=1, source_target_pairs={{0,4},{1,5},{2,6},{3,7},{4,0},{5,1},{6,2},{7,3},{8,12},{9,13},{10,... | collective-permute-start | bytes 110600 | tf_op jit(solution)/shard_map/ppermute | solution.py:510
  283.6 26.0 %collective-permute-start.36 = (bf16[192,3072]{1,0:T(8,128)(2,1)S(1)}, bf16[192,3072]{1,0:T(8,128)(2,1)S(1)}, u32[]{:S(2)}, u32[]{:S(2)}) collective-permute-start(bf16[192,3072]{1,0:T(8,128)(2,1)S(1)} %maximum_select_fusion.refs_0_), channel_id=1, source_target_pairs={{0,2},{1,3},{2,0},{3,1},{4,6},{5,7},{6,4},{7,5},{8,10},{9,11},{10,... | collective-permute-start | bytes 3538952 | tf_op jit(solution)/shard_map/ppermute | solution.py:510
  283.7 47.1 %all-to-all-start.3 = ((bf16[16,64,384]{2,1,0:T(8,128)(2,1)}), bf16[16,64,384]{2,1,0:T(8,128)(2,1)S(1)}, u32[]{:S(2)}, u32[]{:S(2)}) async-start(bf16[16,64,384]{2,1,0:T(8,128)(2,1)} %bitcast.15), calls=%async_computation.3 | async-start | bytes 1572864 | tf_op jit(solution)/shard_map/all_to_all | solution.py:524
  289.1 20.5 %collective-permute-start.34 = (bf16[96,1536]{1,0:T(8,128)(2,1)S(1)}, bf16[96,1536]{1,0:T(8,128)(2,1)}, u32[]{:S(2)}, u32[]{:S(2)}) collective-permute-start(bf16[96,1536]{1,0:T(8,128)(2,1)S(1)} %add_convert_fusion.5), channel_id=1, source_target_pairs={{0,8},{1,9},{2,10},{3,11},{4,12},{5,13},{6,14},{7,15},{8,0},{9,1},... | collective-permute-start | bytes 884744 | tf_op jit(solution)/shard_map/ppermute | solution.py:510
  311.4 9.5 %collective-permute-start.37 = (bf16[48,1536]{1,0:T(8,128)(2,1)S(1)}, bf16[48,1536]{1,0:T(8,128)(2,1)S(1)}, u32[]{:S(2)}, u32[]{:S(2)}) collective-permute-start(bf16[48,1536]{1,0:T(8,128)(2,1)S(1)} %add_convert_fusion.11), channel_id=1, source_target_pairs={{0,16},{1,17},{2,18},{3,19},{4,20},{5,21},{6,22},{7,23},{8,24},{9,... | collective-permute-start | bytes 442376 | tf_op jit(solution)/shard_map/ppermute | solution.py:510
  314.0 28.3 %collective-permute-start.43 = (bf16[192,3072]{1,0:T(8,128)(2,1)S(1)}, bf16[192,3072]{1,0:T(8,128)(2,1)}, u32[]{:S(2)}, u32[]{:S(2)}) collective-permute-start(bf16[192,3072]{1,0:T(8,128)(2,1)S(1)} %maximum_select_fusion.refs_0_), channel_id=1, source_target_pairs={{0,4},{1,5},{2,6},{3,7},{4,0},{5,1},{6,2},{7,3},{8,12},{9,13},{10,... | collective-permute-start | bytes 3538952 | tf_op jit(solution)/shard_map/ppermute | solution.py:510
  315.6 4.2 %collective-permute-start.38 = (f32[12,768]{1,0:T(8,128)S(1)}, f32[12,768]{1,0:T(8,128)}, u32[]{:S(2)}, u32[]{:S(2)}) collective-permute-start(f32[12,768]{1,0:T(8,128)S(1)} %add.296), channel_id=1, source_target_pairs={{0,1},{1,0},{2,3},{3,2},{4,5},{5,4},{6,7},{7,6},{8,9},{9,8},{10,11... | collective-permute-start | bytes 110600 | tf_op jit(solution)/shard_map/ppermute | solution.py:507
  322.2 8.7 %collective-permute-start.39 = (bf16[48,1536]{1,0:T(8,128)(2,1)S(1)}, bf16[48,1536]{1,0:T(8,128)(2,1)}, u32[]{:S(2)}, u32[]{:S(2)}) collective-permute-start(bf16[48,1536]{1,0:T(8,128)(2,1)S(1)} %add_convert_fusion.10), channel_id=1, source_target_pairs={{0,16},{1,17},{2,18},{3,19},{4,20},{5,21},{6,22},{7,23},{8,24},{9,... | collective-permute-start | bytes 442376 | tf_op jit(solution)/shard_map/ppermute | solution.py:510
  322.4 5.2 %collective-permute-start.40 = (f32[12,768]{1,0:T(8,128)S(1)}, f32[12,768]{1,0:T(8,128)S(1)}, u32[]{:S(2)}, u32[]{:S(2)}) collective-permute-start(f32[12,768]{1,0:T(8,128)S(1)} %add.303), channel_id=1, source_target_pairs={{0,8},{1,9},{2,10},{3,11},{4,12},{5,13},{6,14},{7,15},{8,0},{9,1},... | collective-permute-start | bytes 110600 | tf_op jit(solution)/shard_map/ppermute | solution.py:510
  332.4 9.9 %collective-permute-start.41 = (bf16[96,1536]{1,0:T(8,128)(2,1)S(1)}, bf16[96,1536]{1,0:T(8,128)(2,1)S(1)}, u32[]{:S(2)}, u32[]{:S(2)}) collective-permute-start(bf16[96,1536]{1,0:T(8,128)(2,1)S(1)} %maximum_select_fusion.3), channel_id=1, source_target_pairs={{0,8},{1,9},{2,10},{3,11},{4,12},{5,13},{6,14},{7,15},{8,0},{9,1},... | collective-permute-start | bytes 884744 | tf_op jit(solution)/shard_map/ppermute | solution.py:510
  332.4 7.6 %collective-permute-start.42 = (f32[12,768]{1,0:T(8,128)S(1)}, f32[12,768]{1,0:T(8,128)S(1)}, u32[]{:S(2)}, u32[]{:S(2)}) collective-permute-start(f32[12,768]{1,0:T(8,128)S(1)} %add.305), channel_id=1, source_target_pairs={{0,16},{1,17},{2,18},{3,19},{4,20},{5,21},{6,22},{7,23},{8,24},{9,... | collective-permute-start | bytes 110600 | tf_op jit(solution)/shard_map/ppermute | solution.py:510
  342.4 5.0 %collective-permute-start.45 = (bf16[192,3072]{1,0:T(8,128)(2,1)}, bf16[192,3072]{1,0:T(8,128)(2,1)S(1)}, u32[]{:S(2)}, u32[]{:S(2)}) collective-permute-start(bf16[192,3072]{1,0:T(8,128)(2,1)} %collective-permute-done.43.refs_1_), channel_id=1, source_target_pairs={{0,2},{1,3},{2,0},{3,1},{4,6},{5,7},{6,4},{7,5},{8,10},{9,11},{10,... | collective-permute-start | bytes 3538952 | tf_op jit(solution)/shard_map/ppermute | solution.py:510
  342.4 15.7 %collective-permute-start.44 = (bf16[192,1536]{1,0:T(8,128)(2,1)S(1)}, bf16[192,1536]{1,0:T(8,128)(2,1)S(1)}, u32[]{:S(2)}, u32[]{:S(2)}) collective-permute-start(bf16[192,1536]{1,0:T(8,128)(2,1)S(1)} %maximum_select_fusion.2.refs_0_), channel_id=1, source_target_pairs={{0,4},{1,5},{2,6},{3,7},{4,0},{5,1},{6,2},{7,3},{8,12},{9,13},{10,... | collective-permute-start | bytes 1769480 | tf_op jit(solution)/shard_map/ppermute | solution.py:510
  347.2 15.2 %collective-permute-start.46 = (bf16[192,1536]{1,0:T(8,128)(2,1)S(1)}, bf16[192,1536]{1,0:T(8,128)(2,1)S(1)}, u32[]{:S(2)}, u32[]{:S(2)}) collective-permute-start(bf16[192,1536]{1,0:T(8,128)(2,1)S(1)} %maximum_select_fusion.2.refs_0_), channel_id=1, source_target_pairs={{0,2},{1,3},{2,0},{3,1},{4,6},{5,7},{6,4},{7,5},{8,10},{9,11},{10,... | collective-permute-start | bytes 1769480 | tf_op jit(solution)/shard_map/ppermute | solution.py:510
  358.2 4.2 %collective-permute-start.47 = (bf16[192,1536]{1,0:T(8,128)(2,1)S(1)}, bf16[192,1536]{1,0:T(8,128)(2,1)S(1)}, u32[]{:S(2)}, u32[]{:S(2)}) collective-permute-start(bf16[192,1536]{1,0:T(8,128)(2,1)S(1)} %collective-permute-done.44.refs_1_), channel_id=1, source_target_pairs={{0,2},{1,3},{2,0},{3,1},{4,6},{5,7},{6,4},{7,5},{8,10},{9,11},{10,... | collective-permute-start | bytes 1769480 | tf_op jit(solution)/shard_map/ppermute | solution.py:510
  (57 other events, 374.2 us)

commit v3 on v0

--- a/solution.py
+++ b/solution.py
@@ -577,18 +577,19 @@
             [rowwise] * 4, [rows_f, rows_bf, rows_bf, rows_bf],
         )(info, dealt, thought_rows, norms_in, qv_bias, qv_other,
           qkv_weight, qkv_weight, kv_direct, kv_partner)
+        q_direct, keys_own, values_own, normed = lax.optimization_barrier((q_direct, keys_own, values_own, normed))
+        q_partner = flip(q_direct)
         keys_other, values_other = flip(keys_own), flip(values_own)
-        grad_mlp = call(
-            functools.partial(cotangent_kernel, tile, block), "cotangent", (steps,), [pieces_spec], rowwise, rows_bf
-        )(info, cot_pieces)
-        q_direct, grad_mlp = lax.optimization_barrier((q_direct, grad_mlp))
-        q_partner = flip(q_direct)
         queries = call(
             queries_kernel, "queries", (steps,),
             [rowwise, whole((2, half_width)), whole((2, half_width)), one, *q_specs], rowwise, rows_bf,
         )(info, normed, qv_bias, qv_other, qkv_weight, q_direct, q_partner)
-        queries, grad_mlp, keys_other, values_other, out_direct = lax.optimization_barrier(
-            (queries, grad_mlp, keys_other, values_other, out_direct)
+        queries, out_direct, cot_pieces = lax.optimization_barrier((queries, out_direct, cot_pieces))
+        grad_mlp = call(
+            functools.partial(cotangent_kernel, tile, block), "cotangent", (steps,), [pieces_spec], rowwise, rows_bf
+        )(info, cot_pieces)
+        queries, grad_mlp, keys_other, values_other = lax.optimization_barrier(
+            (queries, grad_mlp, keys_other, values_other)
         )
         grad_far = cross(grad_mlp)
         out_partner = flip(out_direct)
@@ -726,15 +727,17 @@
         own, (mlp_stage,) = with_far(own, mlp_section(1))
         mlp_stage = flip(mlp_stage, upper[1])
         keep_own, send_own = attention_grads(0, own)
-        keep_own, send_own, mlp_stage = lax.optimization_barrier((keep_own, send_own, mlp_stage))
+        block_out = gather_slots(restore, block_back, F32)
+        keep_own, send_own, mlp_stage, x_last, block_out = lax.optimization_barrier(
+            (keep_own, send_own, mlp_stage, x_last, block_out)
+        )
         mlp_rows_kept.append((mlp_stage, -starts[2]))
         for level in range(2, levels):
             mlp_rows_kept.append((flip(mlp_section(level), upper[level]), -starts[level + 1]))
         mlp_piece = mlp_section(levels)
         for level in reversed(range(2, levels)):
             mlp_piece = widen(level, mlp_piece, flip(mlp_piece, upper[level]))
-        block_out = gather_slots(restore, block_back, F32)
-        mlp_piece, block_out, *own = lax.optimization_barrier((mlp_piece, block_out, *own))
+        mlp_piece, *own = lax.optimization_barrier((mlp_piece, *own))
         mlp_stage = flip(mlp_piece, upper[1])
         got_own = flip(send_own)
         half_rows = spec((tile, half_width), lambda i, _: (i, 0))
@@ -745,8 +748,8 @@
             [like((slots // 2, 2, block, half_width), BF16), like((4, width), F32)],
             [pltpu.VMEM((tile, width), F32)],
         )(info, inputs, grad_residual, norm_gain[:1], *own, *other, qkv_weight, kv_direct, kv_partner, q_direct, q_partner)
-        input_pieces, small_attn, got_own, x_last, mlp_stage = lax.optimization_barrier(
-            (input_pieces, small_attn, got_own, x_last, mlp_stage)
+        input_pieces, small_attn, got_own, mlp_stage = lax.optimization_barrier(
+            (input_pieces, small_attn, got_own, mlp_stage)
         )
         sent = rows_sum([(keep_own, (1 - near) * half), (got_own, (1 - near) * half), (x_first, 0)], 0, half)
         over_bit = flip(sent, 1)

time: 359 us -> 353 us (0.983)
  waiting for transfers between devices: 107 us -> 95.6 us
    ppermute x36, waiting for transfers between devices: 71 us -> 62.1 us  [flip(): return lax.ppermute(value, AXES, bit_pairs[bit])]
    unnamed x92 -> x98, local copies, waits for them, and re-layouts: 6.96 us -> 8.11 us
  transfers between devices with their start and end apart: 52 -> 52, of which waited for: 27 -> 26; matrix products, arithmetic and copies ran while one was open for 8% -> 9% of each run, Pallas kernels for 36% -> 36%
where the time goes in v3:
time: 353 us; the launch traced here: 352 us
  Pallas kernels  150 us (42%)
  waiting for transfers between devices  95.6 us (27%)
  starting transfers between devices  62.2 us (18%)
  other arithmetic  24.1 us (7%)
  local copies, waits for them, and re-layouts  16.8 us (5%)
    ppermute x36, waiting for transfers between devices, flip(): return lax.ppermute(value, AXES, bit_pairs[bit])  62.1 us
    pallas_call x2, Pallas kernels, mlp_rows(): call(mlp_rows_kernel, 'mlp_rows', (steps, 3), [by_row, by_row, spec((widt...  24.9 us
    ppermute x36, starting transfers between devices, flip(): return lax.ppermute(value, AXES, bit_pairs[bit])  24.6 us
    pallas_call x2, Pallas kernels, attend_backward(): pl.pallas_call(functools.partial(attend_backward_kernel, tile, block), gr...  23.7 us
    ppermute x12, waiting for transfers between devices, cross(): return lax.ppermute(value, AXES, tensor_pairs)  23.7 us
    all_to_all x4, starting transfers between devices, exchange(): lax.all_to_all(array, AXES, split_axis=0, concat_axis=0, tiled=True, axis...  23.3 us
    convert_element_type x10, other arithmetic, rows_sum(): return total.astype(BF16)  17.7 us
    pallas_call x1, Pallas kernels, attend_forward(): pl.pallas_call(functools.partial(attend_forward_kernel, tile, block), gri...  15.3 us
  transfers between devices with their start and end apart: 52, of which 26 were waited for; matrix products, arithmetic and copies ran while one was open for 9% of the time, Pallas kernels for 36%

profile of v3, /device:TPU:0, one launch (start us, length us, event | category | flops | bytes accessed | tf_op | source)
XLA Modules:
  0.0 351.5 jit_solution(341513758219691382)
XLA Ops:
  1.2 2.6 collective-permute-start.3
  6.0 3.3 gather_slots.5
  9.3 7.3 %all-to-all-start = ((bf16[16,64,384]{2,1,0:T(8,128)(2,1)}), bf16[16,64,384]{2,1,0:T(8,128)(2,1)S(1)}, u32[]{:S(2)}, u32[]{:S(2)}) async-start(bf16[16,64,384]{2,1,0:T(8,128)(2,1)} %gather_slots.5), calls=%async_computation | async-start | bytes 1572864 | tf_op jit(solution)/shard_map/all_to_all | solution.py:524
  22.2 3.3 gather_slots.4
  31.1 5.4 %all-to-all-done = bf16[16,64,384]{2,1,0:T(8,128)(2,1)S(1)} async-done(((bf16[16,64,384]{2,1,0:T(8,128)(2,1)}), bf16[16,64,384]{2,1,0:T(8,128)(2,1)S(1)}, u32[]{:S(2)}, u32[]{:S(2)}) %all-to-all-start) | async-done | bytes 786464 | tf_op jit(solution)/shard_map/all_to_all | solution.py:524
  36.5 5.0 %all-to-all-start.1 = ((bf16[16,64,384]{2,1,0:T(8,128)(2,1)}), bf16[16,64,384]{2,1,0:T(8,128)(2,1)S(1)}, u32[]{:S(2)}, u32[]{:S(2)}) async-start(bf16[16,64,384]{2,1,0:T(8,128)(2,1)} %gather_slots.4), calls=%async_computation.1 | async-start | bytes 1572864 | tf_op jit(solution)/shard_map/all_to_all | solution.py:524
  44.3 6.9 %enter.1 = (f32[512,768]{1,0:T(8,128)}, bf16[512,768]{1,0:T(8,128)(2,1)}, bf16[512,768]{1,0:T(8,128)(2,1)}, bf16[512,768]{1,0:T(8,128)(2,1)}) custom-call(s32[10]{0:T(128)} %concatenate.50.info, bf16[8,2,64,384]{3,2,1,0:T(8,128)(2,1)} %bitcast.13, f32[6,768]{1,0:T(8,128)} %fusion.1.thoughts, f32[2,768]{1,0:T(2,128)} %pad_maximum_fusion.2.norms, ...), custom_call_target="tpu_custom_call" | custom-call | tf_op jit(solution)/shard_map/enter/pallas_call | solution.py:574
  51.2 5.8 %collective-permute-done.5.direct.direct_q = bf16[1,384,384]{2,1,0:T(8,128)(2,1)S(1)} collective-permute-done((bf16[1,384,384]{2,1,0:T(8,128)(2,1)}, bf16[1,384,384]{2,1,0:T(8,128)(2,1)S(1)}, u32[]{:S(2)}, u32[]{:S(2)}) %collective-permute-start.5) | collective-permute-done | bytes 294944 | tf_op jit(solution)/shard_map/ppermute | solution.py:507
  58.3 2.8 collective-permute-done.7.partner.partner_q
  61.8 4.0 %queries.1.q_ref = bf16[512,768]{1,0:T(8,128)(2,1)} custom-call(s32[10]{0:T(128)} %concatenate.50.info, bf16[512,768]{1,0:T(8,128)(2,1)} %get-tuple-element.171.normed, f32[2,384]{1,0:T(2,128)} %bias_own.3, f32[2,384]{1,0:T(2,128)} %copy-done.37, bf16[3,768,384]{2,1,0:T(8,128)(2,1)} %own.7, bf16[1,384,384]{2,1,0:T(8,128)(2,1)} %copy-done.18, ...), custom_call_target="tpu_custom_call" | custom-call | tf_op jit(solution)/shard_map/queries/pallas_call | solution.py:583
  68.1 2.8 cotangent.1.grad.grad0
  72.1 15.3 %attend_forward.1 = (bf16[512,768]{1,0:T(8,128)(2,1)}, f32[6,2,512]{2,1,0:T(2,128)}) custom-call(s32[10]{0:T(128)} %concatenate.50.info, bf16[512,768]{1,0:T(8,128)(2,1)} %queries.1.q_ref, bf16[512,768]{1,0:T(8,128)(2,1)} %get-tuple-element.177.ko_ref, bf16[512,768]{1,0:T(8,128)(2,1)} %get-tuple-element.178.vo_ref, bf16[512,768]{1,0:T(8,128)(2,1)} %copy-done, ...), custom_call_target="tpu_custom_call" | custom-call | tf_op jit(solution)/shard_map/attend_forward/pallas_call | solution.py:139
  87.4 2.9 collective-permute-done.11.grad.grad1
  91.1 5.1 %middle.1 = (f32[512,768]{1,0:T(8,128)}, bf16[512,768]{1,0:T(8,128)(2,1)}) custom-call(s32[10]{0:T(128)} %concatenate.50.info, bf16[512,768]{1,0:T(8,128)(2,1)} %get-tuple-element.184.heads.out_ref, f32[512,768]{1,0:T(8,128)} %get-tuple-element.185.inputs, f32[3,768]{1,0:T(4,128)} %pad_maximum_fusion.1.norms, bf16[384,768]{1,0:T(8,128)(2,1)} %own.6, ...), custom_call_target="tpu_custom_call" | custom-call | tf_op jit(solution)/shard_map/middle/pallas_call | solution.py:598
  97.5 12.7 %mlp_rows.2 = (f32[512,768]{1,0:T(8,128)}, f32[512,768]{1,0:T(8,128)}, bf16[1536,512]{1,0:T(8,128)(2,1)}, bf16[512,1536]{1,0:T(8,128)(2,1)}, f32[2,1,1536]{2,1,0:T(1,128)}) custom-call(s32[10]{0:T(128)} %concatenate.50.info, bf16[512,768]{1,0:T(8,128)(2,1)} %get-tuple-element.188.normed.normed0, bf16[512,768]{1,0:T(8,128)(2,1)} %cotangent.1.grad.grad0, ...), custom_call_target="tpu_custom_call" | custom-call | tf_op jit(solution)/shard_map/mlp_rows/pallas_call | solution.py:613
  110.3 4.4 %collective-permute-done.13.normed.normed1 = bf16[512,768]{1,0:T(8,128)(2,1)S(1)} collective-permute-done((bf16[512,768]{1,0:T(8,128)(2,1)}, bf16[512,768]{1,0:T(8,128)(2,1)S(1)}, u32[]{:S(2)}, u32[]{:S(2)}) %collective-permute-start.13) | collective-permute-done | bytes 786464 | tf_op jit(solution)/shard_map/ppermute | solution.py:507
  115.6 12.1 %mlp_rows.3 = (bf16[512,768]{1,0:T(8,128)(2,1)}, bf16[512,768]{1,0:T(8,128)(2,1)}, bf16[1536,512]{1,0:T(8,128)(2,1)}, bf16[512,1536]{1,0:T(8,128)(2,1)}, f32[2,1,1536]{2,1,0:T(1,128)}) custom-call(s32[10]{0:T(128)} %concatenate.50.info, bf16[512,768]{1,0:T(8,128)(2,1)} %copy-done.9, bf16[512,768]{1,0:T(8,128)(2,1)} %copy-done.8, bf16[768,1536]{1,0:T(8,128)(2,1)} %fc.3, ...), custom_call_target="tpu_custom_call" | custom-call | tf_op jit(solution)/shard_map/mlp_rows/pallas_call | solution.py:613
  128.5 10.5 %mlp_grads.1 = (bf16[384,3072]{1,0:T(8,128)(2,1)}, bf16[384,3072]{1,0:T(8,128)(2,1)}) custom-call(s32[10]{0:T(128)} %concatenate.50.info, bf16[512,768]{1,0:T(8,128)(2,1)} %get-tuple-element.188.normed.normed0, bf16[512,768]{1,0:T(8,128)(2,1)} %copy-done.9, bf16[512,768]{1,0:T(8,128)(2,1)} %cotangent.1.grad.grad0, bf16[512,768]{1,0:T(8,128)(2,1)} %copy-done.8, ...), custom_call_target="tpu_custom_call" | custom-call | tf_op jit(solution)/shard_map/mlp_grads/pallas_call | solution.py:631
  139.0 6.4 %collective-permute-done.14.back_far = bf16[512,768]{1,0:T(8,128)(2,1)S(1)} collective-permute-done((bf16[512,768]{1,0:T(8,128)(2,1)}, bf16[512,768]{1,0:T(8,128)(2,1)S(1)}, u32[]{:S(2)}, u32[]{:S(2)}) %collective-permute-start.14) | collective-permute-done | bytes 786464 | tf_op jit(solution)/shard_map/ppermute | solution.py:507
  146.3 6.7 %back.1 = (f32[512,768]{1,0:T(8,128)}, bf16[512,768]{1,0:T(8,128)(2,1)}, bf16[512,768]{1,0:T(8,128)(2,1)}, f32[4,768]{1,0:T(4,128)}) custom-call(s32[10]{0:T(128)} %concatenate.50.info, f32[512,768]{1,0:T(8,128)} %get-tuple-element.189.back, bf16[512,768]{1,0:T(8,128)(2,1)} %copy-done.26, f32[512,768]{1,0:T(8,128)} %get-tuple-element.202.residual, ...), custom_call_target="tpu_custom_call" | custom-call | tf_op jit(solution)/shard_map/back/pallas_call | solution.py:662
  156.2 2.3 collective-permute-start.17
  158.5 11.9 %attend_backward.2 = (bf16[512,384]{1,0:T(8,128)(2,1)}, f32[512,384]{1,0:T(8,128)}, f32[512,384]{1,0:T(8,128)}, bf16[512,384]{1,0:T(8,128)(2,1)}, bf16[512,384]{1,0:T(8,128)(2,1)}) custom-call(s32[10]{0:T(128)} %concatenate.50.info, bf16[512,768]{1,0:T(8,128)(2,1)} %queries.1.q_ref, bf16[512,768]{1,0:T(8,128)(2,1)} %get-tuple-element.177.ko_ref, ...), custom_call_target="tpu_custom_call" | custom-call | tf_op jit(solution)/shard_map/attend_backward/pallas_call | solution.py:162
  175.0 3.8 %block.1 = bf16[8,2,64,384]{3,2,1,0:T(8,128)(2,1)} custom-call(s32[10]{0:T(128)} %concatenate.50.info, f32[512,768]{1,0:T(8,128)} %get-tuple-element.202.residual, f32[512,768]{1,0:T(8,128)} %get-tuple-element.224.mlp, bf16[512,768]{1,0:T(8,128)(2,1)} %collective-permute-done.15.mlp_far, f32[1,768]{1,0:T(1,128)} %get-tuple-element.325.bias), custom_call_target="tpu_custom_call" | custom-call | tf_op jit(solution)/shard_map/block/pallas_call | solution.py:695
  179.6 6.0 %attention_grads.2 = (bf16[384,1536]{1,0:T(8,128)(2,1)}, bf16[384,1536]{1,0:T(8,128)(2,1)}) custom-call(s32[10]{0:T(128)} %concatenate.50.info, bf16[512,768]{1,0:T(8,128)(2,1)} %get-tuple-element.171.normed, bf16[512,768]{1,0:T(8,128)(2,1)} %get-tuple-element.184.heads.out_ref, bf16[512,768]{1,0:T(8,128)(2,1)} %get-tuple-element.203.grad_attn, ...), custom_call_target="tpu_custom_call" | custom-call | tf_op jit(solution)/shard_map/attention_grads/pallas_call | solution.py:705
  185.8 2.4 add_convert_fusion.1
  188.9 2.5 add_convert_fusion.2
  193.3 5.9 %all-to-all-start.2 = ((bf16[16,64,384]{2,1,0:T(8,128)(2,1)}), bf16[16,64,384]{2,1,0:T(8,128)(2,1)S(1)}, u32[]{:S(2)}, u32[]{:S(2)}) async-start(bf16[16,64,384]{2,1,0:T(8,128)(2,1)} %bitcast.8), calls=%async_computation.2 | async-start | bytes 1572864 | tf_op jit(solution)/shard_map/all_to_all | solution.py:524
  201.1 11.9 %attend_backward.3 = (bf16[512,384]{1,0:T(8,128)(2,1)}, f32[512,384]{1,0:T(8,128)}, f32[512,384]{1,0:T(8,128)}, bf16[512,384]{1,0:T(8,128)(2,1)}, bf16[512,384]{1,0:T(8,128)(2,1)}) custom-call(s32[10]{0:T(128)} %concatenate.50.info, bf16[512,768]{1,0:T(8,128)(2,1)} %queries.1.q_ref, bf16[512,768]{1,0:T(8,128)(2,1)} %get-tuple-element.177.ko_ref, ...), custom_call_target="tpu_custom_call" | custom-call | tf_op jit(solution)/shard_map/attend_backward/pallas_call | solution.py:162
  213.0 2.8 collective-permute-done.23
  220.3 4.5 %all-to-all-done.2.array_ref = bf16[16,64,384]{2,1,0:T(8,128)(2,1)S(1)} async-done(((bf16[16,64,384]{2,1,0:T(8,128)(2,1)}), bf16[16,64,384]{2,1,0:T(8,128)(2,1)S(1)}, u32[]{:S(2)}, u32[]{:S(2)}) %all-to-all-start.2) | async-done | bytes 786464 | tf_op jit(solution)/shard_map/all_to_all | solution.py:524
  225.6 3.5 gather_slots.6
  229.1 6.0 %attention_grads.3 = (bf16[384,1536]{1,0:T(8,128)(2,1)}, bf16[384,1536]{1,0:T(8,128)(2,1)}) custom-call(s32[10]{0:T(128)} %concatenate.50.info, bf16[512,768]{1,0:T(8,128)(2,1)} %get-tuple-element.171.normed, bf16[512,768]{1,0:T(8,128)(2,1)} %get-tuple-element.184.heads.out_ref, bf16[512,768]{1,0:T(8,128)(2,1)} %get-tuple-element.203.grad_attn, ...), custom_call_target="tpu_custom_call" | custom-call | tf_op jit(solution)/shard_map/attention_grads/pallas_call | solution.py:705
  236.9 9.4 %leave.1 = (bf16[8,2,64,384]{3,2,1,0:T(8,128)(2,1)}, f32[4,768]{1,0:T(4,128)}) custom-call(s32[10]{0:T(128)} %concatenate.50.info, f32[512,768]{1,0:T(8,128)} %get-tuple-element.185.inputs, f32[512,768]{1,0:T(8,128)} %get-tuple-element.263.grad_residual, f32[1,768]{1,0:T(1,128)} %copy-done.34, bf16[512,384]{1,0:T(8,128)(2,1)} %get-tuple-element.266.dq.dq0, ...), custom_call_target="tpu_custom_call" | custom-call | tf_op jit(solution)/shard_map/leave/pallas_call | solution.py:744
  246.3 5.9 %collective-permute-done.30 = bf16[48,3072]{1,0:T(8,128)(2,1)S(1)} collective-permute-done((bf16[48,3072]{1,0:T(8,128)(2,1)S(1)}, bf16[48,3072]{1,0:T(8,128)(2,1)S(1)}, u32[]{:S(2)}, u32[]{:S(2)}) %collective-permute-start.30) | collective-permute-done | bytes 294944 | tf_op jit(solution)/shard_map/ppermute | solution.py:510
  252.2 5.2 %all-to-all-start.3 = ((bf16[16,64,384]{2,1,0:T(8,128)(2,1)}), bf16[16,64,384]{2,1,0:T(8,128)(2,1)S(1)}, u32[]{:S(2)}, u32[]{:S(2)}) async-start(bf16[16,64,384]{2,1,0:T(8,128)(2,1)} %bitcast.15), calls=%async_computation.3 | async-start | bytes 1572864 | tf_op jit(solution)/shard_map/all_to_all | solution.py:524
  259.5 2.3 add_convert_fusion
  264.6 20.1 %collective-permute-done.32 = bf16[96,3072]{1,0:T(8,128)(2,1)S(1)} collective-permute-done((bf16[96,3072]{1,0:T(8,128)(2,1)S(1)}, bf16[96,3072]{1,0:T(8,128)(2,1)S(1)}, u32[]{:S(2)}, u32[]{:S(2)}) %collective-permute-start.32) | collective-permute-done | bytes 589856 | tf_op jit(solution)/shard_map/ppermute | solution.py:510
  288.1 2.4 collective-permute-done.35
  291.1 3.1 collective-permute-done.34
  300.7 3.6 %collective-permute-done.36 = bf16[48,1536]{1,0:T(8,128)(2,1)S(1)} collective-permute-done((bf16[48,1536]{1,0:T(8,128)(2,1)S(1)}, bf16[48,1536]{1,0:T(8,128)(2,1)S(1)}, u32[]{:S(2)}, u32[]{:S(2)}) %collective-permute-start.36) | collective-permute-done | bytes 147488 | tf_op jit(solution)/shard_map/ppermute | solution.py:510
  308.4 2.2 collective-permute-done.39
  310.6 2.4 collective-permute-done.38
  313.1 3.1 collective-permute-start.41
  320.4 7.2 %collective-permute-done.43.refs_1_ = bf16[192,3072]{1,0:T(8,128)(2,1)S(1)} collective-permute-done((bf16[192,3072]{1,0:T(8,128)(2,1)S(1)}, bf16[192,3072]{1,0:T(8,128)(2,1)S(1)}, u32[]{:S(2)}, u32[]{:S(2)}) %collective-permute-start.43) | collective-permute-done | bytes 1179680 | tf_op jit(solution)/shard_map/ppermute | solution.py:510
  328.2 3.5 gather_slots.7
  332.0 6.3 %finish_mlp.1 = (f32[768,1536]{1,0:T(8,128)}, f32[1536,768]{1,0:T(8,128)}) custom-call(s32[10]{0:T(128)} %concatenate.50.info, bf16[192,3072]{1,0:T(8,128)(2,1)} %copy-done.2, bf16[192,3072]{1,0:T(8,128)(2,1)} %copy-done.23, bf16[192,3072]{1,0:T(8,128)(2,1)} %copy-done.22, bf16[192,3072]{1,0:T(8,128)(2,1)} %collective-permute-done.45.refs_3_), custom_call_target="tpu_custom_call" | custom-call | tf_op jit(solution)/shard_map/finish_mlp/pallas_call | solution.py:795
  338.3 5.0 %collective-permute-done.42.refs_1_ = bf16[192,1536]{1,0:T(8,128)(2,1)S(1)} collective-permute-done((bf16[192,1536]{1,0:T(8,128)(2,1)S(1)}, bf16[192,1536]{1,0:T(8,128)(2,1)S(1)}, u32[]{:S(2)}, u32[]{:S(2)}) %collective-permute-start.42) | collective-permute-done | bytes 589856 | tf_op jit(solution)/shard_map/ppermute | solution.py:510
  346.8 4.7 %finish_attention.1 = (f32[3,768,384]{2,1,0:T(8,128)}, f32[384,768]{1,0:T(8,128)}) custom-call(s32[10]{0:T(128)} %concatenate.50.info, bf16[192,1536]{1,0:T(8,128)(2,1)} %copy-done.10, bf16[192,1536]{1,0:T(8,128)(2,1)} %copy-done.27, bf16[192,1536]{1,0:T(8,128)(2,1)} %collective-permute-done.46.refs_2_, bf16[192,1536]{1,0:T(8,128)(2,1)} %copy-done.29), custom_call_target="tpu_custom_call" | custom-call | tf_op jit(solution)/shard_map/finish_attention/pallas_call | solution.py:801
  (226 shorter events, 73.5 us)
Async XLA Ops:
  0.7 28.1 %collective-permute-start.4 = (s32[1,6]{1,0:T(1,128)}, s32[1,6]{1,0:T(1,128)S(1)}, u32[]{:S(2)}, u32[]{:S(2)}) collective-permute-start(s32[1,6]{1,0:T(1,128)} %param.18), channel_id=1, source_target_pairs={{0,2},{1,3},{2,0},{3,1},{4,6},{5,7},{6,4},{7,5},{8,10},{9,11},{10,... | collective-permute-start | bytes 80 | tf_op jit(solution)/shard_map/ppermute | solution.py:510
  1.2 29.9 %collective-permute-start.3 = (f32[2,384]{1,0:T(2,128)}, f32[2,384]{1,0:T(2,128)S(1)}, u32[]{:S(2)}, u32[]{:S(2)}) collective-permute-start(f32[2,384]{1,0:T(2,128)} %bias_own.3), channel_id=1, source_target_pairs={{0,1},{1,0},{2,3},{3,2},{4,5},{5,4},{6,7},{7,6},{8,9},{9,8},{10,11... | collective-permute-start | bytes 9224 | tf_op jit(solution)/shard_map/ppermute | solution.py:507
  5.0 26.0 %collective-permute-start = (bf16[2,384,384]{2,1,0:T(8,128)(2,1)S(1)}, bf16[2,384,384]{2,1,0:T(8,128)(2,1)S(1)}, u32[]{:S(2)}, u32[]{:S(2)}) collective-permute-start(bf16[2,384,384]{2,1,0:T(8,128)(2,1)S(1)} %constant_dynamic-slice_fusion.3), channel_id=1, source_target_pairs={{0,1},{1,0},{2,3},{3,2},{4,5},{5,4},{6,7},{7,6},{8,9},{9,8},{10,11... | collective-permute-start | bytes 1769480 | tf_op jit(solution)/shard_map/ppermute | solution.py:507
  9.3 27.2 %all-to-all-start = ((bf16[16,64,384]{2,1,0:T(8,128)(2,1)}), bf16[16,64,384]{2,1,0:T(8,128)(2,1)S(1)}, u32[]{:S(2)}, u32[]{:S(2)}) async-start(bf16[16,64,384]{2,1,0:T(8,128)(2,1)} %gather_slots.5), calls=%async_computation | async-start | bytes 1572864 | tf_op jit(solution)/shard_map/all_to_all | solution.py:524
  26.7 3.7 %collective-permute-start.2 = (bf16[6,384]{1,0:T(8,128)(2,1)S(1)}, bf16[6,384]{1,0:T(8,128)(2,1)S(1)}, u32[]{:S(2)}, u32[]{:S(2)}) collective-permute-start(bf16[6,384]{1,0:T(8,128)(2,1)S(1)} %get-tuple-element.324), channel_id=1, source_target_pairs={{0,1},{1,0},{2,3},{3,2},{4,5},{5,4},{6,7},{7,6},{8,9},{9,8},{10,11... | collective-permute-start | bytes 13832 | tf_op jit(solution)/shard_map/ppermute | solution.py:507
  36.5 30.7 %all-to-all-start.1 = ((bf16[16,64,384]{2,1,0:T(8,128)(2,1)}), bf16[16,64,384]{2,1,0:T(8,128)(2,1)S(1)}, u32[]{:S(2)}, u32[]{:S(2)}) async-start(bf16[16,64,384]{2,1,0:T(8,128)(2,1)} %gather_slots.4), calls=%async_computation.1 | async-start | bytes 1572864 | tf_op jit(solution)/shard_map/all_to_all | solution.py:524
  41.5 15.5 %collective-permute-start.5 = (bf16[1,384,384]{2,1,0:T(8,128)(2,1)}, bf16[1,384,384]{2,1,0:T(8,128)(2,1)S(1)}, u32[]{:S(2)}, u32[]{:S(2)}) collective-permute-start(bf16[1,384,384]{2,1,0:T(8,128)(2,1)} %constant_dynamic-slice_fusion), channel_id=1, source_target_pairs={{0,1},{1,0},{2,3},{3,2},{4,5},{5,4},{6,7},{7,6},{8,9},{9,8},{10,11... | collective-permute-start | bytes 884744 | tf_op jit(solution)/shard_map/ppermute | solution.py:507
  57.0 13.9 %collective-permute-start.9 = (bf16[512,768]{1,0:T(8,128)(2,1)}, bf16[512,768]{1,0:T(8,128)(2,1)S(1)}, u32[]{:S(2)}, u32[]{:S(2)}) collective-permute-start(bf16[512,768]{1,0:T(8,128)(2,1)} %get-tuple-element.177.ko_ref), channel_id=1, source_target_pairs={{0,2},{1,3},{2,0},{3,1},{4,6},{5,7},{6,4},{7,5},{8,10},{9,11},{10,... | collective-permute-start | bytes 2359304 | tf_op jit(solution)/shard_map/ppermute | solution.py:510
  57.0 13.9 %collective-permute-start.10 = (bf16[512,768]{1,0:T(8,128)(2,1)}, bf16[512,768]{1,0:T(8,128)(2,1)S(1)}, u32[]{:S(2)}, u32[]{:S(2)}) collective-permute-start(bf16[512,768]{1,0:T(8,128)(2,1)} %get-tuple-element.178.vo_ref), channel_id=1, source_target_pairs={{0,2},{1,3},{2,0},{3,1},{4,6},{5,7},{6,4},{7,5},{8,10},{9,11},{10,... | collective-permute-start | bytes 2359304 | tf_op jit(solution)/shard_map/ppermute | solution.py:510
  57.5 3.5 %collective-permute-start.7 = (bf16[1,384,384]{2,1,0:T(8,128)(2,1)S(1)}, bf16[1,384,384]{2,1,0:T(8,128)(2,1)S(1)}, u32[]{:S(2)}, u32[]{:S(2)}) collective-permute-start(bf16[1,384,384]{2,1,0:T(8,128)(2,1)S(1)} %collective-permute-done.5.direct.direct_q), channel_id=1, source_target_pairs={{0,2},{1,3},{2,0},{3,1},{4,6},{5,7},{6,4},{7,5},{8,10},{9,11},{10,... | collective-permute-start | bytes 884744 | tf_op jit(solution)/shard_map/ppermute | solution.py:510
  57.5 9.6 %collective-permute-start.8 = (bf16[384,384]{1,0:T(8,128)(2,1)}, bf16[384,384]{1,0:T(8,128)(2,1)S(1)}, u32[]{:S(2)}, u32[]{:S(2)}) collective-permute-start(bf16[384,384]{1,0:T(8,128)(2,1)} %constant_dynamic-slice_fusion.2), channel_id=1, source_target_pairs={{0,1},{1,0},{2,3},{3,2},{4,5},{5,4},{6,7},{7,6},{8,9},{9,8},{10,11... | collective-permute-start | bytes 884744 | tf_op jit(solution)/shard_map/ppermute | solution.py:507
  70.9 19.4 %collective-permute-start.11 = (bf16[512,768]{1,0:T(8,128)(2,1)}, bf16[512,768]{1,0:T(8,128)(2,1)S(1)}, u32[]{:S(2)}, u32[]{:S(2)}) collective-permute-start(bf16[512,768]{1,0:T(8,128)(2,1)} %cotangent.1.grad.grad0), channel_id=1, source_target_pairs={{0,1},{1,0},{2,3},{3,2},{4,5},{5,4},{6,7},{7,6},{8,9},{9,8},{10,11... | collective-permute-start | bytes 2359304 | tf_op jit(solution)/shard_map/ppermute | solution.py:507
  71.7 18.6 %collective-permute-start.12 = (bf16[384,384]{1,0:T(8,128)(2,1)S(1)}, bf16[384,384]{1,0:T(8,128)(2,1)S(1)}, u32[]{:S(2)}, u32[]{:S(2)}) collective-permute-start(bf16[384,384]{1,0:T(8,128)(2,1)S(1)} %collective-permute-done.8.direct), channel_id=1, source_target_pairs={{0,2},{1,3},{2,0},{3,1},{4,6},{5,7},{6,4},{7,5},{8,10},{9,11},{10,... | collective-permute-start | bytes 884744 | tf_op jit(solution)/shard_map/ppermute | solution.py:510
  96.1 18.5 %collective-permute-start.13 = (bf16[512,768]{1,0:T(8,128)(2,1)}, bf16[512,768]{1,0:T(8,128)(2,1)S(1)}, u32[]{:S(2)}, u32[]{:S(2)}) collective-permute-start(bf16[512,768]{1,0:T(8,128)(2,1)} %get-tuple-element.188.normed.normed0), channel_id=1, source_target_pairs={{0,1},{1,0},{2,3},{3,2},{4,5},{5,4},{6,7},{7,6},{8,9},{9,8},{10,11... | collective-permute-start | bytes 2359304 | tf_op jit(solution)/shard_map/ppermute | solution.py:507
  127.7 17.7 %collective-permute-start.14 = (bf16[512,768]{1,0:T(8,128)(2,1)}, bf16[512,768]{1,0:T(8,128)(2,1)S(1)}, u32[]{:S(2)}, u32[]{:S(2)}) collective-permute-start(bf16[512,768]{1,0:T(8,128)(2,1)} %get-tuple-element.193), channel_id=1, source_target_pairs={{0,1},{1,0},{2,3},{3,2},{4,5},{5,4},{6,7},{7,6},{8,9},{9,8},{10,11... | collective-permute-start | bytes 2359304 | tf_op jit(solution)/shard_map/ppermute | solution.py:507
  145.4 7.6 %collective-permute-start.16 = (bf16[384,3072]{1,0:T(8,128)(2,1)}, bf16[384,3072]{1,0:T(8,128)(2,1)}, u32[]{:S(2)}, u32[]{:S(2)}) collective-permute-start(bf16[384,3072]{1,0:T(8,128)(2,1)} %get-tuple-element.206), channel_id=1, source_target_pairs={{0,2},{1,3},{2,0},{3,1},{4,6},{5,7},{6,4},{7,5},{8,10},{9,11},{10,... | collective-permute-start | bytes 7077896 | tf_op jit(solution)/shard_map/ppermute | solution.py:510
  145.4 25.0 %collective-permute-start.15 = (bf16[512,768]{1,0:T(8,128)(2,1)}, bf16[512,768]{1,0:T(8,128)(2,1)}, u32[]{:S(2)}, u32[]{:S(2)}) collective-permute-start(bf16[512,768]{1,0:T(8,128)(2,1)} %get-tuple-element.204), channel_id=1, source_target_pairs={{0,1},{1,0},{2,3},{3,2},{4,5},{5,4},{6,7},{7,6},{8,9},{9,8},{10,11... | collective-permute-start | bytes 2359304 | tf_op jit(solution)/shard_map/ppermute | solution.py:507
  156.2 15.7 %collective-permute-start.17 = (bf16[96,3072]{1,0:T(8,128)(2,1)S(1)}, bf16[96,3072]{1,0:T(8,128)(2,1)S(1)}, u32[]{:S(2)}, u32[]{:S(2)}) collective-permute-start(bf16[96,3072]{1,0:T(8,128)(2,1)S(1)} %add_convert_fusion.4), channel_id=1, source_target_pairs={{0,4},{1,5},{2,6},{3,7},{4,0},{5,1},{6,2},{7,3},{8,12},{9,13},{10,... | collective-permute-start | bytes 1769480 | tf_op jit(solution)/shard_map/ppermute | solution.py:510
  172.7 6.0 %collective-permute-start.18 = (bf16[512,384]{1,0:T(8,128)(2,1)}, bf16[512,384]{1,0:T(8,128)(2,1)S(1)}, u32[]{:S(2)}, u32[]{:S(2)}) collective-permute-start(bf16[512,384]{1,0:T(8,128)(2,1)} %get-tuple-element.222), channel_id=1, source_target_pairs={{0,2},{1,3},{2,0},{3,1},{4,6},{5,7},{6,4},{7,5},{8,10},{9,11},{10,... | collective-permute-start | bytes 1179656 | tf_op jit(solution)/shard_map/ppermute | solution.py:510
  172.7 6.0 %collective-permute-start.19 = (bf16[512,384]{1,0:T(8,128)(2,1)}, bf16[512,384]{1,0:T(8,128)(2,1)S(1)}, u32[]{:S(2)}, u32[]{:S(2)}) collective-permute-start(bf16[512,384]{1,0:T(8,128)(2,1)} %get-tuple-element.223), channel_id=1, source_target_pairs={{0,2},{1,3},{2,0},{3,1},{4,6},{5,7},{6,4},{7,5},{8,10},{9,11},{10,... | collective-permute-start | bytes 1179656 | tf_op jit(solution)/shard_map/ppermute | solution.py:510
  173.3 12.4 %collective-permute-start.20 = (bf16[48,3072]{1,0:T(8,128)(2,1)}, bf16[48,3072]{1,0:T(8,128)(2,1)S(1)}, u32[]{:S(2)}, u32[]{:S(2)}) collective-permute-start(bf16[48,3072]{1,0:T(8,128)(2,1)} %get-tuple-element.232), channel_id=1, source_target_pairs={{0,4},{1,5},{2,6},{3,7},{4,0},{5,1},{6,2},{7,3},{8,12},{9,13},{10,... | collective-permute-start | bytes 884744 | tf_op jit(solution)/shard_map/ppermute | solution.py:510
  185.7 3.3 collective-permute-start.21
  191.5 21.5 %collective-permute-start.22 = (bf16[192,1536]{1,0:T(8,128)(2,1)}, bf16[192,1536]{1,0:T(8,128)(2,1)}, u32[]{:S(2)}, u32[]{:S(2)}) collective-permute-start(bf16[192,1536]{1,0:T(8,128)(2,1)} %get-tuple-element.237), channel_id=1, source_target_pairs={{0,1},{1,0},{2,3},{3,2},{4,5},{5,4},{6,7},{7,6},{8,9},{9,8},{10,11... | collective-permute-start | bytes 1769480 | tf_op jit(solution)/shard_map/ppermute | solution.py:507
  192.9 22.8 %collective-permute-start.23 = (bf16[96,3072]{1,0:T(8,128)(2,1)}, bf16[96,3072]{1,0:T(8,128)(2,1)}, u32[]{:S(2)}, u32[]{:S(2)}) collective-permute-start(bf16[96,3072]{1,0:T(8,128)(2,1)} %add_convert_fusion.1), channel_id=1, source_target_pairs={{0,8},{1,9},{2,10},{3,11},{4,12},{5,13},{6,14},{7,15},{8,0},{9,1},... | collective-permute-start | bytes 1769480 | tf_op jit(solution)/shard_map/ppermute | solution.py:510
  193.3 31.5 %all-to-all-start.2 = ((bf16[16,64,384]{2,1,0:T(8,128)(2,1)}), bf16[16,64,384]{2,1,0:T(8,128)(2,1)S(1)}, u32[]{:S(2)}, u32[]{:S(2)}) async-start(bf16[16,64,384]{2,1,0:T(8,128)(2,1)} %bitcast.8), calls=%async_computation.2 | async-start | bytes 1572864 | tf_op jit(solution)/shard_map/all_to_all | solution.py:524
  199.1 13.9 %collective-permute-start.24 = (bf16[48,3072]{1,0:T(8,128)(2,1)S(1)}, bf16[48,3072]{1,0:T(8,128)(2,1)}, u32[]{:S(2)}, u32[]{:S(2)}) collective-permute-start(bf16[48,3072]{1,0:T(8,128)(2,1)S(1)} %copy-done.31), channel_id=1, source_target_pairs={{0,4},{1,5},{2,6},{3,7},{4,0},{5,1},{6,2},{7,3},{8,12},{9,13},{10,... | collective-permute-start | bytes 884744 | tf_op jit(solution)/shard_map/ppermute | solution.py:510
  215.8 3.1 collective-permute-start.25
  215.8 3.1 collective-permute-start.26
  216.3 18.8 %collective-permute-start.28 = (bf16[192,1536]{1,0:T(8,128)(2,1)}, bf16[192,1536]{1,0:T(8,128)(2,1)}, u32[]{:S(2)}, u32[]{:S(2)}) collective-permute-start(bf16[192,1536]{1,0:T(8,128)(2,1)} %get-tuple-element.259), channel_id=1, source_target_pairs={{0,1},{1,0},{2,3},{3,2},{4,5},{5,4},{6,7},{7,6},{8,9},{9,8},{10,11... | collective-permute-start | bytes 1769480 | tf_op jit(solution)/shard_map/ppermute | solution.py:507
  218.9 16.4 %collective-permute-start.27 = (bf16[48,3072]{1,0:T(8,128)(2,1)}, bf16[48,3072]{1,0:T(8,128)(2,1)}, u32[]{:S(2)}, u32[]{:S(2)}) collective-permute-start(bf16[48,3072]{1,0:T(8,128)(2,1)} %add_convert_fusion.7), channel_id=1, source_target_pairs={{0,16},{1,17},{2,18},{3,19},{4,20},{5,21},{6,22},{7,23},{8,24},{9,... | collective-permute-start | bytes 884744 | tf_op jit(solution)/shard_map/ppermute | solution.py:510
  235.2 16.9 %collective-permute-start.29 = (bf16[384,1536]{1,0:T(8,128)(2,1)}, bf16[384,1536]{1,0:T(8,128)(2,1)}, u32[]{:S(2)}, u32[]{:S(2)}) collective-permute-start(bf16[384,1536]{1,0:T(8,128)(2,1)} %get-tuple-element.273), channel_id=1, source_target_pairs={{0,2},{1,3},{2,0},{3,1},{4,6},{5,7},{6,4},{7,5},{8,10},{9,11},{10,... | collective-permute-start | bytes 3538952 | tf_op jit(solution)/shard_map/ppermute | solution.py:510
  236.7 15.5 %collective-permute-start.30 = (bf16[48,3072]{1,0:T(8,128)(2,1)S(1)}, bf16[48,3072]{1,0:T(8,128)(2,1)S(1)}, u32[]{:S(2)}, u32[]{:S(2)}) collective-permute-start(bf16[48,3072]{1,0:T(8,128)(2,1)S(1)} %add_convert_fusion.6), channel_id=1, source_target_pairs={{0,16},{1,17},{2,18},{3,19},{4,20},{5,21},{6,22},{7,23},{8,24},{9,... | collective-permute-start | bytes 884744 | tf_op jit(solution)/shard_map/ppermute | solution.py:510
  252.2 42.0 %all-to-all-start.3 = ((bf16[16,64,384]{2,1,0:T(8,128)(2,1)}), bf16[16,64,384]{2,1,0:T(8,128)(2,1)S(1)}, u32[]{:S(2)}, u32[]{:S(2)}) async-start(bf16[16,64,384]{2,1,0:T(8,128)(2,1)} %bitcast.15), calls=%async_computation.3 | async-start | bytes 1572864 | tf_op jit(solution)/shard_map/all_to_all | solution.py:524
  257.5 27.2 %collective-permute-start.32 = (bf16[96,3072]{1,0:T(8,128)(2,1)S(1)}, bf16[96,3072]{1,0:T(8,128)(2,1)S(1)}, u32[]{:S(2)}, u32[]{:S(2)}) collective-permute-start(bf16[96,3072]{1,0:T(8,128)(2,1)S(1)} %maximum_select_fusion.1), channel_id=1, source_target_pairs={{0,8},{1,9},{2,10},{3,11},{4,12},{5,13},{6,14},{7,15},{8,0},{9,1},... | collective-permute-start | bytes 1769480 | tf_op jit(solution)/shard_map/ppermute | solution.py:510
  261.8 22.9 %collective-permute-start.31 = (bf16[192,1536]{1,0:T(8,128)(2,1)}, bf16[192,1536]{1,0:T(8,128)(2,1)}, u32[]{:S(2)}, u32[]{:S(2)}) collective-permute-start(bf16[192,1536]{1,0:T(8,128)(2,1)} %add_convert_fusion), channel_id=1, source_target_pairs={{0,4},{1,5},{2,6},{3,7},{4,0},{5,1},{6,2},{7,3},{8,12},{9,13},{10,... | collective-permute-start | bytes 1769480 | tf_op jit(solution)/shard_map/ppermute | solution.py:510
  286.0 8.2 %collective-permute-start.34 = (bf16[96,1536]{1,0:T(8,128)(2,1)S(1)}, bf16[96,1536]{1,0:T(8,128)(2,1)}, u32[]{:S(2)}, u32[]{:S(2)}) collective-permute-start(bf16[96,1536]{1,0:T(8,128)(2,1)S(1)} %add_convert_fusion.5), channel_id=1, source_target_pairs={{0,8},{1,9},{2,10},{3,11},{4,12},{5,13},{6,14},{7,15},{8,0},{9,1},... | collective-permute-start | bytes 884744 | tf_op jit(solution)/shard_map/ppermute | solution.py:510
  286.4 4.1 %collective-permute-start.35 = (f32[12,768]{1,0:T(8,128)S(1)}, f32[12,768]{1,0:T(8,128)S(1)}, u32[]{:S(2)}, u32[]{:S(2)}) collective-permute-start(f32[12,768]{1,0:T(8,128)S(1)} %fusion.3), channel_id=1, source_target_pairs={{0,1},{1,0},{2,3},{3,2},{4,5},{5,4},{6,7},{7,6},{8,9},{9,8},{10,11... | collective-permute-start | bytes 110600 | tf_op jit(solution)/shard_map/ppermute | solution.py:507
  294.2 5.7 %collective-permute-start.37 = (f32[12,768]{1,0:T(8,128)}, f32[12,768]{1,0:T(8,128)S(1)}, u32[]{:S(2)}, u32[]{:S(2)}) collective-permute-start(f32[12,768]{1,0:T(8,128)} %add.296), channel_id=1, source_target_pairs={{0,4},{1,5},{2,6},{3,7},{4,0},{5,1},{6,2},{7,3},{8,12},{9,13},{10,... | collective-permute-start | bytes 110600 | tf_op jit(solution)/shard_map/ppermute | solution.py:510
  296.9 7.4 %collective-permute-start.36 = (bf16[48,1536]{1,0:T(8,128)(2,1)S(1)}, bf16[48,1536]{1,0:T(8,128)(2,1)S(1)}, u32[]{:S(2)}, u32[]{:S(2)}) collective-permute-start(bf16[48,1536]{1,0:T(8,128)(2,1)S(1)} %add_convert_fusion.11), channel_id=1, source_target_pairs={{0,16},{1,17},{2,18},{3,19},{4,20},{5,21},{6,22},{7,23},{8,24},{9,... | collective-permute-start | bytes 442376 | tf_op jit(solution)/shard_map/ppermute | solution.py:510
  299.2 21.3 %collective-permute-start.44 = (bf16[192,3072]{1,0:T(8,128)(2,1)S(1)}, bf16[192,3072]{1,0:T(8,128)(2,1)S(1)}, u32[]{:S(2)}, u32[]{:S(2)}) collective-permute-start(bf16[192,3072]{1,0:T(8,128)(2,1)S(1)} %maximum_select_fusion.refs_0_), channel_id=1, source_target_pairs={{0,2},{1,3},{2,0},{3,1},{4,6},{5,7},{6,4},{7,5},{8,10},{9,11},{10,... | collective-permute-start | bytes 3538952 | tf_op jit(solution)/shard_map/ppermute | solution.py:510
  299.3 28.4 %collective-permute-start.43 = (bf16[192,3072]{1,0:T(8,128)(2,1)S(1)}, bf16[192,3072]{1,0:T(8,128)(2,1)S(1)}, u32[]{:S(2)}, u32[]{:S(2)}) collective-permute-start(bf16[192,3072]{1,0:T(8,128)(2,1)S(1)} %maximum_select_fusion.refs_0_), channel_id=1, source_target_pairs={{0,4},{1,5},{2,6},{3,7},{4,0},{5,1},{6,2},{7,3},{8,12},{9,13},{10,... | collective-permute-start | bytes 3538952 | tf_op jit(solution)/shard_map/ppermute | solution.py:510
  305.6 7.3 %collective-permute-start.38 = (bf16[48,1536]{1,0:T(8,128)(2,1)S(1)}, bf16[48,1536]{1,0:T(8,128)(2,1)S(1)}, u32[]{:S(2)}, u32[]{:S(2)}) collective-permute-start(bf16[48,1536]{1,0:T(8,128)(2,1)S(1)} %add_convert_fusion.10), channel_id=1, source_target_pairs={{0,16},{1,17},{2,18},{3,19},{4,20},{5,21},{6,22},{7,23},{8,24},{9,... | collective-permute-start | bytes 442376 | tf_op jit(solution)/shard_map/ppermute | solution.py:510
  306.4 4.1 %collective-permute-start.39 = (f32[12,768]{1,0:T(8,128)S(1)}, f32[12,768]{1,0:T(8,128)S(1)}, u32[]{:S(2)}, u32[]{:S(2)}) collective-permute-start(f32[12,768]{1,0:T(8,128)S(1)} %add.303), channel_id=1, source_target_pairs={{0,8},{1,9},{2,10},{3,11},{4,12},{5,13},{6,14},{7,15},{8,0},{9,1},... | collective-permute-start | bytes 110600 | tf_op jit(solution)/shard_map/ppermute | solution.py:510
  313.0 7.3 %collective-permute-start.40 = (bf16[96,1536]{1,0:T(8,128)(2,1)S(1)}, bf16[96,1536]{1,0:T(8,128)(2,1)S(1)}, u32[]{:S(2)}, u32[]{:S(2)}) collective-permute-start(bf16[96,1536]{1,0:T(8,128)(2,1)S(1)} %maximum_select_fusion.3), channel_id=1, source_target_pairs={{0,8},{1,9},{2,10},{3,11},{4,12},{5,13},{6,14},{7,15},{8,0},{9,1},... | collective-permute-start | bytes 884744 | tf_op jit(solution)/shard_map/ppermute | solution.py:510
  313.1 5.3 %collective-permute-start.41 = (f32[12,768]{1,0:T(8,128)S(1)}, f32[12,768]{1,0:T(8,128)S(1)}, u32[]{:S(2)}, u32[]{:S(2)}) collective-permute-start(f32[12,768]{1,0:T(8,128)S(1)} %add.305), channel_id=1, source_target_pairs={{0,16},{1,17},{2,18},{3,19},{4,20},{5,21},{6,22},{7,23},{8,24},{9,... | collective-permute-start | bytes 110600 | tf_op jit(solution)/shard_map/ppermute | solution.py:510
  327.6 4.4 %collective-permute-start.45 = (bf16[192,3072]{1,0:T(8,128)(2,1)S(1)}, bf16[192,3072]{1,0:T(8,128)(2,1)}, u32[]{:S(2)}, u32[]{:S(2)}) collective-permute-start(bf16[192,3072]{1,0:T(8,128)(2,1)S(1)} %collective-permute-done.43.refs_1_), channel_id=1, source_target_pairs={{0,2},{1,3},{2,0},{3,1},{4,6},{5,7},{6,4},{7,5},{8,10},{9,11},{10,... | collective-permute-start | bytes 3538952 | tf_op jit(solution)/shard_map/ppermute | solution.py:510
  327.6 15.7 %collective-permute-start.42 = (bf16[192,1536]{1,0:T(8,128)(2,1)S(1)}, bf16[192,1536]{1,0:T(8,128)(2,1)S(1)}, u32[]{:S(2)}, u32[]{:S(2)}) collective-permute-start(bf16[192,1536]{1,0:T(8,128)(2,1)S(1)} %maximum_select_fusion.2.refs_0_), channel_id=1, source_target_pairs={{0,4},{1,5},{2,6},{3,7},{4,0},{5,1},{6,2},{7,3},{8,12},{9,13},{10,... | collective-permute-start | bytes 1769480 | tf_op jit(solution)/shard_map/ppermute | solution.py:510
  331.7 14.3 %collective-permute-start.46 = (bf16[192,1536]{1,0:T(8,128)(2,1)S(1)}, bf16[192,1536]{1,0:T(8,128)(2,1)}, u32[]{:S(2)}, u32[]{:S(2)}) collective-permute-start(bf16[192,1536]{1,0:T(8,128)(2,1)S(1)} %maximum_select_fusion.2.refs_0_), channel_id=1, source_target_pairs={{0,2},{1,3},{2,0},{3,1},{4,6},{5,7},{6,4},{7,5},{8,10},{9,11},{10,... | collective-permute-start | bytes 1769480 | tf_op jit(solution)/shard_map/ppermute | solution.py:510
  (54 other events, 311.5 us)

commit v4 on v3

--- a/solution.py
+++ b/solution.py
@@ -778,13 +778,15 @@
             if level == 0:
                 mlp_over, mlp_core = flip(mlp_piece, 1), flip(mlp_piece)
             small = add_over(small)
-            stage, small, input_back = lax.optimization_barrier((stage, small, input_back))
+            stage, small = lax.optimization_barrier((stage, small))
             kept.append((stage, -starts[level + 1]))
         piece = rows_sum(kept, *section(levels))
         for level in reversed(range(levels)):
             stage = flip(piece, upper[level])
             small = add_over(small)
             stage, small = lax.optimization_barrier((stage, small))
+            if level == levels - 1:
+                stage, input_back = lax.optimization_barrier((stage, input_back))
             piece = widen(level, piece, stage)
         while links:
             small = add_over(small)

time: 353 us -> 346 us (0.980)
  waiting for transfers between devices: 95.6 us -> 88.8 us
    ppermute x36, waiting for transfers between devices: 62.1 us -> 53.8 us  [flip(): return lax.ppermute(value, AXES, bit_pairs[bit])]
    unnamed x98 -> x94, local copies, waits for them, and re-layouts: 8.11 us -> 9.15 us
  transfers between devices with their start and end apart: 52 -> 52, of which waited for: 26 -> 26; matrix products, arithmetic and copies ran while one was open for 9% -> 7% of each run, Pallas kernels for 36% -> 37%
where the time goes in v4:
time: 346 us; the launch traced here: 344 us
  Pallas kernels  150 us (43%)
  waiting for transfers between devices  88.8 us (26%)
  starting transfers between devices  63.7 us (18%)
  other arithmetic  21.2 us (6%)
  local copies, waits for them, and re-layouts  17.7 us (5%)
    ppermute x36, waiting for transfers between devices, flip(): return lax.ppermute(value, AXES, bit_pairs[bit])  53.8 us
    ppermute x36, starting transfers between devices, flip(): return lax.ppermute(value, AXES, bit_pairs[bit])  26.6 us
    pallas_call x2, Pallas kernels, mlp_rows(): call(mlp_rows_kernel, 'mlp_rows', (steps, 3), [by_row, by_row, spec((widt...  25 us
    ppermute x12, waiting for transfers between devices, cross(): return lax.ppermute(value, AXES, tensor_pairs)  24.6 us
    pallas_call x2, Pallas kernels, attend_backward(): pl.pallas_call(functools.partial(attend_backward_kernel, tile, block), gr...  23.7 us
    all_to_all x4, starting transfers between devices, exchange(): lax.all_to_all(array, AXES, split_axis=0, concat_axis=0, tiled=True, axis...  22.7 us
    convert_element_type x10, other arithmetic, rows_sum(): return total.astype(BF16)  16.9 us
    pallas_call x1, Pallas kernels, attend_forward(): pl.pallas_call(functools.partial(attend_forward_kernel, tile, block), gri...  15.3 us
  transfers between devices with their start and end apart: 52, of which 26 were waited for; matrix products, arithmetic and copies ran while one was open for 7% of the time, Pallas kernels for 37%

profile of v4, /device:TPU:0, one launch (start us, length us, event | category | flops | bytes accessed | tf_op | source)
XLA Modules:
  0.0 344.3 jit_solution(10255907015851333455)
XLA Ops:
  1.2 2.6 collective-permute-start.3
  6.0 3.3 gather_slots.5
  9.3 7.3 %all-to-all-start = ((bf16[16,64,384]{2,1,0:T(8,128)(2,1)}), bf16[16,64,384]{2,1,0:T(8,128)(2,1)S(1)}, u32[]{:S(2)}, u32[]{:S(2)}) async-start(bf16[16,64,384]{2,1,0:T(8,128)(2,1)} %gather_slots.5), calls=%async_computation | async-start | bytes 1572864 | tf_op jit(solution)/shard_map/all_to_all | solution.py:524
  21.5 3.3 gather_slots.4
  30.4 6.0 %all-to-all-done = bf16[16,64,384]{2,1,0:T(8,128)(2,1)S(1)} async-done(((bf16[16,64,384]{2,1,0:T(8,128)(2,1)}), bf16[16,64,384]{2,1,0:T(8,128)(2,1)S(1)}, u32[]{:S(2)}, u32[]{:S(2)}) %all-to-all-start) | async-done | bytes 786464 | tf_op jit(solution)/shard_map/all_to_all | solution.py:524
  36.5 5.0 %all-to-all-start.1 = ((bf16[16,64,384]{2,1,0:T(8,128)(2,1)}), bf16[16,64,384]{2,1,0:T(8,128)(2,1)S(1)}, u32[]{:S(2)}, u32[]{:S(2)}) async-start(bf16[16,64,384]{2,1,0:T(8,128)(2,1)} %gather_slots.4), calls=%async_computation.1 | async-start | bytes 1572864 | tf_op jit(solution)/shard_map/all_to_all | solution.py:524
  44.3 6.9 %enter.1 = (f32[512,768]{1,0:T(8,128)}, bf16[512,768]{1,0:T(8,128)(2,1)}, bf16[512,768]{1,0:T(8,128)(2,1)}, bf16[512,768]{1,0:T(8,128)(2,1)}) custom-call(s32[10]{0:T(128)} %concatenate.50.info, bf16[8,2,64,384]{3,2,1,0:T(8,128)(2,1)} %bitcast.13, f32[6,768]{1,0:T(8,128)} %fusion.1.thoughts, f32[2,768]{1,0:T(2,128)} %pad_maximum_fusion.2.norms, ...), custom_call_target="tpu_custom_call" | custom-call | tf_op jit(solution)/shard_map/enter/pallas_call | solution.py:574
  51.2 5.6 %collective-permute-done.5.direct.direct_q = bf16[1,384,384]{2,1,0:T(8,128)(2,1)S(1)} collective-permute-done((bf16[1,384,384]{2,1,0:T(8,128)(2,1)S(1)}, bf16[1,384,384]{2,1,0:T(8,128)(2,1)S(1)}, u32[]{:S(2)}, u32[]{:S(2)}) %collective-permute-start.5) | collective-permute-done | bytes 294944 | tf_op jit(solution)/shard_map/ppermute | solution.py:507
  58.0 2.8 collective-permute-done.7.partner.partner_q
  61.6 4.0 %queries.1.q_ref = bf16[512,768]{1,0:T(8,128)(2,1)} custom-call(s32[10]{0:T(128)} %concatenate.50.info, bf16[512,768]{1,0:T(8,128)(2,1)} %get-tuple-element.171.normed, f32[2,384]{1,0:T(2,128)} %bias_own.3, f32[2,384]{1,0:T(2,128)} %copy-done.35, bf16[3,768,384]{2,1,0:T(8,128)(2,1)} %own.7, bf16[1,384,384]{2,1,0:T(8,128)(2,1)} %copy-done.18, ...), custom_call_target="tpu_custom_call" | custom-call | tf_op jit(solution)/shard_map/queries/pallas_call | solution.py:583
  67.9 2.8 cotangent.1.grad.grad0
  71.9 15.3 %attend_forward.1 = (bf16[512,768]{1,0:T(8,128)(2,1)}, f32[6,2,512]{2,1,0:T(2,128)}) custom-call(s32[10]{0:T(128)} %concatenate.50.info, bf16[512,768]{1,0:T(8,128)(2,1)} %queries.1.q_ref, bf16[512,768]{1,0:T(8,128)(2,1)} %get-tuple-element.177.ko_ref, bf16[512,768]{1,0:T(8,128)(2,1)} %get-tuple-element.178.vo_ref, bf16[512,768]{1,0:T(8,128)(2,1)} %copy-done, ...), custom_call_target="tpu_custom_call" | custom-call | tf_op jit(solution)/shard_map/attend_forward/pallas_call | solution.py:139
  87.2 2.9 collective-permute-done.11.grad.grad1
  90.8 5.1 %middle.1 = (f32[512,768]{1,0:T(8,128)}, bf16[512,768]{1,0:T(8,128)(2,1)}) custom-call(s32[10]{0:T(128)} %concatenate.50.info, bf16[512,768]{1,0:T(8,128)(2,1)} %get-tuple-element.184.heads.out_ref, f32[512,768]{1,0:T(8,128)} %get-tuple-element.185.inputs, f32[3,768]{1,0:T(4,128)} %pad_maximum_fusion.1.norms, bf16[384,768]{1,0:T(8,128)(2,1)} %own.6, ...), custom_call_target="tpu_custom_call" | custom-call | tf_op jit(solution)/shard_map/middle/pallas_call | solution.py:598
  97.3 12.7 %mlp_rows.2 = (f32[512,768]{1,0:T(8,128)}, f32[512,768]{1,0:T(8,128)}, bf16[1536,512]{1,0:T(8,128)(2,1)}, bf16[512,1536]{1,0:T(8,128)(2,1)}, f32[2,1,1536]{2,1,0:T(1,128)}) custom-call(s32[10]{0:T(128)} %concatenate.50.info, bf16[512,768]{1,0:T(8,128)(2,1)} %get-tuple-element.188.normed.normed0, bf16[512,768]{1,0:T(8,128)(2,1)} %cotangent.1.grad.grad0, ...), custom_call_target="tpu_custom_call" | custom-call | tf_op jit(solution)/shard_map/mlp_rows/pallas_call | solution.py:613
  110.0 4.4 %collective-permute-done.13.normed.normed1 = bf16[512,768]{1,0:T(8,128)(2,1)S(1)} collective-permute-done((bf16[512,768]{1,0:T(8,128)(2,1)}, bf16[512,768]{1,0:T(8,128)(2,1)S(1)}, u32[]{:S(2)}, u32[]{:S(2)}) %collective-permute-start.13) | collective-permute-done | bytes 786464 | tf_op jit(solution)/shard_map/ppermute | solution.py:507
  115.3 12.2 %mlp_rows.3 = (bf16[512,768]{1,0:T(8,128)(2,1)}, bf16[512,768]{1,0:T(8,128)(2,1)}, bf16[1536,512]{1,0:T(8,128)(2,1)}, bf16[512,1536]{1,0:T(8,128)(2,1)}, f32[2,1,1536]{2,1,0:T(1,128)}) custom-call(s32[10]{0:T(128)} %concatenate.50.info, bf16[512,768]{1,0:T(8,128)(2,1)} %copy-done.9, bf16[512,768]{1,0:T(8,128)(2,1)} %copy-done.8, bf16[768,1536]{1,0:T(8,128)(2,1)} %fc.3, ...), custom_call_target="tpu_custom_call" | custom-call | tf_op jit(solution)/shard_map/mlp_rows/pallas_call | solution.py:613
  128.3 10.5 %mlp_grads.1 = (bf16[384,3072]{1,0:T(8,128)(2,1)}, bf16[384,3072]{1,0:T(8,128)(2,1)}) custom-call(s32[10]{0:T(128)} %concatenate.50.info, bf16[512,768]{1,0:T(8,128)(2,1)} %get-tuple-element.188.normed.normed0, bf16[512,768]{1,0:T(8,128)(2,1)} %copy-done.9, bf16[512,768]{1,0:T(8,128)(2,1)} %cotangent.1.grad.grad0, bf16[512,768]{1,0:T(8,128)(2,1)} %copy-done.8, ...), custom_call_target="tpu_custom_call" | custom-call | tf_op jit(solution)/shard_map/mlp_grads/pallas_call | solution.py:631
  138.8 6.5 %collective-permute-done.14.back_far = bf16[512,768]{1,0:T(8,128)(2,1)S(1)} collective-permute-done((bf16[512,768]{1,0:T(8,128)(2,1)}, bf16[512,768]{1,0:T(8,128)(2,1)S(1)}, u32[]{:S(2)}, u32[]{:S(2)}) %collective-permute-start.14) | collective-permute-done | bytes 786464 | tf_op jit(solution)/shard_map/ppermute | solution.py:507
  146.1 6.7 %back.1 = (f32[512,768]{1,0:T(8,128)}, bf16[512,768]{1,0:T(8,128)(2,1)}, bf16[512,768]{1,0:T(8,128)(2,1)}, f32[4,768]{1,0:T(4,128)}) custom-call(s32[10]{0:T(128)} %concatenate.50.info, f32[512,768]{1,0:T(8,128)} %get-tuple-element.189.back, bf16[512,768]{1,0:T(8,128)(2,1)} %copy-done.25, f32[512,768]{1,0:T(8,128)} %get-tuple-element.202.residual, ...), custom_call_target="tpu_custom_call" | custom-call | tf_op jit(solution)/shard_map/back/pallas_call | solution.py:662
  156.1 2.3 collective-permute-start.17
  158.3 11.9 %attend_backward.2 = (bf16[512,384]{1,0:T(8,128)(2,1)}, f32[512,384]{1,0:T(8,128)}, f32[512,384]{1,0:T(8,128)}, bf16[512,384]{1,0:T(8,128)(2,1)}, bf16[512,384]{1,0:T(8,128)(2,1)}) custom-call(s32[10]{0:T(128)} %concatenate.50.info, bf16[512,768]{1,0:T(8,128)(2,1)} %queries.1.q_ref, bf16[512,768]{1,0:T(8,128)(2,1)} %get-tuple-element.177.ko_ref, ...), custom_call_target="tpu_custom_call" | custom-call | tf_op jit(solution)/shard_map/attend_backward/pallas_call | solution.py:162
  174.3 3.8 %block.1 = bf16[8,2,64,384]{3,2,1,0:T(8,128)(2,1)} custom-call(s32[10]{0:T(128)} %concatenate.50.info, f32[512,768]{1,0:T(8,128)} %get-tuple-element.202.residual, f32[512,768]{1,0:T(8,128)} %get-tuple-element.224.mlp, bf16[512,768]{1,0:T(8,128)(2,1)} %collective-permute-done.15.mlp_far, f32[1,768]{1,0:T(1,128)} %get-tuple-element.325.bias), custom_call_target="tpu_custom_call" | custom-call | tf_op jit(solution)/shard_map/block/pallas_call | solution.py:695
  179.0 6.0 %attention_grads.2 = (bf16[384,1536]{1,0:T(8,128)(2,1)}, bf16[384,1536]{1,0:T(8,128)(2,1)}) custom-call(s32[10]{0:T(128)} %concatenate.50.info, bf16[512,768]{1,0:T(8,128)(2,1)} %get-tuple-element.171.normed, bf16[512,768]{1,0:T(8,128)(2,1)} %get-tuple-element.184.heads.out_ref, bf16[512,768]{1,0:T(8,128)(2,1)} %get-tuple-element.203.grad_attn, ...), custom_call_target="tpu_custom_call" | custom-call | tf_op jit(solution)/shard_map/attention_grads/pallas_call | solution.py:705
  185.1 2.4 add_convert_fusion.1
  188.3 2.5 add_convert_fusion.2
  192.5 6.0 %all-to-all-start.2 = ((bf16[16,64,384]{2,1,0:T(8,128)(2,1)}), bf16[16,64,384]{2,1,0:T(8,128)(2,1)S(1)}, u32[]{:S(2)}, u32[]{:S(2)}) async-start(bf16[16,64,384]{2,1,0:T(8,128)(2,1)} %bitcast.8), calls=%async_computation.2 | async-start | bytes 1572864 | tf_op jit(solution)/shard_map/all_to_all | solution.py:524
  200.5 11.9 %attend_backward.3 = (bf16[512,384]{1,0:T(8,128)(2,1)}, f32[512,384]{1,0:T(8,128)}, f32[512,384]{1,0:T(8,128)}, bf16[512,384]{1,0:T(8,128)(2,1)}, bf16[512,384]{1,0:T(8,128)(2,1)}) custom-call(s32[10]{0:T(128)} %concatenate.50.info, bf16[512,768]{1,0:T(8,128)(2,1)} %queries.1.q_ref, bf16[512,768]{1,0:T(8,128)(2,1)} %get-tuple-element.177.ko_ref, ...), custom_call_target="tpu_custom_call" | custom-call | tf_op jit(solution)/shard_map/attend_backward/pallas_call | solution.py:162
  212.3 2.5 collective-permute-done.23
  219.6 4.3 %all-to-all-done.2.array_ref = bf16[16,64,384]{2,1,0:T(8,128)(2,1)S(1)} async-done(((bf16[16,64,384]{2,1,0:T(8,128)(2,1)}), bf16[16,64,384]{2,1,0:T(8,128)(2,1)S(1)}, u32[]{:S(2)}, u32[]{:S(2)}) %all-to-all-start.2) | async-done | bytes 786464 | tf_op jit(solution)/shard_map/all_to_all | solution.py:524
  224.8 3.5 %gather_slots.6 = f32[16,64,384]{2,1,0:T(8,128)} custom-call(s32[16]{0:T(128)} %select_reduce_fusion.index_ref, bf16[16,64,384]{2,1,0:T(8,128)(2,1)} %copy-done.6), custom_call_target="tpu_custom_call" | custom-call | tf_op jit(solution)/shard_map/gather_slots/pallas_call | solution.py:217
  228.3 6.0 %attention_grads.3 = (bf16[384,1536]{1,0:T(8,128)(2,1)}, bf16[384,1536]{1,0:T(8,128)(2,1)}) custom-call(s32[10]{0:T(128)} %concatenate.50.info, bf16[512,768]{1,0:T(8,128)(2,1)} %get-tuple-element.171.normed, bf16[512,768]{1,0:T(8,128)(2,1)} %get-tuple-element.184.heads.out_ref, bf16[512,768]{1,0:T(8,128)(2,1)} %get-tuple-element.203.grad_attn, ...), custom_call_target="tpu_custom_call" | custom-call | tf_op jit(solution)/shard_map/attention_grads/pallas_call | solution.py:705
  236.2 9.4 %leave.1 = (bf16[8,2,64,384]{3,2,1,0:T(8,128)(2,1)}, f32[4,768]{1,0:T(4,128)}) custom-call(s32[10]{0:T(128)} %concatenate.50.info, f32[512,768]{1,0:T(8,128)} %get-tuple-element.185.inputs, f32[512,768]{1,0:T(8,128)} %get-tuple-element.263.grad_residual, f32[1,768]{1,0:T(1,128)} %copy-done.32, bf16[512,384]{1,0:T(8,128)(2,1)} %get-tuple-element.266.dq.dq0, ...), custom_call_target="tpu_custom_call" | custom-call | tf_op jit(solution)/shard_map/leave/pallas_call | solution.py:744
  245.7 5.9 %collective-permute-done.30 = bf16[48,3072]{1,0:T(8,128)(2,1)S(1)} collective-permute-done((bf16[48,3072]{1,0:T(8,128)(2,1)S(1)}, bf16[48,3072]{1,0:T(8,128)(2,1)S(1)}, u32[]{:S(2)}, u32[]{:S(2)}) %collective-permute-start.30) | collective-permute-done | bytes 294944 | tf_op jit(solution)/shard_map/ppermute | solution.py:510
  255.9 11.8 %collective-permute-done.32 = bf16[96,3072]{1,0:T(8,128)(2,1)S(1)} collective-permute-done((bf16[96,3072]{1,0:T(8,128)(2,1)S(1)}, bf16[96,3072]{1,0:T(8,128)(2,1)S(1)}, u32[]{:S(2)}, u32[]{:S(2)}) %collective-permute-start.32) | collective-permute-done | bytes 589856 | tf_op jit(solution)/shard_map/ppermute | solution.py:510
  272.5 4.5 %all-to-all-start.3 = ((bf16[16,64,384]{2,1,0:T(8,128)(2,1)}), bf16[16,64,384]{2,1,0:T(8,128)(2,1)S(1)}, u32[]{:S(2)}, u32[]{:S(2)}) async-start(bf16[16,64,384]{2,1,0:T(8,128)(2,1)} %bitcast.9), calls=%async_computation.3 | async-start | bytes 1572864 | tf_op jit(solution)/shard_map/all_to_all | solution.py:524
  279.0 3.3 collective-permute-done.35
  282.3 2.1 collective-permute-start.37
  289.0 13.0 %collective-permute-done.36 = bf16[48,1536]{1,0:T(8,128)(2,1)S(1)} collective-permute-done((bf16[48,1536]{1,0:T(8,128)(2,1)S(1)}, bf16[48,1536]{1,0:T(8,128)(2,1)S(1)}, u32[]{:S(2)}, u32[]{:S(2)}) %collective-permute-start.36) | collective-permute-done | bytes 147488 | tf_op jit(solution)/shard_map/ppermute | solution.py:510
  305.4 2.2 collective-permute-done.39
  307.6 2.2 collective-permute-done.38
  309.9 3.1 collective-permute-start.41
  313.0 2.8 collective-permute-done.41
  317.6 3.8 %collective-permute-start.42 = (bf16[192,1536]{1,0:T(8,128)(2,1)S(1)}, bf16[192,1536]{1,0:T(8,128)(2,1)S(1)}, u32[]{:S(2)}, u32[]{:S(2)}) collective-permute-start(bf16[192,1536]{1,0:T(8,128)(2,1)S(1)} %maximum_select_fusion.2.refs_0_), channel_id=1, source_target_pairs={{0,4},{1,5},{2,6},{3,7},{4,0},{5,1},{6,2},{7,3},{8,12},{9,13},{10,... | collective-permute-start | bytes 1769480 | tf_op jit(solution)/shard_map/ppermute | solution.py:510
  321.4 3.5 %gather_slots.7 = f32[16,64,384]{2,1,0:T(8,128)} custom-call(s32[16]{0:T(128)} %select_reduce_fusion.index_ref, bf16[16,64,384]{2,1,0:T(8,128)(2,1)} %copy-done.4), custom_call_target="tpu_custom_call" | custom-call | tf_op jit(solution)/shard_map/gather_slots/pallas_call | solution.py:217
  326.1 6.2 %finish_mlp.1 = (f32[768,1536]{1,0:T(8,128)}, f32[1536,768]{1,0:T(8,128)}) custom-call(s32[10]{0:T(128)} %concatenate.50.info, bf16[192,3072]{1,0:T(8,128)(2,1)} %copy-done.2, bf16[192,3072]{1,0:T(8,128)(2,1)} %collective-permute-done.43.refs_1_, bf16[192,3072]{1,0:T(8,128)(2,1)} %collective-permute-done.44.refs_2_, bf16[192,3072]{1,0:T(8,128)(2,1)} %copy-done.22), custom_call_target="tpu_custom_call" | custom-call | tf_op jit(solution)/shard_map/finish_mlp/pallas_call | solution.py:797
  332.3 3.0 collective-permute-done.42.refs_1_
  339.6 4.7 %finish_attention.1 = (f32[3,768,384]{2,1,0:T(8,128)}, f32[384,768]{1,0:T(8,128)}) custom-call(s32[10]{0:T(128)} %concatenate.50.info, bf16[192,1536]{1,0:T(8,128)(2,1)} %copy-done.10, bf16[192,1536]{1,0:T(8,128)(2,1)} %copy-done.26, bf16[192,1536]{1,0:T(8,128)(2,1)} %copy-done.27, bf16[192,1536]{1,0:T(8,128)(2,1)} %copy-done.28), custom_call_target="tpu_custom_call" | custom-call | tf_op jit(solution)/shard_map/finish_attention/pallas_call | solution.py:803
  (221 shorter events, 70.6 us)
Async XLA Ops:
  0.7 27.4 %collective-permute-start.4 = (s32[1,6]{1,0:T(1,128)}, s32[1,6]{1,0:T(1,128)S(1)}, u32[]{:S(2)}, u32[]{:S(2)}) collective-permute-start(s32[1,6]{1,0:T(1,128)} %param.18), channel_id=1, source_target_pairs={{0,2},{1,3},{2,0},{3,1},{4,6},{5,7},{6,4},{7,5},{8,10},{9,11},{10,... | collective-permute-start | bytes 80 | tf_op jit(solution)/shard_map/ppermute | solution.py:510
  1.2 29.2 %collective-permute-start.3 = (f32[2,384]{1,0:T(2,128)}, f32[2,384]{1,0:T(2,128)S(1)}, u32[]{:S(2)}, u32[]{:S(2)}) collective-permute-start(f32[2,384]{1,0:T(2,128)} %bias_own.3), channel_id=1, source_target_pairs={{0,1},{1,0},{2,3},{3,2},{4,5},{5,4},{6,7},{7,6},{8,9},{9,8},{10,11... | collective-permute-start | bytes 9224 | tf_op jit(solution)/shard_map/ppermute | solution.py:507
  5.0 25.4 %collective-permute-start = (bf16[2,384,384]{2,1,0:T(8,128)(2,1)S(1)}, bf16[2,384,384]{2,1,0:T(8,128)(2,1)S(1)}, u32[]{:S(2)}, u32[]{:S(2)}) collective-permute-start(bf16[2,384,384]{2,1,0:T(8,128)(2,1)S(1)} %constant_dynamic-slice_fusion.3), channel_id=1, source_target_pairs={{0,1},{1,0},{2,3},{3,2},{4,5},{5,4},{6,7},{7,6},{8,9},{9,8},{10,11... | collective-permute-start | bytes 1769480 | tf_op jit(solution)/shard_map/ppermute | solution.py:507
  9.3 27.2 %all-to-all-start = ((bf16[16,64,384]{2,1,0:T(8,128)(2,1)}), bf16[16,64,384]{2,1,0:T(8,128)(2,1)S(1)}, u32[]{:S(2)}, u32[]{:S(2)}) async-start(bf16[16,64,384]{2,1,0:T(8,128)(2,1)} %gather_slots.5), calls=%async_computation | async-start | bytes 1572864 | tf_op jit(solution)/shard_map/all_to_all | solution.py:524
  26.0 3.8 %collective-permute-start.2 = (bf16[6,384]{1,0:T(8,128)(2,1)S(1)}, bf16[6,384]{1,0:T(8,128)(2,1)S(1)}, u32[]{:S(2)}, u32[]{:S(2)}) collective-permute-start(bf16[6,384]{1,0:T(8,128)(2,1)S(1)} %get-tuple-element.324), channel_id=1, source_target_pairs={{0,1},{1,0},{2,3},{3,2},{4,5},{5,4},{6,7},{7,6},{8,9},{9,8},{10,11... | collective-permute-start | bytes 13832 | tf_op jit(solution)/shard_map/ppermute | solution.py:507
  36.5 30.5 %all-to-all-start.1 = ((bf16[16,64,384]{2,1,0:T(8,128)(2,1)}), bf16[16,64,384]{2,1,0:T(8,128)(2,1)S(1)}, u32[]{:S(2)}, u32[]{:S(2)}) async-start(bf16[16,64,384]{2,1,0:T(8,128)(2,1)} %gather_slots.4), calls=%async_computation.1 | async-start | bytes 1572864 | tf_op jit(solution)/shard_map/all_to_all | solution.py:524
  41.5 15.3 %collective-permute-start.5 = (bf16[1,384,384]{2,1,0:T(8,128)(2,1)S(1)}, bf16[1,384,384]{2,1,0:T(8,128)(2,1)S(1)}, u32[]{:S(2)}, u32[]{:S(2)}) collective-permute-start(bf16[1,384,384]{2,1,0:T(8,128)(2,1)S(1)} %constant_dynamic-slice_fusion), channel_id=1, source_target_pairs={{0,1},{1,0},{2,3},{3,2},{4,5},{5,4},{6,7},{7,6},{8,9},{9,8},{10,11... | collective-permute-start | bytes 884744 | tf_op jit(solution)/shard_map/ppermute | solution.py:507
  56.8 13.9 %collective-permute-start.9 = (bf16[512,768]{1,0:T(8,128)(2,1)}, bf16[512,768]{1,0:T(8,128)(2,1)S(1)}, u32[]{:S(2)}, u32[]{:S(2)}) collective-permute-start(bf16[512,768]{1,0:T(8,128)(2,1)} %get-tuple-element.177.ko_ref), channel_id=1, source_target_pairs={{0,2},{1,3},{2,0},{3,1},{4,6},{5,7},{6,4},{7,5},{8,10},{9,11},{10,... | collective-permute-start | bytes 2359304 | tf_op jit(solution)/shard_map/ppermute | solution.py:510
  56.8 13.9 %collective-permute-start.10 = (bf16[512,768]{1,0:T(8,128)(2,1)}, bf16[512,768]{1,0:T(8,128)(2,1)S(1)}, u32[]{:S(2)}, u32[]{:S(2)}) collective-permute-start(bf16[512,768]{1,0:T(8,128)(2,1)} %get-tuple-element.178.vo_ref), channel_id=1, source_target_pairs={{0,2},{1,3},{2,0},{3,1},{4,6},{5,7},{6,4},{7,5},{8,10},{9,11},{10,... | collective-permute-start | bytes 2359304 | tf_op jit(solution)/shard_map/ppermute | solution.py:510
  57.3 3.5 %collective-permute-start.7 = (bf16[1,384,384]{2,1,0:T(8,128)(2,1)S(1)}, bf16[1,384,384]{2,1,0:T(8,128)(2,1)S(1)}, u32[]{:S(2)}, u32[]{:S(2)}) collective-permute-start(bf16[1,384,384]{2,1,0:T(8,128)(2,1)S(1)} %collective-permute-done.5.direct.direct_q), channel_id=1, source_target_pairs={{0,2},{1,3},{2,0},{3,1},{4,6},{5,7},{6,4},{7,5},{8,10},{9,11},{10,... | collective-permute-start | bytes 884744 | tf_op jit(solution)/shard_map/ppermute | solution.py:510
  57.3 9.6 %collective-permute-start.8 = (bf16[384,384]{1,0:T(8,128)(2,1)}, bf16[384,384]{1,0:T(8,128)(2,1)S(1)}, u32[]{:S(2)}, u32[]{:S(2)}) collective-permute-start(bf16[384,384]{1,0:T(8,128)(2,1)} %constant_dynamic-slice_fusion.2), channel_id=1, source_target_pairs={{0,1},{1,0},{2,3},{3,2},{4,5},{5,4},{6,7},{7,6},{8,9},{9,8},{10,11... | collective-permute-start | bytes 884744 | tf_op jit(solution)/shard_map/ppermute | solution.py:507
  70.7 19.4 %collective-permute-start.11 = (bf16[512,768]{1,0:T(8,128)(2,1)}, bf16[512,768]{1,0:T(8,128)(2,1)S(1)}, u32[]{:S(2)}, u32[]{:S(2)}) collective-permute-start(bf16[512,768]{1,0:T(8,128)(2,1)} %cotangent.1.grad.grad0), channel_id=1, source_target_pairs={{0,1},{1,0},{2,3},{3,2},{4,5},{5,4},{6,7},{7,6},{8,9},{9,8},{10,11... | collective-permute-start | bytes 2359304 | tf_op jit(solution)/shard_map/ppermute | solution.py:507
  71.5 18.6 %collective-permute-start.12 = (bf16[384,384]{1,0:T(8,128)(2,1)S(1)}, bf16[384,384]{1,0:T(8,128)(2,1)S(1)}, u32[]{:S(2)}, u32[]{:S(2)}) collective-permute-start(bf16[384,384]{1,0:T(8,128)(2,1)S(1)} %collective-permute-done.8.direct), channel_id=1, source_target_pairs={{0,2},{1,3},{2,0},{3,1},{4,6},{5,7},{6,4},{7,5},{8,10},{9,11},{10,... | collective-permute-start | bytes 884744 | tf_op jit(solution)/shard_map/ppermute | solution.py:510
  95.9 18.5 %collective-permute-start.13 = (bf16[512,768]{1,0:T(8,128)(2,1)}, bf16[512,768]{1,0:T(8,128)(2,1)S(1)}, u32[]{:S(2)}, u32[]{:S(2)}) collective-permute-start(bf16[512,768]{1,0:T(8,128)(2,1)} %get-tuple-element.188.normed.normed0), channel_id=1, source_target_pairs={{0,1},{1,0},{2,3},{3,2},{4,5},{5,4},{6,7},{7,6},{8,9},{9,8},{10,11... | collective-permute-start | bytes 2359304 | tf_op jit(solution)/shard_map/ppermute | solution.py:507
  127.6 17.7 %collective-permute-start.14 = (bf16[512,768]{1,0:T(8,128)(2,1)}, bf16[512,768]{1,0:T(8,128)(2,1)S(1)}, u32[]{:S(2)}, u32[]{:S(2)}) collective-permute-start(bf16[512,768]{1,0:T(8,128)(2,1)} %get-tuple-element.193), channel_id=1, source_target_pairs={{0,1},{1,0},{2,3},{3,2},{4,5},{5,4},{6,7},{7,6},{8,9},{9,8},{10,11... | collective-permute-start | bytes 2359304 | tf_op jit(solution)/shard_map/ppermute | solution.py:507
  145.2 7.6 %collective-permute-start.16 = (bf16[384,3072]{1,0:T(8,128)(2,1)}, bf16[384,3072]{1,0:T(8,128)(2,1)}, u32[]{:S(2)}, u32[]{:S(2)}) collective-permute-start(bf16[384,3072]{1,0:T(8,128)(2,1)} %get-tuple-element.206), channel_id=1, source_target_pairs={{0,2},{1,3},{2,0},{3,1},{4,6},{5,7},{6,4},{7,5},{8,10},{9,11},{10,... | collective-permute-start | bytes 7077896 | tf_op jit(solution)/shard_map/ppermute | solution.py:510
  145.2 25.0 %collective-permute-start.15 = (bf16[512,768]{1,0:T(8,128)(2,1)}, bf16[512,768]{1,0:T(8,128)(2,1)}, u32[]{:S(2)}, u32[]{:S(2)}) collective-permute-start(bf16[512,768]{1,0:T(8,128)(2,1)} %get-tuple-element.204), channel_id=1, source_target_pairs={{0,1},{1,0},{2,3},{3,2},{4,5},{5,4},{6,7},{7,6},{8,9},{9,8},{10,11... | collective-permute-start | bytes 2359304 | tf_op jit(solution)/shard_map/ppermute | solution.py:507
  156.1 16.0 %collective-permute-start.17 = (bf16[96,3072]{1,0:T(8,128)(2,1)S(1)}, bf16[96,3072]{1,0:T(8,128)(2,1)}, u32[]{:S(2)}, u32[]{:S(2)}) collective-permute-start(bf16[96,3072]{1,0:T(8,128)(2,1)S(1)} %add_convert_fusion.4), channel_id=1, source_target_pairs={{0,4},{1,5},{2,6},{3,7},{4,0},{5,1},{6,2},{7,3},{8,12},{9,13},{10,... | collective-permute-start | bytes 1769480 | tf_op jit(solution)/shard_map/ppermute | solution.py:510
  172.1 6.0 %collective-permute-start.18 = (bf16[512,384]{1,0:T(8,128)(2,1)}, bf16[512,384]{1,0:T(8,128)(2,1)S(1)}, u32[]{:S(2)}, u32[]{:S(2)}) collective-permute-start(bf16[512,384]{1,0:T(8,128)(2,1)} %get-tuple-element.222), channel_id=1, source_target_pairs={{0,2},{1,3},{2,0},{3,1},{4,6},{5,7},{6,4},{7,5},{8,10},{9,11},{10,... | collective-permute-start | bytes 1179656 | tf_op jit(solution)/shard_map/ppermute | solution.py:510
  172.1 6.0 %collective-permute-start.19 = (bf16[512,384]{1,0:T(8,128)(2,1)}, bf16[512,384]{1,0:T(8,128)(2,1)S(1)}, u32[]{:S(2)}, u32[]{:S(2)}) collective-permute-start(bf16[512,384]{1,0:T(8,128)(2,1)} %get-tuple-element.223), channel_id=1, source_target_pairs={{0,2},{1,3},{2,0},{3,1},{4,6},{5,7},{6,4},{7,5},{8,10},{9,11},{10,... | collective-permute-start | bytes 1179656 | tf_op jit(solution)/shard_map/ppermute | solution.py:510
  172.6 12.4 %collective-permute-start.20 = (bf16[48,3072]{1,0:T(8,128)(2,1)}, bf16[48,3072]{1,0:T(8,128)(2,1)S(1)}, u32[]{:S(2)}, u32[]{:S(2)}) collective-permute-start(bf16[48,3072]{1,0:T(8,128)(2,1)} %get-tuple-element.232), channel_id=1, source_target_pairs={{0,4},{1,5},{2,6},{3,7},{4,0},{5,1},{6,2},{7,3},{8,12},{9,13},{10,... | collective-permute-start | bytes 884744 | tf_op jit(solution)/shard_map/ppermute | solution.py:510
  185.0 3.3 collective-permute-start.21
  190.8 21.5 %collective-permute-start.22 = (bf16[192,1536]{1,0:T(8,128)(2,1)}, bf16[192,1536]{1,0:T(8,128)(2,1)}, u32[]{:S(2)}, u32[]{:S(2)}) collective-permute-start(bf16[192,1536]{1,0:T(8,128)(2,1)} %get-tuple-element.237), channel_id=1, source_target_pairs={{0,1},{1,0},{2,3},{3,2},{4,5},{5,4},{6,7},{7,6},{8,9},{9,8},{10,11... | collective-permute-start | bytes 1769480 | tf_op jit(solution)/shard_map/ppermute | solution.py:507
  192.0 22.8 %collective-permute-start.23 = (bf16[96,3072]{1,0:T(8,128)(2,1)}, bf16[96,3072]{1,0:T(8,128)(2,1)}, u32[]{:S(2)}, u32[]{:S(2)}) collective-permute-start(bf16[96,3072]{1,0:T(8,128)(2,1)} %add_convert_fusion.1), channel_id=1, source_target_pairs={{0,8},{1,9},{2,10},{3,11},{4,12},{5,13},{6,14},{7,15},{8,0},{9,1},... | collective-permute-start | bytes 1769480 | tf_op jit(solution)/shard_map/ppermute | solution.py:510
  192.5 31.4 %all-to-all-start.2 = ((bf16[16,64,384]{2,1,0:T(8,128)(2,1)}), bf16[16,64,384]{2,1,0:T(8,128)(2,1)S(1)}, u32[]{:S(2)}, u32[]{:S(2)}) async-start(bf16[16,64,384]{2,1,0:T(8,128)(2,1)} %bitcast.8), calls=%async_computation.2 | async-start | bytes 1572864 | tf_op jit(solution)/shard_map/all_to_all | solution.py:524
  198.5 13.9 %collective-permute-start.24 = (bf16[48,3072]{1,0:T(8,128)(2,1)S(1)}, bf16[48,3072]{1,0:T(8,128)(2,1)}, u32[]{:S(2)}, u32[]{:S(2)}) collective-permute-start(bf16[48,3072]{1,0:T(8,128)(2,1)S(1)} %copy-done.30), channel_id=1, source_target_pairs={{0,4},{1,5},{2,6},{3,7},{4,0},{5,1},{6,2},{7,3},{8,12},{9,13},{10,... | collective-permute-start | bytes 884744 | tf_op jit(solution)/shard_map/ppermute | solution.py:510
  214.9 3.3 collective-permute-start.25
  214.9 3.3 collective-permute-start.26
  215.4 18.9 %collective-permute-start.28 = (bf16[192,1536]{1,0:T(8,128)(2,1)}, bf16[192,1536]{1,0:T(8,128)(2,1)}, u32[]{:S(2)}, u32[]{:S(2)}) collective-permute-start(bf16[192,1536]{1,0:T(8,128)(2,1)} %get-tuple-element.259), channel_id=1, source_target_pairs={{0,1},{1,0},{2,3},{3,2},{4,5},{5,4},{6,7},{7,6},{8,9},{9,8},{10,11... | collective-permute-start | bytes 1769480 | tf_op jit(solution)/shard_map/ppermute | solution.py:507
  218.2 16.3 %collective-permute-start.27 = (bf16[48,3072]{1,0:T(8,128)(2,1)}, bf16[48,3072]{1,0:T(8,128)(2,1)}, u32[]{:S(2)}, u32[]{:S(2)}) collective-permute-start(bf16[48,3072]{1,0:T(8,128)(2,1)} %add_convert_fusion.7), channel_id=1, source_target_pairs={{0,16},{1,17},{2,18},{3,19},{4,20},{5,21},{6,22},{7,23},{8,24},{9,... | collective-permute-start | bytes 884744 | tf_op jit(solution)/shard_map/ppermute | solution.py:510
  234.5 17.0 %collective-permute-start.29 = (bf16[384,1536]{1,0:T(8,128)(2,1)}, bf16[384,1536]{1,0:T(8,128)(2,1)}, u32[]{:S(2)}, u32[]{:S(2)}) collective-permute-start(bf16[384,1536]{1,0:T(8,128)(2,1)} %get-tuple-element.273), channel_id=1, source_target_pairs={{0,2},{1,3},{2,0},{3,1},{4,6},{5,7},{6,4},{7,5},{8,10},{9,11},{10,... | collective-permute-start | bytes 3538952 | tf_op jit(solution)/shard_map/ppermute | solution.py:510
  236.0 15.6 %collective-permute-start.30 = (bf16[48,3072]{1,0:T(8,128)(2,1)S(1)}, bf16[48,3072]{1,0:T(8,128)(2,1)S(1)}, u32[]{:S(2)}, u32[]{:S(2)}) collective-permute-start(bf16[48,3072]{1,0:T(8,128)(2,1)S(1)} %add_convert_fusion.6), channel_id=1, source_target_pairs={{0,16},{1,17},{2,18},{3,19},{4,20},{5,21},{6,22},{7,23},{8,24},{9,... | collective-permute-start | bytes 884744 | tf_op jit(solution)/shard_map/ppermute | solution.py:510
  252.4 15.4 %collective-permute-start.32 = (bf16[96,3072]{1,0:T(8,128)(2,1)S(1)}, bf16[96,3072]{1,0:T(8,128)(2,1)S(1)}, u32[]{:S(2)}, u32[]{:S(2)}) collective-permute-start(bf16[96,3072]{1,0:T(8,128)(2,1)S(1)} %maximum_select_fusion.1), channel_id=1, source_target_pairs={{0,8},{1,9},{2,10},{3,11},{4,12},{5,13},{6,14},{7,15},{8,0},{9,1},... | collective-permute-start | bytes 1769480 | tf_op jit(solution)/shard_map/ppermute | solution.py:510
  254.0 15.5 %collective-permute-start.31 = (bf16[192,1536]{1,0:T(8,128)(2,1)S(1)}, bf16[192,1536]{1,0:T(8,128)(2,1)}, u32[]{:S(2)}, u32[]{:S(2)}) collective-permute-start(bf16[192,1536]{1,0:T(8,128)(2,1)S(1)} %add_convert_fusion), channel_id=1, source_target_pairs={{0,4},{1,5},{2,6},{3,7},{4,0},{5,1},{6,2},{7,3},{8,12},{9,13},{10,... | collective-permute-start | bytes 1769480 | tf_op jit(solution)/shard_map/ppermute | solution.py:510
  270.7 11.6 %collective-permute-start.34 = (bf16[96,1536]{1,0:T(8,128)(2,1)S(1)}, bf16[96,1536]{1,0:T(8,128)(2,1)}, u32[]{:S(2)}, u32[]{:S(2)}) collective-permute-start(bf16[96,1536]{1,0:T(8,128)(2,1)S(1)} %add_convert_fusion.5), channel_id=1, source_target_pairs={{0,8},{1,9},{2,10},{3,11},{4,12},{5,13},{6,14},{7,15},{8,0},{9,1},... | collective-permute-start | bytes 884744 | tf_op jit(solution)/shard_map/ppermute | solution.py:510
  272.5 37.3 %all-to-all-start.3 = ((bf16[16,64,384]{2,1,0:T(8,128)(2,1)}), bf16[16,64,384]{2,1,0:T(8,128)(2,1)S(1)}, u32[]{:S(2)}, u32[]{:S(2)}) async-start(bf16[16,64,384]{2,1,0:T(8,128)(2,1)} %bitcast.9), calls=%async_computation.3 | async-start | bytes 1572864 | tf_op jit(solution)/shard_map/all_to_all | solution.py:524
  277.0 5.2 %collective-permute-start.35 = (f32[12,768]{1,0:T(8,128)S(1)}, f32[12,768]{1,0:T(8,128)S(1)}, u32[]{:S(2)}, u32[]{:S(2)}) collective-permute-start(f32[12,768]{1,0:T(8,128)S(1)} %fusion.3), channel_id=1, source_target_pairs={{0,1},{1,0},{2,3},{3,2},{4,5},{5,4},{6,7},{7,6},{8,9},{9,8},{10,11... | collective-permute-start | bytes 110600 | tf_op jit(solution)/shard_map/ppermute | solution.py:507
  282.3 6.7 %collective-permute-start.37 = (f32[12,768]{1,0:T(8,128)S(1)}, f32[12,768]{1,0:T(8,128)S(1)}, u32[]{:S(2)}, u32[]{:S(2)}) collective-permute-start(f32[12,768]{1,0:T(8,128)S(1)} %add.296), channel_id=1, source_target_pairs={{0,4},{1,5},{2,6},{3,7},{4,0},{5,1},{6,2},{7,3},{8,12},{9,13},{10,... | collective-permute-start | bytes 110600 | tf_op jit(solution)/shard_map/ppermute | solution.py:510
  285.6 16.3 %collective-permute-start.36 = (bf16[48,1536]{1,0:T(8,128)(2,1)S(1)}, bf16[48,1536]{1,0:T(8,128)(2,1)S(1)}, u32[]{:S(2)}, u32[]{:S(2)}) collective-permute-start(bf16[48,1536]{1,0:T(8,128)(2,1)S(1)} %add_convert_fusion.11), channel_id=1, source_target_pairs={{0,16},{1,17},{2,18},{3,19},{4,20},{5,21},{6,22},{7,23},{8,24},{9,... | collective-permute-start | bytes 442376 | tf_op jit(solution)/shard_map/ppermute | solution.py:510
  288.0 29.3 %collective-permute-start.44 = (bf16[192,3072]{1,0:T(8,128)(2,1)S(1)}, bf16[192,3072]{1,0:T(8,128)(2,1)}, u32[]{:S(2)}, u32[]{:S(2)}) collective-permute-start(bf16[192,3072]{1,0:T(8,128)(2,1)S(1)} %maximum_select_fusion.refs_0_), channel_id=1, source_target_pairs={{0,2},{1,3},{2,0},{3,1},{4,6},{5,7},{6,4},{7,5},{8,10},{9,11},{10,... | collective-permute-start | bytes 3538952 | tf_op jit(solution)/shard_map/ppermute | solution.py:510
  288.1 29.5 %collective-permute-start.43 = (bf16[192,3072]{1,0:T(8,128)(2,1)S(1)}, bf16[192,3072]{1,0:T(8,128)(2,1)}, u32[]{:S(2)}, u32[]{:S(2)}) collective-permute-start(bf16[192,3072]{1,0:T(8,128)(2,1)S(1)} %maximum_select_fusion.refs_0_), channel_id=1, source_target_pairs={{0,4},{1,5},{2,6},{3,7},{4,0},{5,1},{6,2},{7,3},{8,12},{9,13},{10,... | collective-permute-start | bytes 3538952 | tf_op jit(solution)/shard_map/ppermute | solution.py:510
  303.3 6.5 %collective-permute-start.38 = (bf16[48,1536]{1,0:T(8,128)(2,1)S(1)}, bf16[48,1536]{1,0:T(8,128)(2,1)S(1)}, u32[]{:S(2)}, u32[]{:S(2)}) collective-permute-start(bf16[48,1536]{1,0:T(8,128)(2,1)S(1)} %add_convert_fusion.10), channel_id=1, source_target_pairs={{0,16},{1,17},{2,18},{3,19},{4,20},{5,21},{6,22},{7,23},{8,24},{9,... | collective-permute-start | bytes 442376 | tf_op jit(solution)/shard_map/ppermute | solution.py:510
  303.4 4.2 %collective-permute-start.39 = (f32[12,768]{1,0:T(8,128)S(1)}, f32[12,768]{1,0:T(8,128)S(1)}, u32[]{:S(2)}, u32[]{:S(2)}) collective-permute-start(f32[12,768]{1,0:T(8,128)S(1)} %add.303), channel_id=1, source_target_pairs={{0,8},{1,9},{2,10},{3,11},{4,12},{5,13},{6,14},{7,15},{8,0},{9,1},... | collective-permute-start | bytes 110600 | tf_op jit(solution)/shard_map/ppermute | solution.py:510
  309.8 7.3 %collective-permute-start.40 = (bf16[96,1536]{1,0:T(8,128)(2,1)S(1)}, bf16[96,1536]{1,0:T(8,128)(2,1)S(1)}, u32[]{:S(2)}, u32[]{:S(2)}) collective-permute-start(bf16[96,1536]{1,0:T(8,128)(2,1)S(1)} %maximum_select_fusion.3), channel_id=1, source_target_pairs={{0,8},{1,9},{2,10},{3,11},{4,12},{5,13},{6,14},{7,15},{8,0},{9,1},... | collective-permute-start | bytes 884744 | tf_op jit(solution)/shard_map/ppermute | solution.py:510
  309.9 5.9 %collective-permute-start.41 = (f32[12,768]{1,0:T(8,128)S(1)}, f32[12,768]{1,0:T(8,128)S(1)}, u32[]{:S(2)}, u32[]{:S(2)}) collective-permute-start(f32[12,768]{1,0:T(8,128)S(1)} %add.305), channel_id=1, source_target_pairs={{0,16},{1,17},{2,18},{3,19},{4,20},{5,21},{6,22},{7,23},{8,24},{9,... | collective-permute-start | bytes 110600 | tf_op jit(solution)/shard_map/ppermute | solution.py:510
  317.6 7.5 %collective-permute-start.45 = (bf16[192,3072]{1,0:T(8,128)(2,1)}, bf16[192,3072]{1,0:T(8,128)(2,1)S(1)}, u32[]{:S(2)}, u32[]{:S(2)}) collective-permute-start(bf16[192,3072]{1,0:T(8,128)(2,1)} %collective-permute-done.43.refs_1_), channel_id=1, source_target_pairs={{0,2},{1,3},{2,0},{3,1},{4,6},{5,7},{6,4},{7,5},{8,10},{9,11},{10,... | collective-permute-start | bytes 3538952 | tf_op jit(solution)/shard_map/ppermute | solution.py:510
  317.6 17.7 %collective-permute-start.42 = (bf16[192,1536]{1,0:T(8,128)(2,1)S(1)}, bf16[192,1536]{1,0:T(8,128)(2,1)S(1)}, u32[]{:S(2)}, u32[]{:S(2)}) collective-permute-start(bf16[192,1536]{1,0:T(8,128)(2,1)S(1)} %maximum_select_fusion.2.refs_0_), channel_id=1, source_target_pairs={{0,4},{1,5},{2,6},{3,7},{4,0},{5,1},{6,2},{7,3},{8,12},{9,13},{10,... | collective-permute-start | bytes 1769480 | tf_op jit(solution)/shard_map/ppermute | solution.py:510
  324.9 13.0 %collective-permute-start.46 = (bf16[192,1536]{1,0:T(8,128)(2,1)S(1)}, bf16[192,1536]{1,0:T(8,128)(2,1)S(1)}, u32[]{:S(2)}, u32[]{:S(2)}) collective-permute-start(bf16[192,1536]{1,0:T(8,128)(2,1)S(1)} %maximum_select_fusion.2.refs_0_), channel_id=1, source_target_pairs={{0,2},{1,3},{2,0},{3,1},{4,6},{5,7},{6,4},{7,5},{8,10},{9,11},{10,... | collective-permute-start | bytes 1769480 | tf_op jit(solution)/shard_map/ppermute | solution.py:510
  (51 other events, 276.0 us)
